TPU v7x, 32 devices: a whole 2x2x4 slice. The times are simulated.
32 devices in a mesh: member: 2 (over y), lat: 4 (over z), lon: 2 (over x), lev: 2 (over core).
Axes of the slice: x: 2, y: 2, z: 4, core: 2. Of those that a mesh axis runs over, the one named last changes fastest.
Arguments:
- adjoint_in: float32 [10, 16, 32, 1152], P('member', 'lev', 'lat', 'lon'), parts along dimension 0, may hold values from -12 to 12
- lat_ahead: float32 [32, 32, 1152], P(('member', 'lev'), 'lat', 'lon'), parts along dimension 0, may hold values from 0.35 to 0.8
- lat_behind: float32 [32, 32, 1152], P(('member', 'lev'), 'lat', 'lon'), parts along dimension 0, may hold values from 0.02 to 0.06
- lon_ahead: float32 [32, 32, 1152], P(('member', 'lev'), 'lat', 'lon'), parts along dimension 0, may hold values from 0.02 to 0.06
- lon_behind: float32 [32, 32, 1152], P(('member', 'lev'), 'lat', 'lon'), parts along dimension 0, may hold values from 0.02 to 0.06
- coupling: float32 [16, 5, 5], P('lev'), may hold values from -0.9 to 0.9
- cutoff: int32 [32], replicated, may hold values from 1 to 576, as said below
Outputs:
- adjoint_out: float32 [10, 16, 32, 1152], P('member', 'lev', 'lat', 'lon'), parts along dimension 0
There are 2 independent parts, one for each index of `member`. A program takes and returns all parts, laid end to end along the dimension named above; an argument that names none is the same for every part. Nothing has to cross between parts.
Inputs may be any that keep to these rules, and one draw needn't show every extreme that they name: Rows 8 to 23 have a cutoff of exactly 576, every other row a cutoff below 576; the first and the last row have cutoff 1.
All inputs are finite; a program needn't handle non-finite values.
Results may differ from a plain program's by a relative error of at most 0.00011.
Values sent between devices are 32-bit elements; how exact they have to be, the bound alone decides.
No kernel may reach another device: no remote copies, remote signals or barrier semaphores. Data moves between devices by JAX's collectives and lax.ppermute only.
A program may use at most 64 MiB of HBM per device.

v0:
```python
import functools
import math

import jax
import jax.numpy as jnp
import numpy as np
from jax import lax
from jax.experimental import pallas as pl
from jax.experimental.pallas import tpu as pltpu
from jax.sharding import PartitionSpec as P

SUBSTEPS = 6
HALO = SUBSTEPS
LANES = 128
CHUNKS = (5,)
VMEM = pl.BlockSpec(memory_space=pltpu.VMEM)
SMEM = pl.BlockSpec(memory_space=pltpu.SMEM)


def split_bf16(values):
    high = values.astype(jnp.bfloat16)
    low = (values - high.astype(jnp.float32)).astype(jnp.bfloat16)
    return high, low


def split_bf16_numpy(values):
    values = values.astype(np.float32)
    high = values.astype(jnp.bfloat16)
    low = (values - high.astype(np.float32)).astype(jnp.bfloat16)
    return high, low


def mode_tables(length):
    ways = length // LANES
    point = np.arange(LANES)[:, None].astype(np.int64)
    column = np.arange(LANES)[None, :].astype(np.int64)
    half = LANES // 2
    wave = np.where(column <= half, column, column - half)
    angle = 2.0 * np.pi * (point * wave % LANES) / LANES
    weight = np.where((column == 0) | (column == half), 1.0 / LANES, 2.0 / LANES)
    real_block = np.where(column <= half, np.cos(angle), np.sin(angle)) * np.sqrt(weight)
    blocks = []
    for first in range(1, (ways + 1) // 2):
        angle = 2.0 * np.pi * (point * (first + ways * column) % length) / length
        cosine, sine = np.cos(angle), np.sin(angle)
        blocks.append(np.block([[cosine, -sine], [sine, cosine]]) / math.sqrt(LANES))
    return split_bf16_numpy(real_block), split_bf16_numpy(np.stack(blocks))


def dot_split(values, high_table, low_table, transposed):
    dims = (((1,), (1 if transposed else 0,)), ((), ()))
    high, low = split_bf16(values)
    dot = functools.partial(lax.dot_general, dimension_numbers=dims, preferred_element_type=jnp.float32)
    return dot(high, high_table) + (dot(low, high_table) + dot(high, low_table))


def damping_of(limit, wavenumber):
    ratio = limit / jnp.maximum(wavenumber, 1.0)
    return jnp.where(wavenumber > limit, ratio * ratio, 1.0)


def filter_kernel(sectors, cutoff_ref, *refs):
    circle_refs = refs[:sectors]
    real_high, real_low, block_high, block_low = refs[sectors:sectors + 4]
    own_out, first_out, second_out = refs[sectors + 4:sectors + 7]
    wide, real_wave, block_wave = refs[sectors + 7:]
    fields, levels, rows, sector = circle_refs[0].shape
    length = sector * sectors
    ways = length // LANES
    pairs = (ways - 1) // 2
    tiles = own_out.shape[-1] // LANES
    per_field = levels * rows
    lat = lax.axis_index("lat")
    limits = [cutoff_ref[lat * rows + j] for j in range(rows)]
    lowest = functools.reduce(jnp.minimum, limits)

    for k in range(sectors):
        wide[:, k * sector:(k + 1) * sector] = circle_refs[k][...].reshape(fields * per_field, sector)

    @pl.when(lowest < length // 2)
    def _():
        sublane = lax.broadcasted_iota(jnp.int32, (rows, LANES), 0)
        limit = jnp.zeros((rows, LANES), jnp.float32)
        for j in range(rows):
            limit = jnp.where(sublane == j, limits[j].astype(jnp.float32), limit)
        lane = lax.broadcasted_iota(jnp.int32, (rows, LANES), 1)

        def forward(field, carry):
            span = pl.ds(pl.multiple_of(field * per_field, per_field), per_field)
            tile = [wide[span, a * LANES:(a + 1) * LANES] for a in range(ways)]
            even = [tile[a] + tile[ways - a] for a in range(1, pairs + 1)]
            odd = [tile[a] - tile[ways - a] for a in range(1, pairs + 1)]
            real_wave[span, :] = tile[0] + sum(even)
            for k in range(1, pairs + 1):
                turn = [2.0 * math.pi * (a * k % ways) / ways for a in range(1, pairs + 1)]
                block_wave[k - 1, span, :LANES] = tile[0] + sum(math.cos(t) * e for t, e in zip(turn, even))
                block_wave[k - 1, span, LANES:] = -sum(math.sin(t) * o for t, o in zip(turn, odd))
            return carry

        lax.fori_loop(0, fields, forward, 0)

        def damp(spectrum, damping):
            shaped = spectrum.reshape(fields * levels, rows, damping.shape[-1])
            return (shaped * damping[None]).reshape(spectrum.shape)

        half = LANES // 2
        wave = (jnp.where(lane <= half, lane, lane - half) * ways).astype(jnp.float32)
        spectrum = dot_split(real_wave[...], real_high[...], real_low[...], False)
        spectrum = damp(spectrum, damping_of(limit, wave))
        real_wave[...] = dot_split(spectrum, real_high[...], real_low[...], True)
        for k in range(1, pairs + 1):
            mode = k + ways * lane
            one = damping_of(limit, jnp.minimum(mode, length - mode).astype(jnp.float32))
            damping = jnp.concatenate([one, one], axis=1)
            spectrum = dot_split(block_wave[k - 1], block_high[k - 1], block_low[k - 1], False)
            block_wave[k - 1] = dot_split(damp(spectrum, damping), block_high[k - 1], block_low[k - 1], True)

        def backward(field, carry):
            span = pl.ds(pl.multiple_of(field * per_field, per_field), per_field)
            base = real_wave[span, :] * (1.0 / ways)
            cosines = [block_wave[k, span, :LANES] for k in range(pairs)]
            sines = [block_wave[k, span, LANES:] for k in range(pairs)]
            wide[span, :LANES] = base + (2.0 / ways) * sum(cosines)
            for a in range(1, pairs + 1):
                turn = [2.0 * math.pi * (a * k % ways) / ways for k in range(1, pairs + 1)]
                even = base + sum((2.0 / ways * math.cos(t)) * c for t, c in zip(turn, cosines))
                odd = sum((2.0 / ways * math.sin(t)) * s for t, s in zip(turn, sines))
                wide[span, a * LANES:(a + 1) * LANES] = even - odd
                wide[span, (ways - a) * LANES:(ways - a + 1) * LANES] = even + odd
            return carry

        lax.fori_loop(0, fields, backward, 0)

    def emit(field, carry):
        span = pl.ds(pl.multiple_of(field * per_field, per_field), per_field)
        lane = lax.broadcasted_iota(jnp.int32, (per_field, LANES), 1)
        for a in range(tiles):
            tile = wide[span, a * LANES:(a + 1) * LANES]
            if a == tiles - 1:
                behind = wide[span, (ways - 1) * LANES:]
                tile = jnp.where(lane >= LANES - HALO, behind, tile)
            turned = jnp.swapaxes(tile.reshape(levels, rows, LANES), 0, 1)
            own_out[pl.ds(field, 1), :, :, a * LANES:(a + 1) * LANES] = turned[None]
        return carry

    lax.fori_loop(0, fields, emit, 0)
    top = rows - HALO
    to_next = lax.rem(lat, 2) == 0

    @pl.when(to_next)
    def _():
        first_out[...] = own_out[:, top:]
        second_out[...] = own_out[:, :HALO]

    @pl.when(jnp.logical_not(to_next))
    def _():
        first_out[...] = own_out[:, :HALO]
        second_out[...] = own_out[:, top:]


def rate_kernel(lat_ahead, lat_behind, lon_ahead, lon_behind, own_out, first_out, second_out):
    levels, rows, sector = lat_ahead.shape
    width = own_out.shape[-1]
    lat = lax.axis_index("lat")
    is_last = lat == lax.axis_size("lat") - 1
    for q, ref in enumerate((lat_ahead, lat_behind, lon_ahead, lon_behind)):
        for start in range(0, sector, LANES):
            stop = min(start + LANES, sector)
            tile = ref[:, :, start:stop]
            if stop - start < LANES:
                tile = jnp.pad(tile, ((0, 0), (0, 0), (0, LANES - (stop - start))))
            if q == 0:
                row = lax.broadcasted_iota(jnp.int32, tile.shape, 1)
                tile = jnp.where(jnp.logical_and(is_last, row == rows - 1), 0.0, tile)
            own_out[:, q, :, start:start + LANES] = jnp.swapaxes(tile, 0, 1)
    top = rows - HALO
    to_next = lax.rem(lat, 2) == 0

    @pl.when(to_next)
    def _():
        first_out[...] = own_out[top:]
        second_out[...] = own_out[:HALO]

    @pl.when(jnp.logical_not(to_next))
    def _():
        first_out[...] = own_out[:HALO]
        second_out[...] = own_out[top:]


def by_side(first_ref, second_ref, use):
    to_next = lax.rem(lax.axis_index("lat"), 2) == 0

    @pl.when(to_next)
    def _():
        use(second_ref, first_ref)

    @pl.when(jnp.logical_not(to_next))
    def _():
        use(first_ref, second_ref)


def rim_kernel(sector, own_ref, first_ref, second_ref, rim_out):
    rows = own_ref.shape[0]
    kinds = own_ref.shape[1]
    levels = own_ref.shape[2]
    edge = sector - HALO
    tile = edge // LANES * LANES
    lane = lax.broadcasted_iota(jnp.int32, (levels, LANES), 1)

    def rim_of(ref, count, base):
        def one(r, carry):
            packed = jnp.zeros((levels, LANES), jnp.float32)
            for q in range(kinds):
                at = 2 * HALO * q
                initial = pltpu.roll(ref[r, q, :, :LANES], at, 1) if at else ref[r, q, :, :LANES]
                shift = (at + HALO - (edge - tile)) % LANES
                last = pltpu.roll(ref[r, q, :, tile:tile + LANES], shift, 1)
                packed = jnp.where((lane >= at) & (lane < at + HALO), initial, packed)
                packed = jnp.where((lane >= at + HALO) & (lane < at + 2 * HALO), last, packed)
            rim_out[base + r] = packed
            return carry

        lax.fori_loop(0, count, one, 0)

    rim_of(own_ref, rows, HALO)

    def halos(below, above):
        rim_of(below, HALO, 0)
        rim_of(above, HALO, HALO + rows)

    by_side(first_ref, second_ref, halos)


def transport_kernel(chunks, sector, amplify, *refs):
    count = len(chunks)
    own_refs = refs[0:3 * count:3]
    first_refs = refs[1:3 * count:3]
    second_refs = refs[2:3 * count:3]
    rate_own, rate_first, rate_second, rim_ahead, rim_behind = refs[3 * count:3 * count + 5]
    out_ref = refs[3 * count + 5]
    current, coupled, rates = refs[3 * count + 6:]
    rows = own_refs[0].shape[1]
    levels, width = own_refs[0].shape[2:]
    fields = sum(chunks)
    kinds = 4
    extent = rows + 2 * HALO

    def load(below, above, own, field):
        def put(ref, base, number):
            def one(r, carry):
                current[base + r, field] = ref[r]
                return carry

            lax.fori_loop(0, number, one, 0)

        put(below, 0, HALO)
        put(own, HALO, rows)
        put(above, HALO + rows, HALO)

    field = 0
    for c in range(count):
        for j in range(chunks[c]):
            def use(below, above, c=c, j=j, field=field):
                load(below.at[j], above.at[j], own_refs[c].at[j], field)

            by_side(first_refs[c], second_refs[c], use)
            field += 1

    lane = lax.broadcasted_iota(jnp.int32, (levels, LANES), 1)
    ahead_tile, ahead_lane = sector // LANES, sector % LANES
    final = width // LANES - 1

    def extend(ref, count, base):
        def one(r, carry):
            ahead, behind = rim_ahead[base + r], rim_behind[base + r]
            for q in range(kinds):
                at = 2 * HALO * q
                for t in range(width // LANES):
                    piece = ref[r, q, :, t * LANES:(t + 1) * LANES]
                    if t == ahead_tile:
                        moved = pltpu.roll(ahead, (ahead_lane - at) % LANES, 1)
                        piece = jnp.where((lane >= ahead_lane) & (lane < ahead_lane + HALO), moved, piece)
                    if t == final:
                        moved = pltpu.roll(behind, (LANES - HALO - at - HALO) % LANES, 1)
                        piece = jnp.where(lane >= LANES - HALO, moved, piece)
                    if t >= ahead_tile:
                        inside = lane < sector + HALO - t * LANES
                        if t == final:
                            inside = inside | (lane >= LANES - HALO)
                        piece = jnp.where(inside, piece, 0.0)
                    rates[base + r, q, :, t * LANES:(t + 1) * LANES] = piece
            return carry

        lax.fori_loop(0, count, one, 0)

    extend(rate_own, rows, HALO)
    by_side(
        rate_first,
        rate_second,
        lambda below, above: (extend(below, HALO, 0), extend(above, HALO, HALO + rows)),
    )

    def combine(step, carry):
        r = extent - 2 - step
        south = rates[r - 1, 1]
        north = rates[r, 0]
        east = rates[r, 2]
        west = pltpu.roll(rates[r, 3], 1, 1)
        rates[r, 1] = south
        rates[r, 3] = west
        rates[r, 4] = 1.0 - east - west - north - south
        return carry

    lax.fori_loop(0, extent - 2, combine, 0)

    def couple(r):
        values = [current[r, g] for g in range(fields)]
        for f in range(fields):
            pieces = []
            for t in range(width // LANES):
                total = None
                for g in range(fields):
                    term = amplify[g, f] * values[g][:, t * LANES:(t + 1) * LANES]
                    total = term if total is None else total + term
                pieces.append(total)
            coupled[r, f] = jnp.concatenate(pieces, axis=1)

    def move(r):
        north, south, east, west, stay = (rates[r, q] for q in range(5))
        for f in range(fields):
            here = coupled[r, f]
            current[r, f] = (
                stay * here
                + east * pltpu.roll(here, width - 1, 1)
                + west * pltpu.roll(here, 1, 1)
                + north * coupled[r + 1, f]
                + south * coupled[r - 1, f]
            )

    def substep(step, carry):
        couple(step)
        couple(step + 1)

        def row(r, inner):
            couple(r + 1)
            move(r)
            return inner

        return lax.fori_loop(step + 1, extent - 1 - step, row, carry)

    lax.fori_loop(0, SUBSTEPS, substep, 0)

    for f in range(fields):
        for start in range(0, sector, LANES):
            stop = min(start + LANES, sector)
            tile = jnp.stack([current[HALO + r, f, :, start:start + LANES] for r in range(rows)])
            out_ref[f, :, :, start:stop] = jnp.swapaxes(tile, 0, 1)[:, :, :stop - start]


def lat_pairs(count):
    def both(start):
        ups = [(i, i + 1) for i in range(start, count - 1, 2)]
        return ups + [(j, i) for i, j in ups]

    return both(0), both(1)


def shards(adjoint_in, lat_ahead, lat_behind, lon_ahead, lon_behind, coupling, cutoff):
    fields, levels, rows, sector = adjoint_in.shape
    sectors = lax.axis_size("lon")
    length = sector * sectors
    width = -(-(sector + 2 * HALO) // LANES) * LANES
    even_pairs, odd_pairs = lat_pairs(lax.axis_size("lat"))
    f32 = jnp.float32
    chunks = CHUNKS if sum(CHUNKS) == fields else (fields,)

    def sector_ahead(values, offset):
        return lax.ppermute(values, "lon", [(s, (s - offset) % sectors) for s in range(sectors)])

    def to_bands(first, second):
        return lax.ppermute(first, "lat", even_pairs), lax.ppermute(second, "lat", odd_pairs)

    starts = [sum(chunks[:c]) for c in range(len(chunks))]
    parts = [adjoint_in[s:s + n] for s, n in zip(starts, chunks)]
    circles = [[part] + [sector_ahead(part, k) for k in range(1, sectors)] for part in parts]

    rate_shape = (4, levels, width)
    rate_own, rate_first, rate_second = pl.pallas_call(
        rate_kernel,
        out_shape=(
            jax.ShapeDtypeStruct((rows,) + rate_shape, f32),
            jax.ShapeDtypeStruct((HALO,) + rate_shape, f32),
            jax.ShapeDtypeStruct((HALO,) + rate_shape, f32),
        ),
        in_specs=[VMEM] * 4,
        out_specs=(VMEM,) * 3,
        name="rates",
    )(lat_ahead, lat_behind, lon_ahead, lon_behind)
    rate_first, rate_second = to_bands(rate_first, rate_second)
    rim = pl.pallas_call(
        functools.partial(rim_kernel, sector),
        out_shape=jax.ShapeDtypeStruct((rows + 2 * HALO, levels, LANES), f32),
        in_specs=[VMEM] * 3,
        out_specs=VMEM,
        name="rims",
    )(rate_own, rate_first, rate_second)
    rim_ahead = sector_ahead(rim, 1)
    rim_behind = rim_ahead if sectors == 2 else sector_ahead(rim, sectors - 1)

    (real_high, real_low), (block_high, block_low) = mode_tables(length)
    tables = [jnp.asarray(t) for t in (real_high, real_low, block_high, block_low)]
    moved = []
    for n, circle in zip(chunks, circles):
        lines = n * levels * rows
        own, first, second = pl.pallas_call(
            functools.partial(filter_kernel, sectors),
            out_shape=(
                jax.ShapeDtypeStruct((n, rows, levels, width), f32),
                jax.ShapeDtypeStruct((n, HALO, levels, width), f32),
                jax.ShapeDtypeStruct((n, HALO, levels, width), f32),
            ),
            in_specs=[SMEM] + [VMEM] * (sectors + 4),
            out_specs=(VMEM,) * 3,
            scratch_shapes=[
                pltpu.VMEM((lines, length), f32),
                pltpu.VMEM((lines, LANES), f32),
                pltpu.VMEM((block_high.shape[0], lines, 2 * LANES), f32),
            ],
            name="polar_filter",
        )(cutoff, *circle, *tables)
        moved += [own, *to_bands(first, second)]

    amplify = jnp.transpose(coupling + jnp.eye(fields, dtype=f32)[None], (1, 2, 0))
    amplify = jnp.broadcast_to(amplify[..., None], (fields, fields, levels, LANES))
    extent = rows + 2 * HALO
    return pl.pallas_call(
        functools.partial(transport_kernel, chunks, sector),
        out_shape=jax.ShapeDtypeStruct(adjoint_in.shape, f32),
        in_specs=[VMEM] * (1 + len(moved) + 5),
        out_specs=VMEM,
        scratch_shapes=[
            pltpu.VMEM((extent, fields, levels, width), f32),
            pltpu.VMEM((extent, fields, levels, width), f32),
            pltpu.VMEM((extent, 5, levels, width), f32),
        ],
        name="transport",
    )(amplify, *moved, rate_own, rate_first, rate_second, rim_ahead, rim_behind)


def solution(mesh):
    placed = (
        P("member", "lev", "lat", "lon"),
        P(("member", "lev"), "lat", "lon"),
        P(("member", "lev"), "lat", "lon"),
        P(("member", "lev"), "lat", "lon"),
        P(("member", "lev"), "lat", "lon"),
        P("lev", None, None),
        P(),
    )
    return jax.shard_map(
        shards,
        mesh=mesh,
        in_specs=placed,
        out_specs=P("member", "lev", "lat", "lon"),
        check_vma=False,
    )
```

profile of v0, /device:TPU:16, one launch (start us, length us, event | category | flops | bytes accessed | tf_op | source)
XLA Modules:
  0.0 63.3 jit_solution(13075921835899020967)
XLA Ops:
  0.0 1.5 %collective-permute-start = (f32[5,8,8,576]{3,2,1,0:T(8,128)}, f32[5,8,8,576]{3,2,1,0:T(8,128)S(1)}, u32[]{:S(2)}, u32[]{:S(2)}) collective-permute-start(f32[5,8,8,576]{3,2,1,0:T(8,128)} %refs_0_.1), channel_id=1, source_target_pairs={{0,2},{2,0},{1,3},{3,1},{4,6},{6,4},{5,7},{7,5},{8,10},{10,8},{9,1... | collective-permute-start | bytes 2211848 | tf_op jit(solution)/shard_map/ppermute | solution.py:378
  1.5 2.5 %rates.1 = (f32[8,4,8,640]{3,2,1,0:T(8,128)}, f32[6,4,8,640]{3,2,1,0:T(8,128)}, f32[6,4,8,640]{3,2,1,0:T(8,128)}) custom-call(f32[8,8,576]{2,1,0:T(8,128)} %lat_ahead.1, f32[8,8,576]{2,1,0:T(8,128)} %lat_behind.1, f32[8,8,576]{2,1,0:T(8,128)} %lon_ahead.1, f32[8,8,576]{2,1,0:T(8,128)} %lon_behind.1), custom_call_target="tpu_custom_call" | custom-call | tf_op jit(solution)/shard_map/rates/pallas_call | solution.py:388
  4.0 1.6 %collective-permute-start.3 = (f32[6,4,8,640]{3,2,1,0:T(8,128)}, f32[6,4,8,640]{3,2,1,0:T(8,128)S(1)}, u32[]{:S(2)}, u32[]{:S(2)}) collective-permute-start(f32[6,4,8,640]{3,2,1,0:T(8,128)} %get-tuple-element.15), channel_id=1, source_target_pairs={{0,4},{8,12},{4,0},{12,8},{1,5},{9,13},{5,1},{13,9},{2,6},{10,14},... | collective-permute-start | bytes 1474568 | tf_op jit(solution)/shard_map/ppermute | solution.py:381
  5.6 1.9 %collective-permute-start.4 = (f32[6,4,8,640]{3,2,1,0:T(8,128)}, f32[6,4,8,640]{3,2,1,0:T(8,128)S(1)}, u32[]{:S(2)}, u32[]{:S(2)}) collective-permute-start(f32[6,4,8,640]{3,2,1,0:T(8,128)} %get-tuple-element.16), channel_id=1, source_target_pairs={{4,8},{8,4},{5,9},{9,5},{6,10},{10,6},{7,11},{11,7},{20,24},{24,20... | collective-permute-start | bytes 1474568 | tf_op jit(solution)/shard_map/ppermute | solution.py:381
  7.5 12.7 %collective-permute-done.refs_1_ = f32[5,8,8,576]{3,2,1,0:T(8,128)S(1)} collective-permute-done((f32[5,8,8,576]{3,2,1,0:T(8,128)}, f32[5,8,8,576]{3,2,1,0:T(8,128)S(1)}, u32[]{:S(2)}, u32[]{:S(2)}) %collective-permute-start) | collective-permute-done | bytes 737312 | tf_op jit(solution)/shard_map/ppermute | solution.py:378
  20.2 0.0 copy-start.2
  20.2 0.9 %copy-done.2 = f32[5,8,8,576]{3,2,1,0:T(8,128)} copy-done((f32[5,8,8,576]{3,2,1,0:T(8,128)}, f32[5,8,8,576]{3,2,1,0:T(8,128)S(1)}, u32[]{:S(2)}) %copy-start.2) | copy-done | bytes 737304
  21.1 3.5 %polar_filter.1 = (f32[5,8,8,640]{3,2,1,0:T(8,128)}, f32[5,6,8,640]{3,2,1,0:T(8,128)}, f32[5,6,8,640]{3,2,1,0:T(8,128)}) custom-call(s32[32]{0:T(128)} %cutoff_ref.1, f32[5,8,8,576]{3,2,1,0:T(8,128)} %refs_0_.1, f32[5,8,8,576]{3,2,1,0:T(8,128)} %copy-done.2, bf16[128,128]{1,0:T(8,128)(2,1)} %constant.8.clone.refs_2_, ...), custom_call_target="tpu_custom_call" | custom-call | tf_op jit(solution)/shard_map/polar_filter/pallas_call | solution.py:415
  24.6 4.0 %collective-permute-start.1 = (f32[5,6,8,640]{3,2,1,0:T(8,128)}, f32[5,6,8,640]{3,2,1,0:T(8,128)S(1)}, u32[]{:S(2)}, u32[]{:S(2)}) collective-permute-start(f32[5,6,8,640]{3,2,1,0:T(8,128)} %get-tuple-element.12), channel_id=1, source_target_pairs={{0,4},{8,12},{4,0},{12,8},{1,5},{9,13},{5,1},{13,9},{2,6},{10,14},... | collective-permute-start | bytes 1843208 | tf_op jit(solution)/shard_map/ppermute | solution.py:381
  28.7 1.9 %collective-permute-start.2 = (f32[5,6,8,640]{3,2,1,0:T(8,128)}, f32[5,6,8,640]{3,2,1,0:T(8,128)S(1)}, u32[]{:S(2)}, u32[]{:S(2)}) collective-permute-start(f32[5,6,8,640]{3,2,1,0:T(8,128)} %get-tuple-element.13), channel_id=1, source_target_pairs={{4,8},{8,4},{5,9},{9,5},{6,10},{10,6},{7,11},{11,7},{20,24},{24,20... | collective-permute-start | bytes 1843208 | tf_op jit(solution)/shard_map/ppermute | solution.py:381
  30.6 0.0 collective-permute-done.3.first_ref.refs_4_
  30.6 0.0 copy-start
  30.6 0.0 collective-permute-done.4.second_ref.refs_5_
  30.6 0.0 copy-start.1
  30.6 0.8 %copy-done = f32[6,4,8,640]{3,2,1,0:T(8,128)} copy-done((f32[6,4,8,640]{3,2,1,0:T(8,128)}, f32[6,4,8,640]{3,2,1,0:T(8,128)S(1)}, u32[]{:S(2)}) %copy-start) | copy-done | bytes 491544
  31.4 0.1 copy-done.1
  31.5 0.0 copy-start.6
  31.5 3.6 %rims.1 = f32[20,8,128]{2,1,0:T(8,128)} custom-call(f32[8,4,8,640]{3,2,1,0:T(8,128)} %get-tuple-element.14.own_ref.refs_3_, f32[6,4,8,640]{3,2,1,0:T(8,128)} %copy-done, f32[6,4,8,640]{3,2,1,0:T(8,128)} %copy-done.1), custom_call_target="tpu_custom_call" | custom-call | tf_op jit(solution)/shard_map/rims/pallas_call | solution.py:400
  35.1 1.5 %collective-permute-start.5 = (f32[20,8,128]{2,1,0:T(8,128)}, f32[20,8,128]{2,1,0:T(8,128)S(1)}, u32[]{:S(2)}, u32[]{:S(2)}) collective-permute-start(f32[20,8,128]{2,1,0:T(8,128)} %rims.1), channel_id=1, source_target_pairs={{0,2},{2,0},{1,3},{3,1},{4,6},{6,4},{5,7},{7,5},{8,10},{10,8},{9,1... | collective-permute-start | bytes 245768 | tf_op jit(solution)/shard_map/ppermute | solution.py:378
  36.6 0.0 copy-done.6
  36.6 0.1 copy.12
  36.7 3.0 %collective-permute-done.5.refs_6_.refs_7_ = f32[20,8,128]{2,1,0:T(8,128)S(1)} collective-permute-done((f32[20,8,128]{2,1,0:T(8,128)}, f32[20,8,128]{2,1,0:T(8,128)S(1)}, u32[]{:S(2)}, u32[]{:S(2)}) %collective-permute-start.5) | collective-permute-done | bytes 81952 | tf_op jit(solution)/shard_map/ppermute | solution.py:378
  39.8 0.0 copy-start.5
  39.8 2.1 %collective-permute-done.1.refs_1_ = f32[5,6,8,640]{3,2,1,0:T(8,128)S(1)} collective-permute-done((f32[5,6,8,640]{3,2,1,0:T(8,128)}, f32[5,6,8,640]{3,2,1,0:T(8,128)S(1)}, u32[]{:S(2)}, u32[]{:S(2)}) %collective-permute-start.1) | collective-permute-done | bytes 614432 | tf_op jit(solution)/shard_map/ppermute | solution.py:381
  41.9 0.0 copy-start.3
  41.9 3.3 %collective-permute-done.2.refs_2_ = f32[5,6,8,640]{3,2,1,0:T(8,128)S(1)} collective-permute-done((f32[5,6,8,640]{3,2,1,0:T(8,128)}, f32[5,6,8,640]{3,2,1,0:T(8,128)S(1)}, u32[]{:S(2)}, u32[]{:S(2)}) %collective-permute-start.2) | collective-permute-done | bytes 614432 | tf_op jit(solution)/shard_map/ppermute | solution.py:381
  45.2 0.0 copy-start.4
  45.2 0.8 %broadcast_in_dim.2.amplify = f32[5,5,8,128]{3,2,1,0:T(8,128)} broadcast(f32[5,5,8]{2,1,0:T(8,128)S(1)} %copy.12), dimensions={0,1,2} | broadcast | bytes 103200 | tf_op jit(solution)/shard_map/broadcast_in_dim | solution.py:434
  46.1 0.0 copy-done.5
  46.1 0.0 copy-done.3
  46.1 0.0 copy-done.4
  46.1 17.2 %transport.1 = f32[5,8,8,576]{3,2,1,0:T(8,128)} custom-call(f32[5,5,8,128]{3,2,1,0:T(8,128)} %broadcast_in_dim.2.amplify, f32[5,8,8,640]{3,2,1,0:T(8,128)} %get-tuple-element.11.refs_0_, f32[5,6,8,640]{3,2,1,0:T(8,128)} %copy-done.3, f32[5,6,8,640]{3,2,1,0:T(8,128)} %copy-done.4, f32[8,4,8,640]{3,2,1,0:T(8,128)} %get-tuple-element.14.own_ref.refs_3_, ...), custom_call_target="tpu_custom_call" | custom-call | tf_op jit(solution)/shard_map/transport/pallas_call | solution.py:436
  (2 shorter events, 0.0 us)
Async XLA Ops:
  0.0 20.2 %collective-permute-start = (f32[5,8,8,576]{3,2,1,0:T(8,128)}, f32[5,8,8,576]{3,2,1,0:T(8,128)S(1)}, u32[]{:S(2)}, u32[]{:S(2)}) collective-permute-start(f32[5,8,8,576]{3,2,1,0:T(8,128)} %refs_0_.1), channel_id=1, source_target_pairs={{0,2},{2,0},{1,3},{3,1},{4,6},{6,4},{5,7},{7,5},{8,10},{10,8},{9,1... | collective-permute-start | bytes 2211848 | tf_op jit(solution)/shard_map/ppermute | solution.py:378
  4.0 26.6 %collective-permute-start.3 = (f32[6,4,8,640]{3,2,1,0:T(8,128)}, f32[6,4,8,640]{3,2,1,0:T(8,128)S(1)}, u32[]{:S(2)}, u32[]{:S(2)}) collective-permute-start(f32[6,4,8,640]{3,2,1,0:T(8,128)} %get-tuple-element.15), channel_id=1, source_target_pairs={{0,4},{8,12},{4,0},{12,8},{1,5},{9,13},{5,1},{13,9},{2,6},{10,14},... | collective-permute-start | bytes 1474568 | tf_op jit(solution)/shard_map/ppermute | solution.py:381
  5.6 25.0 %collective-permute-start.4 = (f32[6,4,8,640]{3,2,1,0:T(8,128)}, f32[6,4,8,640]{3,2,1,0:T(8,128)S(1)}, u32[]{:S(2)}, u32[]{:S(2)}) collective-permute-start(f32[6,4,8,640]{3,2,1,0:T(8,128)} %get-tuple-element.16), channel_id=1, source_target_pairs={{4,8},{8,4},{5,9},{9,5},{6,10},{10,6},{7,11},{11,7},{20,24},{24,20... | collective-permute-start | bytes 1474568 | tf_op jit(solution)/shard_map/ppermute | solution.py:381
  20.2 0.9 %copy-start.2 = (f32[5,8,8,576]{3,2,1,0:T(8,128)}, f32[5,8,8,576]{3,2,1,0:T(8,128)S(1)}, u32[]{:S(2)}) copy-start(f32[5,8,8,576]{3,2,1,0:T(8,128)S(1)} %collective-permute-done.refs_1_) | copy-start | bytes 2211844
  24.6 17.3 %collective-permute-start.1 = (f32[5,6,8,640]{3,2,1,0:T(8,128)}, f32[5,6,8,640]{3,2,1,0:T(8,128)S(1)}, u32[]{:S(2)}, u32[]{:S(2)}) collective-permute-start(f32[5,6,8,640]{3,2,1,0:T(8,128)} %get-tuple-element.12), channel_id=1, source_target_pairs={{0,4},{8,12},{4,0},{12,8},{1,5},{9,13},{5,1},{13,9},{2,6},{10,14},... | collective-permute-start | bytes 1843208 | tf_op jit(solution)/shard_map/ppermute | solution.py:381
  28.7 16.6 %collective-permute-start.2 = (f32[5,6,8,640]{3,2,1,0:T(8,128)}, f32[5,6,8,640]{3,2,1,0:T(8,128)S(1)}, u32[]{:S(2)}, u32[]{:S(2)}) collective-permute-start(f32[5,6,8,640]{3,2,1,0:T(8,128)} %get-tuple-element.13), channel_id=1, source_target_pairs={{4,8},{8,4},{5,9},{9,5},{6,10},{10,6},{7,11},{11,7},{20,24},{24,20... | collective-permute-start | bytes 1843208 | tf_op jit(solution)/shard_map/ppermute | solution.py:381
  30.6 0.8 %copy-start = (f32[6,4,8,640]{3,2,1,0:T(8,128)}, f32[6,4,8,640]{3,2,1,0:T(8,128)S(1)}, u32[]{:S(2)}) copy-start(f32[6,4,8,640]{3,2,1,0:T(8,128)S(1)} %collective-permute-done.3.first_ref.refs_4_) | copy-start | bytes 1474564
  30.6 0.9 %copy-start.1 = (f32[6,4,8,640]{3,2,1,0:T(8,128)}, f32[6,4,8,640]{3,2,1,0:T(8,128)S(1)}, u32[]{:S(2)}) copy-start(f32[6,4,8,640]{3,2,1,0:T(8,128)S(1)} %collective-permute-done.4.second_ref.refs_5_) | copy-start | bytes 1474564
  31.5 5.1 %copy-start.6 = (f32[8,5,5]{2,0,1:T(8,128)S(1)}, f32[8,5,5]{2,0,1:T(8,128)}, u32[]{:S(2)}) copy-start(f32[8,5,5]{2,0,1:T(8,128)} %param.16) | copy-start | bytes 2404
  35.1 4.7 %collective-permute-start.5 = (f32[20,8,128]{2,1,0:T(8,128)}, f32[20,8,128]{2,1,0:T(8,128)S(1)}, u32[]{:S(2)}, u32[]{:S(2)}) collective-permute-start(f32[20,8,128]{2,1,0:T(8,128)} %rims.1), channel_id=1, source_target_pairs={{0,2},{2,0},{1,3},{3,1},{4,6},{6,4},{5,7},{7,5},{8,10},{10,8},{9,1... | collective-permute-start | bytes 245768 | tf_op jit(solution)/shard_map/ppermute | solution.py:378
  39.8 6.3 %copy-start.5 = (f32[20,8,128]{2,1,0:T(8,128)}, f32[20,8,128]{2,1,0:T(8,128)S(1)}, u32[]{:S(2)}) copy-start(f32[20,8,128]{2,1,0:T(8,128)S(1)} %collective-permute-done.5.refs_6_.refs_7_) | copy-start | bytes 245764
  41.9 4.2 %copy-start.3 = (f32[5,6,8,640]{3,2,1,0:T(8,128)}, f32[5,6,8,640]{3,2,1,0:T(8,128)S(1)}, u32[]{:S(2)}) copy-start(f32[5,6,8,640]{3,2,1,0:T(8,128)S(1)} %collective-permute-done.1.refs_1_) | copy-start | bytes 1843204
  45.2 0.9 %copy-start.4 = (f32[5,6,8,640]{3,2,1,0:T(8,128)}, f32[5,6,8,640]{3,2,1,0:T(8,128)S(1)}, u32[]{:S(2)}) copy-start(f32[5,6,8,640]{3,2,1,0:T(8,128)S(1)} %collective-permute-done.2.refs_2_) | copy-start | bytes 1843204
where the time goes:
time: 63.5 us; the launch traced here: 63.3 us
  Pallas kernels  26.8 us (42%)
  waiting for transfers between devices  21.2 us (33%)
  starting transfers between devices  12.4 us (20%)
  local copies, waits for them, and re-layouts  2.79 us (4%)
    pallas_call x1, Pallas kernels, shards(): pl.pallas_call(functools.partial(transport_kernel, chunks, sector), out_s...  17.2 us
    ppermute x2, waiting for transfers between devices, sector_ahead(): lax.ppermute(values, 'lon', [(s, (s - offset) % sectors) for s in range(s...  15.7 us
    ppermute x2, starting transfers between devices, to_bands(): lax.ppermute(first, 'lat', even_pairs)  5.62 us
    ppermute x2, starting transfers between devices, to_bands(): lax.ppermute(second, 'lat', odd_pairs)  3.82 us
    pallas_call x1, Pallas kernels, shards(): pl.pallas_call(functools.partial(rim_kernel, sector), out_shape=jax.Shape...  3.57 us
    pallas_call x1, Pallas kernels, shards(): pl.pallas_call(functools.partial(filter_kernel, sectors), out_shape=(jax....  3.53 us
    ppermute x2, waiting for transfers between devices, to_bands(): lax.ppermute(second, 'lat', odd_pairs)  3.34 us
    ppermute x2, starting transfers between devices, sector_ahead(): lax.ppermute(values, 'lon', [(s, (s - offset) % sectors) for s in range(s...  2.98 us
  transfers between devices with their start and end apart: 6, of which 4 were waited for; matrix products, arithmetic and copies ran while one was open for 0% of the time, Pallas kernels for 15%

commit v1 on v0

--- a/solution.py
+++ b/solution.py
@@ -12,7 +12,8 @@
 SUBSTEPS = 6
 HALO = SUBSTEPS
 LANES = 128
-CHUNKS = (5,)
+CHUNKS = (2, 2, 1)
+PARAMS = pltpu.CompilerParams(vmem_limit_bytes=12 * 2**20)
 VMEM = pl.BlockSpec(memory_space=pltpu.VMEM)
 SMEM = pl.BlockSpec(memory_space=pltpu.SMEM)
 
@@ -49,9 +50,11 @@
 
 def dot_split(values, high_table, low_table, transposed):
     dims = (((1,), (1 if transposed else 0,)), ((), ()))
+    count = values.shape[0]
     high, low = split_bf16(values)
     dot = functools.partial(lax.dot_general, dimension_numbers=dims, preferred_element_type=jnp.float32)
-    return dot(high, high_table) + (dot(low, high_table) + dot(high, low_table))
+    main = dot(jnp.concatenate([high, low], axis=0), high_table)
+    return main[:count] + (main[count:] + dot(high, low_table))
 
 
 def damping_of(limit, wavenumber):
@@ -199,7 +202,37 @@
         use(first_ref, second_ref)
 
 
-def rim_kernel(sector, own_ref, first_ref, second_ref, rim_out):
+def coupling_power(coupling_ref):
+    levels, fields, _ = coupling_ref.shape
+    sublane = lax.broadcasted_iota(jnp.int32, (levels, LANES), 0)
+    base = []
+    for g in range(fields):
+        base.append([])
+        for f in range(fields):
+            value = jnp.full((levels, LANES), coupling_ref[0, g, f], jnp.float32)
+            for level in range(1, levels):
+                value = jnp.where(sublane == level, coupling_ref[level, g, f], value)
+            base[g].append(value + 1.0 if g == f else value)
+
+    def product(left, right):
+        def entry(g, f):
+            return functools.reduce(jnp.add, [left[g][h] * right[h][f] for h in range(fields)])
+
+        return [[entry(g, f) for f in range(fields)] for g in range(fields)]
+
+    power = base
+    for bit in bin(SUBSTEPS)[3:]:
+        power = product(power, power)
+        if bit == "1":
+            power = product(power, base)
+    return power
+
+
+def rim_kernel(sector, coupling_ref, own_ref, first_ref, second_ref, rim_out, power_out):
+    power = coupling_power(coupling_ref)
+    for g, line in enumerate(power):
+        for f, value in enumerate(line):
+            power_out[g, f] = value
     rows = own_ref.shape[0]
     kinds = own_ref.shape[1]
     levels = own_ref.shape[2]
@@ -231,41 +264,9 @@
     by_side(first_ref, second_ref, halos)
 
 
-def transport_kernel(chunks, sector, amplify, *refs):
-    count = len(chunks)
-    own_refs = refs[0:3 * count:3]
-    first_refs = refs[1:3 * count:3]
-    second_refs = refs[2:3 * count:3]
-    rate_own, rate_first, rate_second, rim_ahead, rim_behind = refs[3 * count:3 * count + 5]
-    out_ref = refs[3 * count + 5]
-    current, coupled, rates = refs[3 * count + 6:]
-    rows = own_refs[0].shape[1]
-    levels, width = own_refs[0].shape[2:]
-    fields = sum(chunks)
-    kinds = 4
+def face_kernel(sector, rate_own, rate_first, rate_second, rim_ahead, rim_behind, rates):
+    rows, kinds, levels, width = rate_own.shape
     extent = rows + 2 * HALO
-
-    def load(below, above, own, field):
-        def put(ref, base, number):
-            def one(r, carry):
-                current[base + r, field] = ref[r]
-                return carry
-
-            lax.fori_loop(0, number, one, 0)
-
-        put(below, 0, HALO)
-        put(own, HALO, rows)
-        put(above, HALO + rows, HALO)
-
-    field = 0
-    for c in range(count):
-        for j in range(chunks[c]):
-            def use(below, above, c=c, j=j, field=field):
-                load(below.at[j], above.at[j], own_refs[c].at[j], field)
-
-            by_side(first_refs[c], second_refs[c], use)
-            field += 1
-
     lane = lax.broadcasted_iota(jnp.int32, (levels, LANES), 1)
     ahead_tile, ahead_lane = sector // LANES, sector % LANES
     final = width // LANES - 1
@@ -291,7 +292,7 @@
                     rates[base + r, q, :, t * LANES:(t + 1) * LANES] = piece
             return carry
 
-        lax.fori_loop(0, count, one, 0)
+        lax.fori_loop(0, count, one, 0, unroll=2)
 
     extend(rate_own, rows, HALO)
     by_side(
@@ -302,59 +303,90 @@
 
     def combine(step, carry):
         r = extent - 2 - step
-        south = rates[r - 1, 1]
-        north = rates[r, 0]
-        east = rates[r, 2]
-        west = pltpu.roll(rates[r, 3], 1, 1)
-        rates[r, 1] = south
-        rates[r, 3] = west
-        rates[r, 4] = 1.0 - east - west - north - south
+        here = [[rates[r - (q == 1), q, :, t * LANES:(t + 1) * LANES] for q in range(kinds)] for t in range(final + 1)]
+        west = shifted([h[3] for h in here], 1)
+        for t, (north, south, east, _) in enumerate(here):
+            stay = 1.0 - east - west[t] - north - south
+            for q, value in ((1, south), (3, west[t]), (4, stay)):
+                rates[r, q, :, t * LANES:(t + 1) * LANES] = value
         return carry
 
-    lax.fori_loop(0, extent - 2, combine, 0)
-
-    def couple(r):
-        values = [current[r, g] for g in range(fields)]
+    lax.fori_loop(0, extent - 2, combine, 0, unroll=2)
+
+
+def shifted(tiles, step):
+    lane = lax.broadcasted_iota(jnp.int32, tiles[0].shape, 1)
+    rolled = [pltpu.roll(tile, step % LANES, 1) for tile in tiles]
+    border = lane == (0 if step == 1 else LANES - 1)
+    count = len(tiles)
+    return [jnp.where(border, rolled[(t - step) % count], rolled[t]) for t in range(count)]
+
+
+def transport_kernel(chunk, finished, sector, power_ref, rates, own_ref, first_ref, second_ref, *refs):
+    earlier = refs[:finished]
+    out_ref, even, odd = refs[finished:]
+    rows, levels, width = own_ref.shape[1:]
+    extent = rows + 2 * HALO
+    tiles = width // LANES
+    last = finished > 0
+
+    def put(ref, base):
+        even[:, base:base + ref.shape[1]] = ref[...]
+
+    put(own_ref, HALO)
+
+    def halos(below, above):
+        put(below, 0)
+        put(above, HALO + rows)
+
+    by_side(first_ref, second_ref, halos)
+
+    def line(source, r, field):
+        return [source[field, r, :, t * LANES:(t + 1) * LANES] for t in range(tiles)]
+
+    for step in range(SUBSTEPS):
+        source, target = (even, odd) if step % 2 == 0 else (odd, even)
+
+        def move(r):
+            for field in range(chunk):
+                here = line(source, r, field)
+                above, below = line(source, r + 1, field), line(source, r - 1, field)
+                ahead, behind = shifted(here, -1), shifted(here, 1)
+                for t in range(tiles):
+                    north, south, east, west, stay = (
+                        rates[r, q, :, t * LANES:(t + 1) * LANES] for q in range(5)
+                    )
+                    target[field, r, :, t * LANES:(t + 1) * LANES] = (
+                        stay * here[t]
+                        + east * ahead[t]
+                        + west * behind[t]
+                        + north * above[t]
+                        + south * below[t]
+                    )
+
+        def two_rows(pair, carry, step=step, move=move):
+            move(step + 1 + 2 * pair)
+            move(step + 2 + 2 * pair)
+            return carry
+
+        count = extent - 2 - 2 * step
+        lax.fori_loop(0, count // 2, two_rows, 0)
+        if count % 2:
+            move(extent - 2 - step)
+    result = even if SUBSTEPS % 2 == 0 else odd
+
+    if not last:
+        out_ref[...] = result[:, HALO:HALO + rows]
+        return
+    sources = [(ref, j, 0) for ref in earlier for j in range(ref.shape[0])]
+    sources += [(result, j, HALO) for j in range(chunk)]
+    fields = len(sources)
+    for start in range(0, sector, LANES):
+        stop = min(start + LANES, sector)
+        values = [ref[j, base:base + rows, :, start:start + LANES] for ref, j, base in sources]
         for f in range(fields):
-            pieces = []
-            for t in range(width // LANES):
-                total = None
-                for g in range(fields):
-                    term = amplify[g, f] * values[g][:, t * LANES:(t + 1) * LANES]
-                    total = term if total is None else total + term
-                pieces.append(total)
-            coupled[r, f] = jnp.concatenate(pieces, axis=1)
-
-    def move(r):
-        north, south, east, west, stay = (rates[r, q] for q in range(5))
-        for f in range(fields):
-            here = coupled[r, f]
-            current[r, f] = (
-                stay * here
-                + east * pltpu.roll(here, width - 1, 1)
-                + west * pltpu.roll(here, 1, 1)
-                + north * coupled[r + 1, f]
-                + south * coupled[r - 1, f]
-            )
-
-    def substep(step, carry):
-        couple(step)
-        couple(step + 1)
-
-        def row(r, inner):
-            couple(r + 1)
-            move(r)
-            return inner
-
-        return lax.fori_loop(step + 1, extent - 1 - step, row, carry)
-
-    lax.fori_loop(0, SUBSTEPS, substep, 0)
-
-    for f in range(fields):
-        for start in range(0, sector, LANES):
-            stop = min(start + LANES, sector)
-            tile = jnp.stack([current[HALO + r, f, :, start:start + LANES] for r in range(rows)])
-            out_ref[f, :, :, start:stop] = jnp.swapaxes(tile, 0, 1)[:, :, :stop - start]
+            total = functools.reduce(jnp.add, [power_ref[g, f][None] * values[g] for g in range(fields)])
+            out_ref[f, :, :, start:stop] = jnp.swapaxes(total, 0, 1)[:, :, :stop - start]
 
 
 def lat_pairs(count):
@@ -394,23 +426,38 @@
         ),
         in_specs=[VMEM] * 4,
         out_specs=(VMEM,) * 3,
+        compiler_params=PARAMS,
         name="rates",
     )(lat_ahead, lat_behind, lon_ahead, lon_behind)
     rate_first, rate_second = to_bands(rate_first, rate_second)
-    rim = pl.pallas_call(
+    rim, power = pl.pallas_call(
         functools.partial(rim_kernel, sector),
-        out_shape=jax.ShapeDtypeStruct((rows + 2 * HALO, levels, LANES), f32),
-        in_specs=[VMEM] * 3,
-        out_specs=VMEM,
+        out_shape=(
+            jax.ShapeDtypeStruct((rows + 2 * HALO, levels, LANES), f32),
+            jax.ShapeDtypeStruct((fields, fields, levels, LANES), f32),
+        ),
+        in_specs=[SMEM] + [VMEM] * 3,
+        out_specs=(VMEM,) * 2,
+        compiler_params=PARAMS,
         name="rims",
-    )(rate_own, rate_first, rate_second)
+    )(coupling, rate_own, rate_first, rate_second)
     rim_ahead = sector_ahead(rim, 1)
     rim_behind = rim_ahead if sectors == 2 else sector_ahead(rim, sectors - 1)
 
+    extent = rows + 2 * HALO
+    rates = pl.pallas_call(
+        functools.partial(face_kernel, sector),
+        out_shape=jax.ShapeDtypeStruct((extent, 5, levels, width), f32),
+        in_specs=[VMEM] * 5,
+        out_specs=VMEM,
+        compiler_params=PARAMS,
+        name="faces",
+    )(rate_own, rate_first, rate_second, rim_ahead, rim_behind)
+
     (real_high, real_low), (block_high, block_low) = mode_tables(length)
     tables = [jnp.asarray(t) for t in (real_high, real_low, block_high, block_low)]
-    moved = []
-    for n, circle in zip(chunks, circles):
+    results = []
+    for c, (n, circle) in enumerate(zip(chunks, circles)):
         lines = n * levels * rows
         own, first, second = pl.pallas_call(
             functools.partial(filter_kernel, sectors),
@@ -426,25 +473,26 @@
                 pltpu.VMEM((lines, LANES), f32),
                 pltpu.VMEM((block_high.shape[0], lines, 2 * LANES), f32),
             ],
+            compiler_params=PARAMS,
             name="polar_filter",
         )(cutoff, *circle, *tables)
-        moved += [own, *to_bands(first, second)]
-
-    amplify = jnp.transpose(coupling + jnp.eye(fields, dtype=f32)[None], (1, 2, 0))
-    amplify = jnp.broadcast_to(amplify[..., None], (fields, fields, levels, LANES))
-    extent = rows + 2 * HALO
-    return pl.pallas_call(
-        functools.partial(transport_kernel, chunks, sector),
-        out_shape=jax.ShapeDtypeStruct(adjoint_in.shape, f32),
-        in_specs=[VMEM] * (1 + len(moved) + 5),
-        out_specs=VMEM,
-        scratch_shapes=[
-            pltpu.VMEM((extent, fields, levels, width), f32),
-            pltpu.VMEM((extent, fields, levels, width), f32),
-            pltpu.VMEM((extent, 5, levels, width), f32),
-        ],
-        name="transport",
-    )(amplify, *moved, rate_own, rate_first, rate_second, rim_ahead, rim_behind)
+        first, second = to_bands(first, second)
+        is_last = c == len(chunks) - 1
+        earlier = results if is_last else []
+        shape = adjoint_in.shape if is_last else (n, rows, levels, width)
+        results.append(pl.pallas_call(
+            functools.partial(transport_kernel, n, len(earlier), sector),
+            out_shape=jax.ShapeDtypeStruct(shape, f32),
+            in_specs=[VMEM] * (5 + len(earlier)),
+            out_specs=VMEM,
+            scratch_shapes=[
+                pltpu.VMEM((n, extent, levels, width), f32),
+                pltpu.VMEM((n, extent, levels, width), f32),
+            ],
+            compiler_params=PARAMS,
+            name="transport",
+        )(power, rates, own, first, second, *earlier))
+    return results[-1]
 
 
 def solution(mesh):

time: 63.5 us -> 61.8 us (0.973)
  waiting for transfers between devices: 21.2 us -> 10.4 us
  starting transfers between devices: 12.4 us -> 20.5 us
  local copies, waits for them, and re-layouts: 2.79 us -> 8.01 us
  Pallas kernels: 26.8 us -> 21.9 us
    ppermute x2 -> x4, starting transfers between devices: 3.82 us -> 11.9 us  [to_bands(): lax.ppermute(second, 'lat', odd_pairs)]
    ppermute x2 -> x4, waiting for transfers between devices: 15.7 us -> 10.4 us  [sector_ahead(): lax.ppermute(values, 'lon', [(s, (s - offset) % sectors) for s in range(s...]
    unnamed x14 -> x27, local copies, waits for them, and re-layouts: 1.84 us -> 5.96 us
    ppermute x2 -> x4, waiting for transfers between devices: 3.34 us -> 0.01 us  [to_bands(): lax.ppermute(second, 'lat', odd_pairs)]
    pallas_call x1, Pallas kernels: 2.52 us -> 0.18 us  [shards(): pl.pallas_call(rate_kernel, out_shape=(jax.ShapeDtypeStruct((rows,) + rat...]
    ppermute x2 -> x4, waiting for transfers between devices: 2.11 us -> 0.01 us  [to_bands(): lax.ppermute(first, 'lat', even_pairs)]
    slice x0 -> x2, local copies, waits for them, and re-layouts: none -> 2.05 us  [shards(): parts = [adjoint_in[s:s + n] for s, n in zip(starts, chunks)]]
    ppermute x2 -> x4, starting transfers between devices: 2.98 us -> 4.4 us  [sector_ahead(): lax.ppermute(values, 'lon', [(s, (s - offset) % sectors) for s in range(s...]
  transfers between devices with their start and end apart: 6 -> 12, of which waited for: 4 -> 3; matrix products, arithmetic and copies ran while one was open for 0% -> 3% of each run, Pallas kernels for 15% -> 27%
where the time goes in v1:
time: 61.8 us; the launch traced here: 61 us
  Pallas kernels  21.9 us (35%)
  starting transfers between devices  20.5 us (33%)
  waiting for transfers between devices  10.4 us (17%)
  local copies, waits for them, and re-layouts  8.01 us (13%)
    pallas_call x3, Pallas kernels, shards(): pl.pallas_call(functools.partial(transport_kernel, n, len(earlier), secto...  14.4 us
    ppermute x4, starting transfers between devices, to_bands(): lax.ppermute(second, 'lat', odd_pairs)  11.9 us
    ppermute x4, waiting for transfers between devices, sector_ahead(): lax.ppermute(values, 'lon', [(s, (s - offset) % sectors) for s in range(s...  10.4 us
    unnamed x27, local copies, waits for them, and re-layouts  5.96 us
    ppermute x4, starting transfers between devices, sector_ahead(): lax.ppermute(values, 'lon', [(s, (s - offset) % sectors) for s in range(s...  4.4 us
    ppermute x4, starting transfers between devices, to_bands(): lax.ppermute(first, 'lat', even_pairs)  4.21 us
    pallas_call x1, Pallas kernels, shards(): pl.pallas_call(functools.partial(rim_kernel, sector), out_shape=(jax.Shap...  2.76 us
    pallas_call x1, Pallas kernels, shards(): pl.pallas_call(functools.partial(face_kernel, sector), out_shape=jax.Shap...  2.3 us
  transfers between devices with their start and end apart: 12, of which 3 were waited for; matrix products, arithmetic and copies ran while one was open for 3% of the time, Pallas kernels for 27%

profile of v1, /device:TPU:16, one launch (start us, length us, event | category | flops | bytes accessed | tf_op | source)
XLA Modules:
  0.0 61.0 jit_solution(11517249237439623445)
XLA Ops:
  0.0 1.0 %copy-done.6 = f32[8,8,576]{2,1,0:T(8,128)S(1)} copy-done((f32[8,8,576]{2,1,0:T(8,128)S(1)}, f32[8,8,576]{2,1,0:T(8,128)}, u32[]{:S(2)}) %copy-start.6) | copy-done | bytes 147480
  1.0 0.9 %copy-done.7 = f32[8,8,576]{2,1,0:T(8,128)S(1)} copy-done((f32[8,8,576]{2,1,0:T(8,128)S(1)}, f32[8,8,576]{2,1,0:T(8,128)}, u32[]{:S(2)}) %copy-start.7) | copy-done | bytes 147480
  1.9 0.9 %copy-done.8 = f32[8,8,576]{2,1,0:T(8,128)S(1)} copy-done((f32[8,8,576]{2,1,0:T(8,128)S(1)}, f32[8,8,576]{2,1,0:T(8,128)}, u32[]{:S(2)}) %copy-start.8) | copy-done | bytes 147480
  2.8 0.9 %copy-done.9 = f32[8,8,576]{2,1,0:T(8,128)S(1)} copy-done((f32[8,8,576]{2,1,0:T(8,128)S(1)}, f32[8,8,576]{2,1,0:T(8,128)}, u32[]{:S(2)}) %copy-start.9) | copy-done | bytes 147480
  3.8 0.2 rates.1
  3.9 1.6 %collective-permute-start = (f32[6,4,8,640]{3,2,1,0:T(8,128)S(1)}, f32[6,4,8,640]{3,2,1,0:T(8,128)S(1)}, u32[]{:S(2)}, u32[]{:S(2)}) collective-permute-start(f32[6,4,8,640]{3,2,1,0:T(8,128)S(1)} %get-tuple-element.20), channel_id=1, source_target_pairs={{0,4},{8,12},{4,0},{12,8},{1,5},{9,13},{5,1},{13,9},{2,6},{10,14},... | collective-permute-start | bytes 1474568 | tf_op jit(solution)/shard_map/ppermute | solution.py:413
  5.6 1.9 %collective-permute-start.1 = (f32[6,4,8,640]{3,2,1,0:T(8,128)S(1)}, f32[6,4,8,640]{3,2,1,0:T(8,128)S(1)}, u32[]{:S(2)}, u32[]{:S(2)}) collective-permute-start(f32[6,4,8,640]{3,2,1,0:T(8,128)S(1)} %get-tuple-element.21), channel_id=1, source_target_pairs={{4,8},{8,4},{5,9},{9,5},{6,10},{10,6},{7,11},{11,7},{20,24},{24,20... | collective-permute-start | bytes 1474568 | tf_op jit(solution)/shard_map/ppermute | solution.py:413
  7.5 1.1 %fusion = (f32[2,8,8,576]{3,2,1,0:T(8,128)S(1)}, f32[2,8,8,576]{3,2,1,0:T(8,128)S(1)}) fusion(f32[5,8,8,576]{3,2,1,0:T(8,128)} %param.11), kind=kLoop, calls=%fused_computation | loop fusion | bytes 1179648 | tf_op jit(solution)/shard_map/slice | solution.py:416
  8.6 1.6 %collective-permute-start.9 = (f32[2,8,8,576]{3,2,1,0:T(8,128)S(1)}, f32[2,8,8,576]{3,2,1,0:T(8,128)S(1)}, u32[]{:S(2)}, u32[]{:S(2)}) collective-permute-start(f32[2,8,8,576]{3,2,1,0:T(8,128)S(1)} %get-tuple-element.33.refs_0_), channel_id=1, source_target_pairs={{0,2},{2,0},{1,3},{3,1},{4,6},{6,4},{5,7},{7,5},{8,10},{10,8},{9,1... | collective-permute-start | bytes 884744 | tf_op jit(solution)/shard_map/ppermute | solution.py:410
  10.2 0.5 collective-permute-start.6
  10.7 8.6 %collective-permute-done.9.refs_1_ = f32[2,8,8,576]{3,2,1,0:T(8,128)S(1)} collective-permute-done((f32[2,8,8,576]{3,2,1,0:T(8,128)S(1)}, f32[2,8,8,576]{3,2,1,0:T(8,128)S(1)}, u32[]{:S(2)}, u32[]{:S(2)}) %collective-permute-start.9) | collective-permute-done | bytes 294944 | tf_op jit(solution)/shard_map/ppermute | solution.py:410
  19.3 0.8 %copy-done.2 = bf16[128,128]{1,0:T(8,128)(2,1)S(1)} copy-done((bf16[128,128]{1,0:T(8,128)(2,1)S(1)}, bf16[128,128]{1,0:T(8,128)(2,1)}, u32[]{:S(2)}) %copy-start.2) | copy-done | bytes 32792
  20.1 0.8 %copy-done.4 = bf16[128,128]{1,0:T(8,128)(2,1)S(1)} copy-done((bf16[128,128]{1,0:T(8,128)(2,1)S(1)}, bf16[128,128]{1,0:T(8,128)(2,1)}, u32[]{:S(2)}) %copy-start.4) | copy-done | bytes 32792
  20.8 0.7 %copy-done.10 = s32[32]{0:T(128)S(1)} copy-done((s32[32]{0:T(128)S(1)}, s32[32]{0:T(128)}, u32[]{:S(2)}) %copy-start.10) | copy-done | bytes 152
  21.5 0.8 %polar_filter.5 = (f32[2,8,8,640]{3,2,1,0:T(8,128)S(1)}, f32[2,6,8,640]{3,2,1,0:T(8,128)S(1)}, f32[2,6,8,640]{3,2,1,0:T(8,128)S(1)}) custom-call(s32[32]{0:T(128)S(1)} %copy-done.10, f32[2,8,8,576]{3,2,1,0:T(8,128)S(1)} %get-tuple-element.33.refs_0_, f32[2,8,8,576]{3,2,1,0:T(8,128)S(1)} %collective-permute-done.9.refs_1_, bf16[128,128]{1,0:T(8,128)(2,1)S(1)} %copy-done.2, ...), custom_call_target="tpu_custom_call" | custom-call | tf_op jit(solution)/shard_map/polar_filter/pallas_call | solution.py:462
  22.3 0.8 %collective-permute-start.10 = (f32[2,6,8,640]{3,2,1,0:T(8,128)S(1)}, f32[2,6,8,640]{3,2,1,0:T(8,128)S(1)}, u32[]{:S(2)}, u32[]{:S(2)}) collective-permute-start(f32[2,6,8,640]{3,2,1,0:T(8,128)S(1)} %get-tuple-element.31), channel_id=1, source_target_pairs={{0,4},{8,12},{4,0},{12,8},{1,5},{9,13},{5,1},{13,9},{2,6},{10,14},... | collective-permute-start | bytes 737288 | tf_op jit(solution)/shard_map/ppermute | solution.py:413
  23.1 0.9 %slice.9.refs_0_ = f32[1,8,8,576]{3,2,1,0:T(8,128)S(1)} slice(f32[5,8,8,576]{3,2,1,0:T(8,128)} %param.11), slice={[4:5], [0:8], [0:8], [0:576]} | slice | bytes 294912 | tf_op jit(solution)/shard_map/slice | solution.py:416
  24.0 1.6 %collective-permute-start.3 = (f32[1,8,8,576]{3,2,1,0:T(8,128)S(1)}, f32[1,8,8,576]{3,2,1,0:T(8,128)S(1)}, u32[]{:S(2)}, u32[]{:S(2)}) collective-permute-start(f32[1,8,8,576]{3,2,1,0:T(8,128)S(1)} %slice.9.refs_0_), channel_id=1, source_target_pairs={{0,2},{2,0},{1,3},{3,1},{4,6},{6,4},{5,7},{7,5},{8,10},{10,8},{9,1... | collective-permute-start | bytes 442376 | tf_op jit(solution)/shard_map/ppermute | solution.py:410
  25.6 0.5 collective-permute-done.6.refs_1_
  26.1 4.1 %collective-permute-start.11 = (f32[2,6,8,640]{3,2,1,0:T(8,128)S(1)}, f32[2,6,8,640]{3,2,1,0:T(8,128)S(1)}, u32[]{:S(2)}, u32[]{:S(2)}) collective-permute-start(f32[2,6,8,640]{3,2,1,0:T(8,128)S(1)} %get-tuple-element.32), channel_id=1, source_target_pairs={{4,8},{8,4},{5,9},{9,5},{6,10},{10,6},{7,11},{11,7},{20,24},{24,20... | collective-permute-start | bytes 737288 | tf_op jit(solution)/shard_map/ppermute | solution.py:413
  30.2 0.8 %polar_filter.4 = (f32[2,8,8,640]{3,2,1,0:T(8,128)S(1)}, f32[2,6,8,640]{3,2,1,0:T(8,128)S(1)}, f32[2,6,8,640]{3,2,1,0:T(8,128)S(1)}) custom-call(s32[32]{0:T(128)S(1)} %copy-done.10, f32[2,8,8,576]{3,2,1,0:T(8,128)S(1)} %get-tuple-element.34.refs_0_, f32[2,8,8,576]{3,2,1,0:T(8,128)S(1)} %collective-permute-done.6.refs_1_, bf16[128,128]{1,0:T(8,128)(2,1)S(1)} %copy-done.2, ...), custom_call_target="tpu_custom_call" | custom-call | tf_op jit(solution)/shard_map/polar_filter/pallas_call | solution.py:462
  31.1 2.7 %collective-permute-start.8 = (f32[2,6,8,640]{3,2,1,0:T(8,128)S(1)}, f32[2,6,8,640]{3,2,1,0:T(8,128)S(1)}, u32[]{:S(2)}, u32[]{:S(2)}) collective-permute-start(f32[2,6,8,640]{3,2,1,0:T(8,128)S(1)} %get-tuple-element.29), channel_id=1, source_target_pairs={{4,8},{8,4},{5,9},{9,5},{6,10},{10,6},{7,11},{11,7},{20,24},{24,20... | collective-permute-start | bytes 737288 | tf_op jit(solution)/shard_map/ppermute | solution.py:413
  33.9 2.8 %rims.1 = (f32[20,8,128]{2,1,0:T(8,128)S(1)}, f32[5,5,8,128]{3,2,1,0:T(8,128)S(1)}) custom-call(f32[8,5,5]{2,1,0:T(8,128)S(1)} %copy.12.coupling_ref, f32[8,4,8,640]{3,2,1,0:T(8,128)S(1)} %get-tuple-element.19.own_ref.rate_own, f32[6,4,8,640]{3,2,1,0:T(8,128)S(1)} %collective-permute-done.first_ref.rate_first, ...), custom_call_target="tpu_custom_call" | custom-call | tf_op jit(solution)/shard_map/rims/pallas_call | solution.py:433
  36.7 0.8 %collective-permute-start.2 = (f32[20,8,128]{2,1,0:T(8,128)S(1)}, f32[20,8,128]{2,1,0:T(8,128)S(1)}, u32[]{:S(2)}, u32[]{:S(2)}) collective-permute-start(f32[20,8,128]{2,1,0:T(8,128)S(1)} %get-tuple-element.23), channel_id=1, source_target_pairs={{0,2},{2,0},{1,3},{3,1},{4,6},{6,4},{5,7},{7,5},{8,10},{10,8},{9,1... | collective-permute-start | bytes 245768 | tf_op jit(solution)/shard_map/ppermute | solution.py:410
  37.4 0.7 %polar_filter.3 = (f32[1,8,8,640]{3,2,1,0:T(8,128)S(1)}, f32[1,6,8,640]{3,2,1,0:T(8,128)S(1)}, f32[1,6,8,640]{3,2,1,0:T(8,128)S(1)}) custom-call(s32[32]{0:T(128)S(1)} %copy-done.11, f32[1,8,8,576]{3,2,1,0:T(8,128)S(1)} %slice.9.refs_0_, f32[1,8,8,576]{3,2,1,0:T(8,128)S(1)} %collective-permute-done.3.refs_1_, bf16[128,128]{1,0:T(8,128)(2,1)S(1)} %copy-done.3, ...), custom_call_target="tpu_custom_call" | custom-call | tf_op jit(solution)/shard_map/polar_filter/pallas_call | solution.py:462
  38.2 1.7 %collective-permute-start.4 = (f32[1,6,8,640]{3,2,1,0:T(8,128)S(1)}, f32[1,6,8,640]{3,2,1,0:T(8,128)S(1)}, u32[]{:S(2)}, u32[]{:S(2)}) collective-permute-start(f32[1,6,8,640]{3,2,1,0:T(8,128)S(1)} %get-tuple-element.25), channel_id=1, source_target_pairs={{0,4},{8,12},{4,0},{12,8},{1,5},{9,13},{5,1},{13,9},{2,6},{10,14},... | collective-permute-start | bytes 368648 | tf_op jit(solution)/shard_map/ppermute | solution.py:413
  39.9 1.3 %collective-permute-done.2.rim_ahead.rim_behind = f32[20,8,128]{2,1,0:T(8,128)S(1)} collective-permute-done((f32[20,8,128]{2,1,0:T(8,128)S(1)}, f32[20,8,128]{2,1,0:T(8,128)S(1)}, u32[]{:S(2)}, u32[]{:S(2)}) %collective-permute-start.2) | collective-permute-done | bytes 81952 | tf_op jit(solution)/shard_map/ppermute | solution.py:410
  41.2 3.1 %collective-permute-start.5 = (f32[1,6,8,640]{3,2,1,0:T(8,128)S(1)}, f32[1,6,8,640]{3,2,1,0:T(8,128)S(1)}, u32[]{:S(2)}, u32[]{:S(2)}) collective-permute-start(f32[1,6,8,640]{3,2,1,0:T(8,128)S(1)} %get-tuple-element.26), channel_id=1, source_target_pairs={{4,8},{8,4},{5,9},{9,5},{6,10},{10,6},{7,11},{11,7},{20,24},{24,20... | collective-permute-start | bytes 368648 | tf_op jit(solution)/shard_map/ppermute | solution.py:413
  44.3 2.3 %faces.1.rates = f32[20,5,8,640]{3,2,1,0:T(8,128)S(1)} custom-call(f32[8,4,8,640]{3,2,1,0:T(8,128)S(1)} %get-tuple-element.19.own_ref.rate_own, f32[6,4,8,640]{3,2,1,0:T(8,128)S(1)} %collective-permute-done.first_ref.rate_first, f32[6,4,8,640]{3,2,1,0:T(8,128)S(1)} %collective-permute-done.1.second_ref.rate_second, ...), custom_call_target="tpu_custom_call" | custom-call | tf_op jit(solution)/shard_map/faces/pallas_call | solution.py:448
  46.6 4.7 %transport.4.refs_1_ = f32[2,8,8,640]{3,2,1,0:T(8,128)S(1)} custom-call(f32[5,5,8,128]{3,2,1,0:T(8,128)S(1)} %get-tuple-element.22.power_ref, f32[20,5,8,640]{3,2,1,0:T(8,128)S(1)} %faces.1.rates, f32[2,8,8,640]{3,2,1,0:T(8,128)S(1)} %get-tuple-element.30.own_ref, f32[2,6,8,640]{3,2,1,0:T(8,128)S(1)} %collective-permute-done.10.first_ref, ...), custom_call_target="tpu_custom_call" | custom-call | tf_op jit(solution)/shard_map/transport/pallas_call | solution.py:483
  51.3 4.7 %transport.3.refs_0_ = f32[2,8,8,640]{3,2,1,0:T(8,128)S(1)} custom-call(f32[5,5,8,128]{3,2,1,0:T(8,128)S(1)} %get-tuple-element.22.power_ref, f32[20,5,8,640]{3,2,1,0:T(8,128)S(1)} %faces.1.rates, f32[2,8,8,640]{3,2,1,0:T(8,128)S(1)} %get-tuple-element.27.own_ref, f32[2,6,8,640]{3,2,1,0:T(8,128)S(1)} %collective-permute-done.7.first_ref, ...), custom_call_target="tpu_custom_call" | custom-call | tf_op jit(solution)/shard_map/transport/pallas_call | solution.py:483
  56.0 5.0 %transport.5 = f32[5,8,8,576]{3,2,1,0:T(8,128)} custom-call(f32[5,5,8,128]{3,2,1,0:T(8,128)S(1)} %get-tuple-element.22.power_ref, f32[20,5,8,640]{3,2,1,0:T(8,128)S(1)} %faces.1.rates, f32[1,8,8,640]{3,2,1,0:T(8,128)S(1)} %get-tuple-element.24.own_ref, f32[1,6,8,640]{3,2,1,0:T(8,128)S(1)} %collective-permute-done.4.first_ref, ...), custom_call_target="tpu_custom_call" | custom-call | tf_op jit(solution)/shard_map/transport/pallas_call | solution.py:483
  (30 shorter events, 0.2 us)
Async XLA Ops:
  0.0 19.3 %copy-start = (bf16[4,256,256]{2,1,0:T(8,128)(2,1)S(1)}, bf16[4,256,256]{2,1,0:T(8,128)(2,1)}, u32[]{:S(2)}) copy-start(bf16[4,256,256]{2,1,0:T(8,128)(2,1)} %constant.10.clone.refs_4_) | copy-start | bytes 1572868
  0.0 19.3 %copy-start.1 = (bf16[4,256,256]{2,1,0:T(8,128)(2,1)S(1)}, bf16[4,256,256]{2,1,0:T(8,128)(2,1)}, u32[]{:S(2)}) copy-start(bf16[4,256,256]{2,1,0:T(8,128)(2,1)} %constant.11.clone.refs_5_) | copy-start | bytes 1572868
  0.0 1.0 %copy-start.6 = (f32[8,8,576]{2,1,0:T(8,128)S(1)}, f32[8,8,576]{2,1,0:T(8,128)}, u32[]{:S(2)}) copy-start(f32[8,8,576]{2,1,0:T(8,128)} %lat_ahead.1) | copy-start | bytes 442372
  1.0 0.9 %copy-start.7 = (f32[8,8,576]{2,1,0:T(8,128)S(1)}, f32[8,8,576]{2,1,0:T(8,128)}, u32[]{:S(2)}) copy-start(f32[8,8,576]{2,1,0:T(8,128)} %lat_behind.1) | copy-start | bytes 442372
  1.9 0.9 %copy-start.8 = (f32[8,8,576]{2,1,0:T(8,128)S(1)}, f32[8,8,576]{2,1,0:T(8,128)}, u32[]{:S(2)}) copy-start(f32[8,8,576]{2,1,0:T(8,128)} %lon_ahead.1) | copy-start | bytes 442372
  2.8 0.9 %copy-start.9 = (f32[8,8,576]{2,1,0:T(8,128)S(1)}, f32[8,8,576]{2,1,0:T(8,128)}, u32[]{:S(2)}) copy-start(f32[8,8,576]{2,1,0:T(8,128)} %lon_behind.1) | copy-start | bytes 442372
  3.9 27.1 %collective-permute-start = (f32[6,4,8,640]{3,2,1,0:T(8,128)S(1)}, f32[6,4,8,640]{3,2,1,0:T(8,128)S(1)}, u32[]{:S(2)}, u32[]{:S(2)}) collective-permute-start(f32[6,4,8,640]{3,2,1,0:T(8,128)S(1)} %get-tuple-element.20), channel_id=1, source_target_pairs={{0,4},{8,12},{4,0},{12,8},{1,5},{9,13},{5,1},{13,9},{2,6},{10,14},... | collective-permute-start | bytes 1474568 | tf_op jit(solution)/shard_map/ppermute | solution.py:413
  5.6 25.5 %collective-permute-start.1 = (f32[6,4,8,640]{3,2,1,0:T(8,128)S(1)}, f32[6,4,8,640]{3,2,1,0:T(8,128)S(1)}, u32[]{:S(2)}, u32[]{:S(2)}) collective-permute-start(f32[6,4,8,640]{3,2,1,0:T(8,128)S(1)} %get-tuple-element.21), channel_id=1, source_target_pairs={{4,8},{8,4},{5,9},{9,5},{6,10},{10,6},{7,11},{11,7},{20,24},{24,20... | collective-permute-start | bytes 1474568 | tf_op jit(solution)/shard_map/ppermute | solution.py:413
  7.5 26.4 %copy-start.12 = (f32[8,5,5]{2,0,1:T(8,128)S(1)}, f32[8,5,5]{2,0,1:T(8,128)}, u32[]{:S(2)}) copy-start(f32[8,5,5]{2,0,1:T(8,128)} %param.16) | copy-start | bytes 2404
  8.6 10.6 %collective-permute-start.9 = (f32[2,8,8,576]{3,2,1,0:T(8,128)S(1)}, f32[2,8,8,576]{3,2,1,0:T(8,128)S(1)}, u32[]{:S(2)}, u32[]{:S(2)}) collective-permute-start(f32[2,8,8,576]{3,2,1,0:T(8,128)S(1)} %get-tuple-element.33.refs_0_), channel_id=1, source_target_pairs={{0,2},{2,0},{1,3},{3,1},{4,6},{6,4},{5,7},{7,5},{8,10},{10,8},{9,1... | collective-permute-start | bytes 884744 | tf_op jit(solution)/shard_map/ppermute | solution.py:410
  10.2 15.9 %collective-permute-start.6 = (f32[2,8,8,576]{3,2,1,0:T(8,128)S(1)}, f32[2,8,8,576]{3,2,1,0:T(8,128)S(1)}, u32[]{:S(2)}, u32[]{:S(2)}) collective-permute-start(f32[2,8,8,576]{3,2,1,0:T(8,128)S(1)} %get-tuple-element.34.refs_0_), channel_id=1, source_target_pairs={{0,2},{2,0},{1,3},{3,1},{4,6},{6,4},{5,7},{7,5},{8,10},{10,8},{9,1... | collective-permute-start | bytes 884744 | tf_op jit(solution)/shard_map/ppermute | solution.py:410
  19.3 0.8 %copy-start.2 = (bf16[128,128]{1,0:T(8,128)(2,1)S(1)}, bf16[128,128]{1,0:T(8,128)(2,1)}, u32[]{:S(2)}) copy-start(bf16[128,128]{1,0:T(8,128)(2,1)} %constant.8.clone.refs_2_) | copy-start | bytes 98308
  20.1 0.8 %copy-start.4 = (bf16[128,128]{1,0:T(8,128)(2,1)S(1)}, bf16[128,128]{1,0:T(8,128)(2,1)}, u32[]{:S(2)}) copy-start(bf16[128,128]{1,0:T(8,128)(2,1)} %constant.9.clone.refs_3_) | copy-start | bytes 98308
  20.8 0.7 %copy-start.10 = (s32[32]{0:T(128)S(1)}, s32[32]{0:T(128)}, u32[]{:S(2)}) copy-start(s32[32]{0:T(128)} %cutoff_ref.5) | copy-start | bytes 388
  22.3 15.2 %copy-start.3 = (bf16[128,128]{1,0:T(8,128)(2,1)S(1)}, bf16[128,128]{1,0:T(8,128)(2,1)}, u32[]{:S(2)}) copy-start(bf16[128,128]{1,0:T(8,128)(2,1)} %constant.8.clone.refs_2_) | copy-start | bytes 98308
  22.3 15.2 %copy-start.5 = (bf16[128,128]{1,0:T(8,128)(2,1)S(1)}, bf16[128,128]{1,0:T(8,128)(2,1)}, u32[]{:S(2)}) copy-start(bf16[128,128]{1,0:T(8,128)(2,1)} %constant.9.clone.refs_3_) | copy-start | bytes 98308
  22.3 15.1 %copy-start.11 = (s32[32]{0:T(128)S(1)}, s32[32]{0:T(128)}, u32[]{:S(2)}) copy-start(s32[32]{0:T(128)} %cutoff_ref.5) | copy-start | bytes 388
  22.3 15.8 %collective-permute-start.10 = (f32[2,6,8,640]{3,2,1,0:T(8,128)S(1)}, f32[2,6,8,640]{3,2,1,0:T(8,128)S(1)}, u32[]{:S(2)}, u32[]{:S(2)}) collective-permute-start(f32[2,6,8,640]{3,2,1,0:T(8,128)S(1)} %get-tuple-element.31), channel_id=1, source_target_pairs={{0,4},{8,12},{4,0},{12,8},{1,5},{9,13},{5,1},{13,9},{2,6},{10,14},... | collective-permute-start | bytes 737288 | tf_op jit(solution)/shard_map/ppermute | solution.py:413
  24.0 12.6 %collective-permute-start.3 = (f32[1,8,8,576]{3,2,1,0:T(8,128)S(1)}, f32[1,8,8,576]{3,2,1,0:T(8,128)S(1)}, u32[]{:S(2)}, u32[]{:S(2)}) collective-permute-start(f32[1,8,8,576]{3,2,1,0:T(8,128)S(1)} %slice.9.refs_0_), channel_id=1, source_target_pairs={{0,2},{2,0},{1,3},{3,1},{4,6},{6,4},{5,7},{7,5},{8,10},{10,8},{9,1... | collective-permute-start | bytes 442376 | tf_op jit(solution)/shard_map/ppermute | solution.py:410
  26.1 20.5 %collective-permute-start.11 = (f32[2,6,8,640]{3,2,1,0:T(8,128)S(1)}, f32[2,6,8,640]{3,2,1,0:T(8,128)S(1)}, u32[]{:S(2)}, u32[]{:S(2)}) collective-permute-start(f32[2,6,8,640]{3,2,1,0:T(8,128)S(1)} %get-tuple-element.32), channel_id=1, source_target_pairs={{4,8},{8,4},{5,9},{9,5},{6,10},{10,6},{7,11},{11,7},{20,24},{24,20... | collective-permute-start | bytes 737288 | tf_op jit(solution)/shard_map/ppermute | solution.py:413
  31.0 20.2 %collective-permute-start.7 = (f32[2,6,8,640]{3,2,1,0:T(8,128)S(1)}, f32[2,6,8,640]{3,2,1,0:T(8,128)S(1)}, u32[]{:S(2)}, u32[]{:S(2)}) collective-permute-start(f32[2,6,8,640]{3,2,1,0:T(8,128)S(1)} %get-tuple-element.28), channel_id=1, source_target_pairs={{0,4},{8,12},{4,0},{12,8},{1,5},{9,13},{5,1},{13,9},{2,6},{10,14},... | collective-permute-start | bytes 737288 | tf_op jit(solution)/shard_map/ppermute | solution.py:413
  31.1 20.2 %collective-permute-start.8 = (f32[2,6,8,640]{3,2,1,0:T(8,128)S(1)}, f32[2,6,8,640]{3,2,1,0:T(8,128)S(1)}, u32[]{:S(2)}, u32[]{:S(2)}) collective-permute-start(f32[2,6,8,640]{3,2,1,0:T(8,128)S(1)} %get-tuple-element.29), channel_id=1, source_target_pairs={{4,8},{8,4},{5,9},{9,5},{6,10},{10,6},{7,11},{11,7},{20,24},{24,20... | collective-permute-start | bytes 737288 | tf_op jit(solution)/shard_map/ppermute | solution.py:413
  36.7 4.5 %collective-permute-start.2 = (f32[20,8,128]{2,1,0:T(8,128)S(1)}, f32[20,8,128]{2,1,0:T(8,128)S(1)}, u32[]{:S(2)}, u32[]{:S(2)}) collective-permute-start(f32[20,8,128]{2,1,0:T(8,128)S(1)} %get-tuple-element.23), channel_id=1, source_target_pairs={{0,2},{2,0},{1,3},{3,1},{4,6},{6,4},{5,7},{7,5},{8,10},{10,8},{9,1... | collective-permute-start | bytes 245768 | tf_op jit(solution)/shard_map/ppermute | solution.py:410
  38.2 17.8 %collective-permute-start.4 = (f32[1,6,8,640]{3,2,1,0:T(8,128)S(1)}, f32[1,6,8,640]{3,2,1,0:T(8,128)S(1)}, u32[]{:S(2)}, u32[]{:S(2)}) collective-permute-start(f32[1,6,8,640]{3,2,1,0:T(8,128)S(1)} %get-tuple-element.25), channel_id=1, source_target_pairs={{0,4},{8,12},{4,0},{12,8},{1,5},{9,13},{5,1},{13,9},{2,6},{10,14},... | collective-permute-start | bytes 368648 | tf_op jit(solution)/shard_map/ppermute | solution.py:413
  41.2 14.8 %collective-permute-start.5 = (f32[1,6,8,640]{3,2,1,0:T(8,128)S(1)}, f32[1,6,8,640]{3,2,1,0:T(8,128)S(1)}, u32[]{:S(2)}, u32[]{:S(2)}) collective-permute-start(f32[1,6,8,640]{3,2,1,0:T(8,128)S(1)} %get-tuple-element.26), channel_id=1, source_target_pairs={{4,8},{8,4},{5,9},{9,5},{6,10},{10,6},{7,11},{11,7},{20,24},{24,20... | collective-permute-start | bytes 368648 | tf_op jit(solution)/shard_map/ppermute | solution.py:413

commit v2 on v1

v2 whole, which is shorter than its diff:
```python
import functools
import math

import jax
import jax.numpy as jnp
import numpy as np
from jax import lax
from jax.experimental import pallas as pl
from jax.experimental.pallas import tpu as pltpu
from jax.sharding import PartitionSpec as P

SUBSTEPS = 6
HALO = SUBSTEPS
LANES = 128
RATES = 4
CHUNKS = (3, 2)
ROWS_AT_ONCE = 2
PARAMS = pltpu.CompilerParams(vmem_limit_bytes=12 * 2**20)
VMEM = pl.BlockSpec(memory_space=pltpu.VMEM)
HBM = pl.BlockSpec(memory_space=pltpu.HBM)


def split_bf16(values):
    high = values.astype(jnp.bfloat16)
    low = (values - high.astype(jnp.float32)).astype(jnp.bfloat16)
    return high, low


def split_bf16_numpy(values):
    values = values.astype(np.float32)
    high = values.astype(jnp.bfloat16)
    low = (values - high.astype(np.float32)).astype(jnp.bfloat16)
    return high, low


def mode_tables(length):
    ways = length // LANES
    point = np.arange(LANES)[:, None].astype(np.int64)
    column = np.arange(LANES)[None, :].astype(np.int64)
    half = LANES // 2
    wave = np.where(column <= half, column, column - half)
    angle = 2.0 * np.pi * (point * wave % LANES) / LANES
    weight = np.where((column == 0) | (column == half), 1.0 / LANES, 2.0 / LANES)
    real_block = np.where(column <= half, np.cos(angle), np.sin(angle)) * np.sqrt(weight)
    blocks = []
    for first in range(1, (ways + 1) // 2):
        angle = 2.0 * np.pi * (point * (first + ways * column) % length) / length
        cosine, sine = np.cos(angle), np.sin(angle)
        blocks.append(np.block([[cosine, -sine], [sine, cosine]]) / math.sqrt(LANES))
    block_high, block_low = split_bf16_numpy(np.stack(blocks))
    real = np.zeros((1, 2 * LANES, 2 * LANES), block_high.dtype)
    real[0, :LANES, :LANES], real[0, :LANES, LANES:] = split_bf16_numpy(real_block)
    return np.concatenate([block_high, block_low, real])


def dot_split(values, high_table, low_table, transposed):
    dims = (((1,), (1 if transposed else 0,)), ((), ()))
    count = values.shape[0]
    high, low = split_bf16(values)
    dot = functools.partial(lax.dot_general, dimension_numbers=dims, preferred_element_type=jnp.float32)
    main = dot(jnp.concatenate([high, low], axis=0), high_table)
    return main[:count] + (main[count:] + dot(high, low_table))


def damping_of(limit, wavenumber):
    ratio = limit / jnp.maximum(wavenumber, 1.0)
    return jnp.where(wavenumber > limit, ratio * ratio, 1.0)


def filter_kernel(sectors, edges, limit_ref, table, *refs):
    circle_refs = refs[:sectors]
    own_out, first_out, second_out = refs[sectors:sectors + 3]
    wide, real_wave, block_wave = refs[sectors + 3:]
    fields, levels, rows, width = circle_refs[0].shape
    sector = wide.shape[1] // sectors
    length = sector * sectors
    ways = length // LANES
    pairs = (ways - 1) // 2
    tiles = width // LANES
    per_field = levels * rows
    lat = lax.axis_index("lat")
    limit = limit_ref[...]

    for k in range(sectors):
        wide[:, k * sector:(k + 1) * sector] = circle_refs[k][:, :, :, :sector].reshape(fields * per_field, sector)

    @pl.when(jnp.min(limit) < length // 2)
    def _():
        lane = lax.broadcasted_iota(jnp.int32, (rows, LANES), 1)

        def forward(field, carry):
            span = pl.ds(pl.multiple_of(field * per_field, per_field), per_field)
            tile = [wide[span, a * LANES:(a + 1) * LANES] for a in range(ways)]
            even = [tile[a] + tile[ways - a] for a in range(1, pairs + 1)]
            odd = [tile[a] - tile[ways - a] for a in range(1, pairs + 1)]
            real_wave[span, :] = tile[0] + sum(even)
            for k in range(1, pairs + 1):
                turn = [2.0 * math.pi * (a * k % ways) / ways for a in range(1, pairs + 1)]
                block_wave[k - 1, span, :LANES] = tile[0] + sum(math.cos(t) * e for t, e in zip(turn, even))
                block_wave[k - 1, span, LANES:] = -sum(math.sin(t) * o for t, o in zip(turn, odd))
            return carry

        lax.fori_loop(0, fields, forward, 0)

        def damp(spectrum, damping):
            shaped = spectrum.reshape(fields * levels, rows, damping.shape[-1])
            return (shaped * damping[None]).reshape(spectrum.shape)

        half = LANES // 2
        wave = (jnp.where(lane <= half, lane, lane - half) * ways).astype(jnp.float32)
        real_high, real_low = table[2 * pairs, :LANES, :LANES], table[2 * pairs, :LANES, LANES:]
        spectrum = dot_split(real_wave[...], real_high, real_low, False)
        spectrum = damp(spectrum, damping_of(limit, wave))
        real_wave[...] = dot_split(spectrum, real_high, real_low, True)
        for k in range(1, pairs + 1):
            mode = k + ways * lane
            one = damping_of(limit, jnp.minimum(mode, length - mode).astype(jnp.float32))
            damping = jnp.concatenate([one, one], axis=1)
            high, low = table[k - 1], table[pairs + k - 1]
            spectrum = dot_split(block_wave[k - 1], high, low, False)
            block_wave[k - 1] = dot_split(damp(spectrum, damping), high, low, True)

        def backward(field, carry):
            span = pl.ds(pl.multiple_of(field * per_field, per_field), per_field)
            base = real_wave[span, :] * (1.0 / ways)
            cosines = [block_wave[k, span, :LANES] for k in range(pairs)]
            sines = [block_wave[k, span, LANES:] for k in range(pairs)]
            wide[span, :LANES] = base + (2.0 / ways) * sum(cosines)
            for a in range(1, pairs + 1):
                turn = [2.0 * math.pi * (a * k % ways) / ways for k in range(1, pairs + 1)]
                even = base + sum((2.0 / ways * math.cos(t)) * c for t, c in zip(turn, cosines))
                odd = sum((2.0 / ways * math.sin(t)) * s for t, s in zip(turn, sines))
                wide[span, a * LANES:(a + 1) * LANES] = even - odd
                wide[span, (ways - a) * LANES:(ways - a + 1) * LANES] = even + odd
            return carry

        lax.fori_loop(0, fields, backward, 0)

    def emit(field, carry):
        span = pl.ds(pl.multiple_of(field * per_field, per_field), per_field)
        lane = lax.broadcasted_iota(jnp.int32, (per_field, LANES), 1)
        for a in range(tiles):
            tile = wide[span, a * LANES:(a + 1) * LANES]
            if a == tiles - 1:
                behind = wide[span, (ways - 1) * LANES:]
                tile = jnp.where(lane >= LANES - HALO, behind, tile)
            turned = jnp.swapaxes(tile.reshape(levels, rows, LANES), 0, 1)
            own_out[pl.ds(field, 1), :, :, a * LANES:(a + 1) * LANES] = turned[None]
        return carry

    lax.fori_loop(0, fields, emit, 0)
    if edges:
        final = slice(width - LANES, width)
        ahead = jnp.swapaxes(circle_refs[1][0, :, :, final], 0, 1)
        behind = jnp.swapaxes(circle_refs[sectors - 1][0, :, :, final], 0, 1)
        first_lane = edge_lane(sector)
        lane = lax.broadcasted_iota(jnp.int32, (rows, levels, LANES), 2) - first_lane
        spare = jnp.where(lane % (2 * HALO) < HALO, ahead, behind)
        spare = jnp.where((lane >= 0) & (lane < RATES * 2 * HALO), spare, own_out[0, :, :, final])
        own_out[0, :, :, final] = spare

    top = rows - HALO
    to_next = lax.rem(lat, 2) == 0

    @pl.when(to_next)
    def _():
        first_out[...] = own_out[:, top:]
        second_out[...] = own_out[:, :HALO]

    @pl.when(jnp.logical_not(to_next))
    def _():
        first_out[...] = own_out[:, :HALO]
        second_out[...] = own_out[:, top:]


def edge_lane(sector):
    return sector % LANES + HALO


def limits_of(cutoff, rows):
    lat = lax.axis_index("lat")
    own = lax.dynamic_slice_in_dim(cutoff, lat * rows, rows, 0).astype(jnp.float32)
    return jnp.broadcast_to(own[:, None], (rows, LANES))


def pack_kernel(chunks, adjoint, *refs):
    sources = (adjoint,) + refs[:RATES]
    count = len(chunks)
    payloads = refs[RATES:RATES + count]
    own_out, first_out, second_out = refs[RATES + count:RATES + count + 3]
    state, rates, sems = refs[RATES + count + 3:]
    levels, rows, sector = sources[1].shape
    width = own_out.shape[-1]
    final = slice(width - LANES, width)
    tail = sector - (width - LANES)
    copies = [pltpu.make_async_copy(src, rates.at[q], sems.at[q]) for q, src in enumerate(sources[1:])]
    copies.append(pltpu.make_async_copy(adjoint, state, sems.at[RATES]))
    for copy in copies:
        copy.start()
    for copy in copies[:RATES]:
        copy.wait()
    lat = lax.axis_index("lat")
    is_last = lat == lax.axis_size("lat") - 1
    lane = lax.broadcasted_iota(jnp.int32, (levels, rows, LANES), 2)
    row = lax.broadcasted_iota(jnp.int32, (levels, rows, LANES), 1)
    edges = jnp.zeros((levels, rows, LANES), jnp.float32)
    for q in range(RATES):
        at = edge_lane(sector) + 2 * HALO * q
        for start in range(0, width, LANES):
            size = min(LANES, sector - start)
            tile = rates[q, :, :, start:start + size]
            if size < LANES:
                tile = jnp.concatenate([tile, jnp.zeros((levels, rows, LANES - size), jnp.float32)], axis=2)
            if q == 0:
                tile = jnp.where(jnp.logical_and(is_last, row == rows - 1), 0.0, tile)
            own_out[:, q, :, start:start + LANES] = jnp.swapaxes(tile, 0, 1)
            if start == 0:
                initial = pltpu.roll(tile, at, 2)
                edges = jnp.where((lane >= at) & (lane < at + HALO), initial, edges)
            if start == width - LANES:
                last = pltpu.roll(tile, (at + HALO - (tail - HALO)) % LANES, 2)
                edges = jnp.where((lane >= at + HALO) & (lane < at + 2 * HALO), last, edges)
    copies[RATES].wait()
    field = 0
    for c in range(count):
        for j in range(chunks[c]):
            payloads[c][j, :, :, :width - LANES] = state[field, :, :, :width - LANES]
            end = state[field, :, :, width - LANES:]
            end = jnp.concatenate([end, jnp.zeros((levels, rows, LANES - tail), jnp.float32)], axis=2)
            if field == 0:
                end = jnp.where(lane < tail, end, edges)
            payloads[c][j, :, :, final] = end
            field += 1
    top = rows - HALO
    to_next = lax.rem(lat, 2) == 0

    @pl.when(to_next)
    def _():
        first_out[...] = own_out[top:]
        second_out[...] = own_out[:HALO]

    @pl.when(jnp.logical_not(to_next))
    def _():
        first_out[...] = own_out[:HALO]
        second_out[...] = own_out[top:]


def by_side(first_ref, second_ref, use):
    to_next = lax.rem(lax.axis_index("lat"), 2) == 0

    @pl.when(to_next)
    def _():
        use(second_ref, first_ref)

    @pl.when(jnp.logical_not(to_next))
    def _():
        use(first_ref, second_ref)


def coupling_power(coupling_ref):
    fields, levels, _ = coupling_ref.shape
    base = []
    for g in range(fields):
        line = coupling_ref[g]
        base.append([jnp.broadcast_to(line[:, f:f + 1], (levels, LANES)) for f in range(fields)])
        base[g][g] = base[g][g] + 1.0

    def product(left, right):
        def entry(g, f):
            return functools.reduce(jnp.add, [left[g][h] * right[h][f] for h in range(fields)])

        return [[entry(g, f) for f in range(fields)] for g in range(fields)]

    power = base
    for bit in bin(SUBSTEPS)[3:]:
        power = product(power, power)
        if bit == "1":
            power = product(power, base)
    return power


def face_kernel(sector, coupling, rate_own, rate_first, rate_second, own, first, second, level, moved, power_out):
    power = coupling_power(coupling)
    for g, entries in enumerate(power):
        for f, value in enumerate(entries):
            power_out[g, f] = value
    rows, kinds, levels, width = rate_own.shape
    extent = rows + 2 * HALO
    tiles = width // LANES
    final = slice(width - LANES, width)
    lane = lax.broadcasted_iota(jnp.int32, (levels, LANES), 1)
    end = sector % LANES

    def extend(ref, edge_ref, base):
        count = ref.shape[0]
        for q in range(kinds):
            at = edge_lane(sector) + 2 * HALO * q
            edges = [edge_ref[0, r, :, final] for r in range(count)]
            ahead = [pltpu.roll(e, (end - at) % LANES, 1) for e in edges]
            behind = [pltpu.roll(e, (LANES - HALO - at - HALO) % LANES, 1) for e in edges]
            for r in range(count):
                piece = jnp.where((lane >= end) & (lane < end + HALO), ahead[r], ref[r, q, :, final])
                piece = jnp.where(lane >= LANES - HALO, behind[r], piece)
                level[base + r, q, :, :width - LANES] = ref[r, q, :, :width - LANES]
                level[base + r, q, :, final] = piece

    extend(rate_own, own, HALO)

    def halos(below, above, below_edges, above_edges):
        extend(below, below_edges, 0)
        extend(above, above_edges, HALO + rows)

    to_next = lax.rem(lax.axis_index("lat"), 2) == 0

    @pl.when(to_next)
    def _():
        halos(rate_second, rate_first, second, first)

    @pl.when(jnp.logical_not(to_next))
    def _():
        halos(rate_first, rate_second, first, second)

    def combine(step, carry):
        r = extent - 2 - step

        def tiles_of(index, q):
            return [level[index, q, :, t * LANES:(t + 1) * LANES] for t in range(tiles)]

        north, south, east, behind = tiles_of(r, 0), tiles_of(r - 1, 1), tiles_of(r, 2), tiles_of(r, 3)
        west = shifted(behind, 1)
        north_moved, south_moved, east_moved = shifted(north, -1), shifted(south, -1), shifted(east, -1)
        for t in range(tiles):
            span = slice(t * LANES, (t + 1) * LANES)
            level[r, 1, :, span] = south[t]
            level[r, 3, :, span] = west[t]
            level[r, 4, :, span] = 1.0 - east[t] - west[t] - north[t] - south[t]
            moved[r, 0, :, span] = north_moved[t]
            moved[r, 1, :, span] = south_moved[t]
            moved[r, 2, :, span] = east_moved[t]
            moved[r, 3, :, span] = behind[t]
            moved[r, 4, :, span] = 1.0 - east_moved[t] - behind[t] - north_moved[t] - south_moved[t]
        return carry

    lax.fori_loop(0, extent - 2, combine, 0)


def shifted(tiles, step):
    lane = lax.broadcasted_iota(jnp.int32, tiles[0].shape, 1)
    rolled = [pltpu.roll(tile, step % LANES, 1) for tile in tiles]
    border = lane == (0 if step == 1 else LANES - 1)
    count = len(tiles)
    return [jnp.where(border, rolled[(t - step) % count], rolled[t]) for t in range(count)]


def transport_kernel(chunk, finished, sector, power_ref, level, moved, own_ref, first_ref, second_ref, *refs):
    earlier = refs[:finished]
    out_ref, even, odd = refs[finished:]
    rows, levels, width = own_ref.shape[1:]
    extent = rows + 2 * HALO
    tiles = width // LANES
    last = finished > 0

    def put(ref, base):
        even[:, base:base + ref.shape[1]] = ref[...]

    put(own_ref, HALO)

    def halos(below, above):
        put(below, 0)
        put(above, HALO + rows)

    by_side(first_ref, second_ref, halos)

    def line(source, r, field):
        return [source[field, r, :, t * LANES:(t + 1) * LANES] for t in range(tiles)]

    for step in range(SUBSTEPS):
        forward = step % 2 == 0
        source, target, rates, way = (even, odd, moved, -1) if forward else (odd, even, level, 1)

        def move(r, field, below, here, above, twice):
            for t in range(tiles):
                span = slice(t * LANES, (t + 1) * LANES)
                north, south, east, west, stay = (rates[r, q, :, span] for q in range(5))
                plain = source[field, r, :, span]
                ahead, behind = (twice[t], plain) if forward else (plain, twice[t])
                target[field, r, :, span] = (
                    (stay * here[t] + (north * above[t] + south * below[t]))
                    + (east * ahead + west * behind)
                )

        for field in range(chunk):
            def turn(r):
                return shifted(line(source, r, field), way)

            def some_rows(index, carry):
                r = step + 1 + ROWS_AT_ONCE * index
                below, here = carry[:tiles], carry[tiles:]
                for j in range(ROWS_AT_ONCE):
                    above = turn(r + j + 1)
                    move(r + j, field, below, here, above, shifted(here, way))
                    below, here = here, above
                return tuple(below) + tuple(here)

            count = extent - 2 - 2 * step
            start = tuple(turn(step)) + tuple(turn(step + 1))
            lax.fori_loop(0, count // ROWS_AT_ONCE, some_rows, start, unroll=2)
    result = even if SUBSTEPS % 2 == 0 else odd

    if not last:
        out_ref[...] = result[:, HALO:HALO + rows]
        return
    sources = [(ref, j, 0) for ref in earlier for j in range(ref.shape[0])]
    sources += [(result, j, HALO) for j in range(chunk)]
    fields = len(sources)
    for start in range(0, sector, LANES):
        stop = min(start + LANES, sector)
        values = [ref[j, base:base + rows, :, start:start + LANES] for ref, j, base in sources]
        for f in range(fields):
            total = functools.reduce(jnp.add, [power_ref[g, f][None] * values[g] for g in range(fields)])
            out_ref[f, :, :, start:stop] = jnp.swapaxes(total, 0, 1)[:, :, :stop - start]


def lat_pairs(count):
    def both(start):
        ups = [(i, i + 1) for i in range(start, count - 1, 2)]
        return ups + [(j, i) for i, j in ups]

    return both(0), both(1)


def shards(adjoint_in, lat_ahead, lat_behind, lon_ahead, lon_behind, coupling, cutoff):
    fields, levels, rows, sector = adjoint_in.shape
    sectors = lax.axis_size("lon")
    length = sector * sectors
    width = -(-(sector + 2 * HALO) // LANES) * LANES
    even_pairs, odd_pairs = lat_pairs(lax.axis_size("lat"))
    f32 = jnp.float32
    chunks = CHUNKS if sum(CHUNKS) == fields else (fields,)

    def sector_ahead(values, offset):
        return lax.ppermute(values, "lon", [(s, (s - offset) % sectors) for s in range(sectors)])

    def to_bands(first, second):
        return lax.ppermute(first, "lat", even_pairs), lax.ppermute(second, "lat", odd_pairs)

    extent = rows + 2 * HALO
    rate_shape = (RATES, levels, width)
    *payloads, rate_own, rate_first, rate_second = pl.pallas_call(
        functools.partial(pack_kernel, chunks),
        out_shape=(
            *(jax.ShapeDtypeStruct((n, levels, rows, width), f32) for n in chunks),
            jax.ShapeDtypeStruct((rows,) + rate_shape, f32),
            jax.ShapeDtypeStruct((HALO,) + rate_shape, f32),
            jax.ShapeDtypeStruct((HALO,) + rate_shape, f32),
        ),
        in_specs=[HBM] * (1 + RATES),
        out_specs=(VMEM,) * (len(chunks) + 3),
        scratch_shapes=[
            pltpu.VMEM(adjoint_in.shape, f32),
            pltpu.VMEM((RATES,) + lat_ahead.shape, f32),
            pltpu.SemaphoreType.DMA((1 + RATES,)),
        ],
        compiler_params=PARAMS,
        name="pack",
    )(adjoint_in, lat_ahead, lat_behind, lon_ahead, lon_behind)
    circles = [[part] + [sector_ahead(part, k) for k in range(1, sectors)] for part in payloads]
    rate_first, rate_second = to_bands(rate_first, rate_second)

    limits = limits_of(cutoff, rows)
    table = jnp.asarray(mode_tables(length))
    results = []
    for c, (n, circle) in enumerate(zip(chunks, circles)):
        lines = n * levels * rows
        own, first, second = pl.pallas_call(
            functools.partial(filter_kernel, sectors, c == 0),
            out_shape=(
                jax.ShapeDtypeStruct((n, rows, levels, width), f32),
                jax.ShapeDtypeStruct((n, HALO, levels, width), f32),
                jax.ShapeDtypeStruct((n, HALO, levels, width), f32),
            ),
            in_specs=[VMEM] * (sectors + 2),
            out_specs=(VMEM,) * 3,
            scratch_shapes=[
                pltpu.VMEM((lines, length), f32),
                pltpu.VMEM((lines, LANES), f32),
                pltpu.VMEM((table.shape[0] // 2, lines, 2 * LANES), f32),
            ],
            compiler_params=PARAMS,
            name="polar_filter",
        )(limits, table, *circle)
        first, second = to_bands(first, second)
        if c == 0:
            level, moved, power = pl.pallas_call(
                functools.partial(face_kernel, sector),
                out_shape=(
                    jax.ShapeDtypeStruct((extent, 5, levels, width), f32),
                    jax.ShapeDtypeStruct((extent, 5, levels, width), f32),
                    jax.ShapeDtypeStruct((fields, fields, levels, LANES), f32),
                ),
                in_specs=[VMEM] * 7,
                out_specs=(VMEM,) * 3,
                compiler_params=PARAMS,
                name="faces",
            )(jnp.transpose(coupling, (1, 0, 2)), rate_own, rate_first, rate_second, own, first, second)
        is_last = c == len(chunks) - 1
        earlier = results if is_last else []
        shape = adjoint_in.shape if is_last else (n, rows, levels, width)
        results.append(pl.pallas_call(
            functools.partial(transport_kernel, n, len(earlier), sector),
            out_shape=jax.ShapeDtypeStruct(shape, f32),
            in_specs=[VMEM] * (6 + len(earlier)),
            out_specs=VMEM,
            scratch_shapes=[
                pltpu.VMEM((n, extent, levels, width), f32),
                pltpu.VMEM((n, extent, levels, width), f32),
            ],
            compiler_params=PARAMS,
            name="transport",
        )(power, level, moved, own, first, second, *earlier))
    return results[-1]


def solution(mesh):
    placed = (
        P("member", "lev", "lat", "lon"),
        P(("member", "lev"), "lat", "lon"),
        P(("member", "lev"), "lat", "lon"),
        P(("member", "lev"), "lat", "lon"),
        P(("member", "lev"), "lat", "lon"),
        P("lev", None, None),
        P(),
    )
    return jax.shard_map(
        shards,
        mesh=mesh,
        in_specs=placed,
        out_specs=P("member", "lev", "lat", "lon"),
        check_vma=False,
    )
```

time: 61.8 us -> 59.2 us (0.958)
  starting transfers between devices: 20.5 us -> 15 us
  Pallas kernels: 21.9 us -> 26.2 us
  local copies, waits for them, and re-layouts: 8.01 us -> 4.98 us
  waiting for transfers between devices: 10.4 us -> 11.8 us
  other arithmetic: 0 us -> 0.73 us
    ppermute x4 -> x3, starting transfers between devices: 11.9 us -> 5.73 us  [to_bands(): lax.ppermute(second, 'lat', odd_pairs)]
    pallas_call x3 -> x2, Pallas kernels: 14.4 us -> 19.1 us  [shards(): pl.pallas_call(functools.partial(transport_kernel, n, len(earlier), secto...]
    ppermute x4 -> x3, waiting for transfers between devices: 0.01 us -> 3.34 us  [to_bands(): lax.ppermute(second, 'lat', odd_pairs)]
    ppermute x4 -> x3, starting transfers between devices: 4.21 us -> 7.16 us  [to_bands(): lax.ppermute(first, 'lat', even_pairs)]
    ppermute x4 -> x2, waiting for transfers between devices: 10.4 us -> 7.94 us  [sector_ahead(): lax.ppermute(values, 'lon', [(s, (s - offset) % sectors) for s in range(s...]
    ppermute x4 -> x2, starting transfers between devices: 4.4 us -> 2.09 us  [sector_ahead(): lax.ppermute(values, 'lon', [(s, (s - offset) % sectors) for s in range(s...]
    slice x2 -> x0, local copies, waits for them, and re-layouts: 2.05 us -> none  [shards(): parts = [adjoint_in[s:s + n] for s, n in zip(starts, chunks)]]
    unnamed x27 -> x14, local copies, waits for them, and re-layouts: 5.96 us -> 4.91 us
  transfers between devices with their start and end apart: 12 -> 8, of which waited for: 3 -> 3; matrix products, arithmetic and copies ran while one was open for 3% -> 1% of each run, Pallas kernels for 27% -> 26%
where the time goes in v2:
time: 59.2 us; the launch traced here: 58.9 us
  Pallas kernels  26.2 us (44%)
  starting transfers between devices  15 us (25%)
  waiting for transfers between devices  11.8 us (20%)
  local copies, waits for them, and re-layouts  4.98 us (8%)
  other arithmetic  0.73 us (1%)
    pallas_call x2, Pallas kernels, shards(): pl.pallas_call(functools.partial(transport_kernel, n, len(earlier), secto...  19.1 us
    ppermute x2, waiting for transfers between devices, sector_ahead(): lax.ppermute(values, 'lon', [(s, (s - offset) % sectors) for s in range(s...  7.94 us
    ppermute x3, starting transfers between devices, to_bands(): lax.ppermute(first, 'lat', even_pairs)  7.16 us
    ppermute x3, starting transfers between devices, to_bands(): lax.ppermute(second, 'lat', odd_pairs)  5.73 us
    unnamed x14, local copies, waits for them, and re-layouts  4.91 us
    ppermute x3, waiting for transfers between devices, to_bands(): lax.ppermute(second, 'lat', odd_pairs)  3.34 us
    pallas_call x2, Pallas kernels, shards(): pl.pallas_call(functools.partial(filter_kernel, sectors, c == 0), out_sha...  2.79 us
    pallas_call x1, Pallas kernels, shards(): pl.pallas_call(functools.partial(pack_kernel, chunks), out_shape=(*(jax.S...  2.34 us
  transfers between devices with their start and end apart: 8, of which 3 were waited for; matrix products, arithmetic and copies ran while one was open for 1% of the time, Pallas kernels for 26%

profile of v2, /device:TPU:16, one launch (start us, length us, event | category | flops | bytes accessed | tf_op | source)
XLA Modules:
  0.0 58.9 jit_solution(2882108563109736579)
XLA Ops:
  0.0 1.2 %copy-done.1 = f32[5,8,8,576]{3,2,1,0:T(8,128)S(1)} copy-done((f32[5,8,8,576]{3,2,1,0:T(8,128)S(1)}, f32[5,8,8,576]{3,2,1,0:T(8,128)}, u32[]{:S(2)}) %copy-start.1) | copy-done | bytes 737304
  1.2 0.9 %copy-done.2 = f32[8,8,576]{2,1,0:T(8,128)S(1)} copy-done((f32[8,8,576]{2,1,0:T(8,128)S(1)}, f32[8,8,576]{2,1,0:T(8,128)}, u32[]{:S(2)}) %copy-start.2) | copy-done | bytes 147480
  2.2 0.9 %copy-done.3 = f32[8,8,576]{2,1,0:T(8,128)S(1)} copy-done((f32[8,8,576]{2,1,0:T(8,128)S(1)}, f32[8,8,576]{2,1,0:T(8,128)}, u32[]{:S(2)}) %copy-start.3) | copy-done | bytes 147480
  3.1 0.9 %copy-done.4 = f32[8,8,576]{2,1,0:T(8,128)S(1)} copy-done((f32[8,8,576]{2,1,0:T(8,128)S(1)}, f32[8,8,576]{2,1,0:T(8,128)}, u32[]{:S(2)}) %copy-start.4) | copy-done | bytes 147480
  4.0 0.9 %copy-done.5 = f32[8,8,576]{2,1,0:T(8,128)S(1)} copy-done((f32[8,8,576]{2,1,0:T(8,128)S(1)}, f32[8,8,576]{2,1,0:T(8,128)}, u32[]{:S(2)}) %copy-start.5) | copy-done | bytes 147480
  4.9 2.3 %pack.1 = (f32[3,8,8,640]{3,2,1,0:T(8,128)S(1)}, f32[2,8,8,640]{3,2,1,0:T(8,128)}, f32[8,4,8,640]{3,2,1,0:T(8,128)S(1)}, f32[6,4,8,640]{3,2,1,0:T(8,128)}, f32[6,4,8,640]{3,2,1,0:T(8,128)}) custom-call(f32[5,8,8,576]{3,2,1,0:T(8,128)S(1)} %copy-done.1, f32[8,8,576]{2,1,0:T(8,128)S(1)} %copy-done.2, f32[8,8,576]{2,1,0:T(8,128)S(1)} %copy-done.3, ...), custom_call_target="tpu_custom_call" | custom-call | tf_op jit(solution)/shard_map/pack/pallas_call | solution.py:449
  7.3 0.0 copy-start.6
  7.3 1.6 %collective-permute-start.2 = (f32[3,8,8,640]{3,2,1,0:T(8,128)S(1)}, f32[3,8,8,640]{3,2,1,0:T(8,128)}, u32[]{:S(2)}, u32[]{:S(2)}) collective-permute-start(f32[3,8,8,640]{3,2,1,0:T(8,128)S(1)} %get-tuple-element.22.refs_0_), channel_id=1, source_target_pairs={{0,2},{2,0},{1,3},{3,1},{4,6},{6,4},{5,7},{7,5},{8,10},{10,8},{9,1... | collective-permute-start | bytes 1474568 | tf_op jit(solution)/shard_map/ppermute | solution.py:442
  8.8 1.6 %collective-permute-start = (f32[6,4,8,640]{3,2,1,0:T(8,128)}, f32[6,4,8,640]{3,2,1,0:T(8,128)S(1)}, u32[]{:S(2)}, u32[]{:S(2)}) collective-permute-start(f32[6,4,8,640]{3,2,1,0:T(8,128)} %get-tuple-element.20), channel_id=1, source_target_pairs={{0,4},{8,12},{4,0},{12,8},{1,5},{9,13},{5,1},{13,9},{2,6},{10,14},... | collective-permute-start | bytes 1474568 | tf_op jit(solution)/shard_map/ppermute | solution.py:445
  10.4 0.5 collective-permute-start.5
  10.9 1.9 %collective-permute-start.1 = (f32[6,4,8,640]{3,2,1,0:T(8,128)}, f32[6,4,8,640]{3,2,1,0:T(8,128)S(1)}, u32[]{:S(2)}, u32[]{:S(2)}) collective-permute-start(f32[6,4,8,640]{3,2,1,0:T(8,128)} %get-tuple-element.21), channel_id=1, source_target_pairs={{4,8},{8,4},{5,9},{9,5},{6,10},{10,6},{7,11},{11,7},{20,24},{24,20... | collective-permute-start | bytes 1474568 | tf_op jit(solution)/shard_map/ppermute | solution.py:445
  12.9 0.7 %dynamic-slice_convert_fusion = f32[8]{0:T(128)S(1)} fusion(s32[32]{0:T(128)} %param.14, s32[]{:T(128)S(6)} %select_n.3), kind=kLoop, calls=%fused_computation | loop fusion | flops 8 | bytes 68 | tf_op jit(solution)/shard_map/convert_element_type | solution.py:182
  13.6 7.9 %collective-permute-done.2.refs_1_ = f32[3,8,8,640]{3,2,1,0:T(8,128)} collective-permute-done((f32[3,8,8,640]{3,2,1,0:T(8,128)S(1)}, f32[3,8,8,640]{3,2,1,0:T(8,128)}, u32[]{:S(2)}, u32[]{:S(2)}) %collective-permute-start.2) | collective-permute-done | bytes 491552 | tf_op jit(solution)/shard_map/ppermute | solution.py:442
  21.5 0.1 broadcast_in_dim.2.limit_ref
  21.6 0.0 copy-done
  21.6 1.4 %polar_filter.2 = (f32[3,8,8,640]{3,2,1,0:T(8,128)S(1)}, f32[3,6,8,640]{3,2,1,0:T(8,128)S(1)}, f32[3,6,8,640]{3,2,1,0:T(8,128)S(1)}) custom-call(f32[8,128]{1,0:T(8,128)S(1)} %broadcast_in_dim.2.limit_ref, bf16[9,256,256]{2,1,0:T(8,128)(2,1)S(1)} %copy-done, f32[3,8,8,640]{3,2,1,0:T(8,128)S(1)} %get-tuple-element.22.refs_0_, ...), custom_call_target="tpu_custom_call" | custom-call | tf_op jit(solution)/shard_map/polar_filter/pallas_call | solution.py:475
  23.0 3.4 %collective-permute-start.3 = (f32[3,6,8,640]{3,2,1,0:T(8,128)S(1)}, f32[3,6,8,640]{3,2,1,0:T(8,128)S(1)}, u32[]{:S(2)}, u32[]{:S(2)}) collective-permute-start(f32[3,6,8,640]{3,2,1,0:T(8,128)S(1)} %get-tuple-element.24), channel_id=1, source_target_pairs={{0,4},{8,12},{4,0},{12,8},{1,5},{9,13},{5,1},{13,9},{2,6},{10,14},... | collective-permute-start | bytes 1105928 | tf_op jit(solution)/shard_map/ppermute | solution.py:445
  26.5 1.9 %collective-permute-start.4 = (f32[3,6,8,640]{3,2,1,0:T(8,128)S(1)}, f32[3,6,8,640]{3,2,1,0:T(8,128)S(1)}, u32[]{:S(2)}, u32[]{:S(2)}) collective-permute-start(f32[3,6,8,640]{3,2,1,0:T(8,128)S(1)} %get-tuple-element.25), channel_id=1, source_target_pairs={{4,8},{8,4},{5,9},{9,5},{6,10},{10,6},{7,11},{11,7},{20,24},{24,20... | collective-permute-start | bytes 1105928 | tf_op jit(solution)/shard_map/ppermute | solution.py:445
  28.4 0.0 collective-permute-done.5.refs_1_
  28.4 1.4 %polar_filter.3 = (f32[2,8,8,640]{3,2,1,0:T(8,128)S(1)}, f32[2,6,8,640]{3,2,1,0:T(8,128)S(1)}, f32[2,6,8,640]{3,2,1,0:T(8,128)S(1)}) custom-call(f32[8,128]{1,0:T(8,128)S(1)} %broadcast_in_dim.2.limit_ref, bf16[9,256,256]{2,1,0:T(8,128)(2,1)S(1)} %copy-done, f32[2,8,8,640]{3,2,1,0:T(8,128)} %get-tuple-element.29.refs_0_, ...), custom_call_target="tpu_custom_call" | custom-call | tf_op jit(solution)/shard_map/polar_filter/pallas_call | solution.py:475
  29.8 2.1 %collective-permute-start.6 = (f32[2,6,8,640]{3,2,1,0:T(8,128)S(1)}, f32[2,6,8,640]{3,2,1,0:T(8,128)S(1)}, u32[]{:S(2)}, u32[]{:S(2)}) collective-permute-start(f32[2,6,8,640]{3,2,1,0:T(8,128)S(1)} %get-tuple-element.31), channel_id=1, source_target_pairs={{0,4},{8,12},{4,0},{12,8},{1,5},{9,13},{5,1},{13,9},{2,6},{10,14},... | collective-permute-start | bytes 737288 | tf_op jit(solution)/shard_map/ppermute | solution.py:445
  31.9 0.0 collective-permute-done.rate_first
  31.9 1.9 %collective-permute-start.7 = (f32[2,6,8,640]{3,2,1,0:T(8,128)S(1)}, f32[2,6,8,640]{3,2,1,0:T(8,128)S(1)}, u32[]{:S(2)}, u32[]{:S(2)}) collective-permute-start(f32[2,6,8,640]{3,2,1,0:T(8,128)S(1)} %get-tuple-element.32), channel_id=1, source_target_pairs={{4,8},{8,4},{5,9},{9,5},{6,10},{10,6},{7,11},{11,7},{20,24},{24,20... | collective-permute-start | bytes 737288 | tf_op jit(solution)/shard_map/ppermute | solution.py:445
  33.8 0.0 collective-permute-done.1.rate_second
  33.8 0.6 collective-permute-done.3.first.first_ref
  34.4 3.3 %collective-permute-done.4.second.second_ref = f32[3,6,8,640]{3,2,1,0:T(8,128)S(1)} collective-permute-done((f32[3,6,8,640]{3,2,1,0:T(8,128)S(1)}, f32[3,6,8,640]{3,2,1,0:T(8,128)S(1)}, u32[]{:S(2)}, u32[]{:S(2)}) %collective-permute-start.4) | collective-permute-done | bytes 368672 | tf_op jit(solution)/shard_map/ppermute | solution.py:445
  37.7 0.0 copy-done.6
  37.7 2.0 %faces.1 = (f32[20,5,8,640]{3,2,1,0:T(8,128)S(1)}, f32[20,5,8,640]{3,2,1,0:T(8,128)S(1)}, f32[5,5,8,128]{3,2,1,0:T(8,128)S(1)}) custom-call(f32[5,8,5]{2,1,0:T(8,128)S(1)} %bitcast.1, f32[8,4,8,640]{3,2,1,0:T(8,128)S(1)} %get-tuple-element.19.rate_own, f32[6,4,8,640]{3,2,1,0:T(8,128)S(1)} %collective-permute-done.rate_first, ...), custom_call_target="tpu_custom_call" | custom-call | tf_op jit(solution)/shard_map/faces/pallas_call | solution.py:494
  39.8 10.7 %transport.2.refs_0_ = f32[3,8,8,640]{3,2,1,0:T(8,128)S(1)} custom-call(f32[5,5,8,128]{3,2,1,0:T(8,128)S(1)} %get-tuple-element.26.power_ref, f32[20,5,8,640]{3,2,1,0:T(8,128)S(1)} %get-tuple-element.27.level, f32[20,5,8,640]{3,2,1,0:T(8,128)S(1)} %get-tuple-element.28.moved, f32[3,8,8,640]{3,2,1,0:T(8,128)S(1)} %get-tuple-element.23.own.own_ref, ...), custom_call_target="tpu_custom_call" | custom-call | tf_op jit(solution)/shard_map/transport/pallas_call | solution.py:509
  50.5 0.0 collective-permute-done.6.first_ref
  50.5 0.0 collective-permute-done.7.second_ref
  50.5 8.4 %transport.3 = f32[5,8,8,576]{3,2,1,0:T(8,128)} custom-call(f32[5,5,8,128]{3,2,1,0:T(8,128)S(1)} %get-tuple-element.26.power_ref, f32[20,5,8,640]{3,2,1,0:T(8,128)S(1)} %get-tuple-element.27.level, f32[20,5,8,640]{3,2,1,0:T(8,128)S(1)} %get-tuple-element.28.moved, f32[2,8,8,640]{3,2,1,0:T(8,128)S(1)} %get-tuple-element.30.own_ref, ...), custom_call_target="tpu_custom_call" | custom-call | tf_op jit(solution)/shard_map/transport/pallas_call | solution.py:509
  (6 shorter events, 0.0 us)
Async XLA Ops:
  0.0 21.6 %copy-start = (bf16[9,256,256]{2,1,0:T(8,128)(2,1)S(1)}, bf16[9,256,256]{2,1,0:T(8,128)(2,1)}, u32[]{:S(2)}) copy-start(bf16[9,256,256]{2,1,0:T(8,128)(2,1)} %constant.13.clone.table) | copy-start | bytes 3538948
  0.0 1.2 %copy-start.1 = (f32[5,8,8,576]{3,2,1,0:T(8,128)S(1)}, f32[5,8,8,576]{3,2,1,0:T(8,128)}, u32[]{:S(2)}) copy-start(f32[5,8,8,576]{3,2,1,0:T(8,128)} %adjoint.1) | copy-start | bytes 2211844
  1.2 0.9 %copy-start.2 = (f32[8,8,576]{2,1,0:T(8,128)S(1)}, f32[8,8,576]{2,1,0:T(8,128)}, u32[]{:S(2)}) copy-start(f32[8,8,576]{2,1,0:T(8,128)} %refs_0_.1) | copy-start | bytes 442372
  2.2 0.9 %copy-start.3 = (f32[8,8,576]{2,1,0:T(8,128)S(1)}, f32[8,8,576]{2,1,0:T(8,128)}, u32[]{:S(2)}) copy-start(f32[8,8,576]{2,1,0:T(8,128)} %refs_1_.1) | copy-start | bytes 442372
  3.1 0.9 %copy-start.4 = (f32[8,8,576]{2,1,0:T(8,128)S(1)}, f32[8,8,576]{2,1,0:T(8,128)}, u32[]{:S(2)}) copy-start(f32[8,8,576]{2,1,0:T(8,128)} %refs_2_.1) | copy-start | bytes 442372
  4.0 0.9 %copy-start.5 = (f32[8,8,576]{2,1,0:T(8,128)S(1)}, f32[8,8,576]{2,1,0:T(8,128)}, u32[]{:S(2)}) copy-start(f32[8,8,576]{2,1,0:T(8,128)} %refs_3_.1) | copy-start | bytes 442372
  7.3 30.5 %copy-start.6 = (f32[8,5,5]{2,0,1:T(8,128)S(1)}, f32[8,5,5]{2,0,1:T(8,128)}, u32[]{:S(2)}) copy-start(f32[8,5,5]{2,0,1:T(8,128)} %param.13) | copy-start | bytes 2404
  7.3 14.3 %collective-permute-start.2 = (f32[3,8,8,640]{3,2,1,0:T(8,128)S(1)}, f32[3,8,8,640]{3,2,1,0:T(8,128)}, u32[]{:S(2)}, u32[]{:S(2)}) collective-permute-start(f32[3,8,8,640]{3,2,1,0:T(8,128)S(1)} %get-tuple-element.22.refs_0_), channel_id=1, source_target_pairs={{0,2},{2,0},{1,3},{3,1},{4,6},{6,4},{5,7},{7,5},{8,10},{10,8},{9,1... | collective-permute-start | bytes 1474568 | tf_op jit(solution)/shard_map/ppermute | solution.py:442
  8.8 23.1 %collective-permute-start = (f32[6,4,8,640]{3,2,1,0:T(8,128)}, f32[6,4,8,640]{3,2,1,0:T(8,128)S(1)}, u32[]{:S(2)}, u32[]{:S(2)}) collective-permute-start(f32[6,4,8,640]{3,2,1,0:T(8,128)} %get-tuple-element.20), channel_id=1, source_target_pairs={{0,4},{8,12},{4,0},{12,8},{1,5},{9,13},{5,1},{13,9},{2,6},{10,14},... | collective-permute-start | bytes 1474568 | tf_op jit(solution)/shard_map/ppermute | solution.py:445
  10.4 18.0 %collective-permute-start.5 = (f32[2,8,8,640]{3,2,1,0:T(8,128)}, f32[2,8,8,640]{3,2,1,0:T(8,128)}, u32[]{:S(2)}, u32[]{:S(2)}) collective-permute-start(f32[2,8,8,640]{3,2,1,0:T(8,128)} %get-tuple-element.29.refs_0_), channel_id=1, source_target_pairs={{0,2},{2,0},{1,3},{3,1},{4,6},{6,4},{5,7},{7,5},{8,10},{10,8},{9,1... | collective-permute-start | bytes 983048 | tf_op jit(solution)/shard_map/ppermute | solution.py:442
  10.9 22.9 %collective-permute-start.1 = (f32[6,4,8,640]{3,2,1,0:T(8,128)}, f32[6,4,8,640]{3,2,1,0:T(8,128)S(1)}, u32[]{:S(2)}, u32[]{:S(2)}) collective-permute-start(f32[6,4,8,640]{3,2,1,0:T(8,128)} %get-tuple-element.21), channel_id=1, source_target_pairs={{4,8},{8,4},{5,9},{9,5},{6,10},{10,6},{7,11},{11,7},{20,24},{24,20... | collective-permute-start | bytes 1474568 | tf_op jit(solution)/shard_map/ppermute | solution.py:445
  23.0 11.4 %collective-permute-start.3 = (f32[3,6,8,640]{3,2,1,0:T(8,128)S(1)}, f32[3,6,8,640]{3,2,1,0:T(8,128)S(1)}, u32[]{:S(2)}, u32[]{:S(2)}) collective-permute-start(f32[3,6,8,640]{3,2,1,0:T(8,128)S(1)} %get-tuple-element.24), channel_id=1, source_target_pairs={{0,4},{8,12},{4,0},{12,8},{1,5},{9,13},{5,1},{13,9},{2,6},{10,14},... | collective-permute-start | bytes 1105928 | tf_op jit(solution)/shard_map/ppermute | solution.py:445
  26.5 11.3 %collective-permute-start.4 = (f32[3,6,8,640]{3,2,1,0:T(8,128)S(1)}, f32[3,6,8,640]{3,2,1,0:T(8,128)S(1)}, u32[]{:S(2)}, u32[]{:S(2)}) collective-permute-start(f32[3,6,8,640]{3,2,1,0:T(8,128)S(1)} %get-tuple-element.25), channel_id=1, source_target_pairs={{4,8},{8,4},{5,9},{9,5},{6,10},{10,6},{7,11},{11,7},{20,24},{24,20... | collective-permute-start | bytes 1105928 | tf_op jit(solution)/shard_map/ppermute | solution.py:445
  29.8 20.7 %collective-permute-start.6 = (f32[2,6,8,640]{3,2,1,0:T(8,128)S(1)}, f32[2,6,8,640]{3,2,1,0:T(8,128)S(1)}, u32[]{:S(2)}, u32[]{:S(2)}) collective-permute-start(f32[2,6,8,640]{3,2,1,0:T(8,128)S(1)} %get-tuple-element.31), channel_id=1, source_target_pairs={{0,4},{8,12},{4,0},{12,8},{1,5},{9,13},{5,1},{13,9},{2,6},{10,14},... | collective-permute-start | bytes 737288 | tf_op jit(solution)/shard_map/ppermute | solution.py:445
  31.9 18.6 %collective-permute-start.7 = (f32[2,6,8,640]{3,2,1,0:T(8,128)S(1)}, f32[2,6,8,640]{3,2,1,0:T(8,128)S(1)}, u32[]{:S(2)}, u32[]{:S(2)}) collective-permute-start(f32[2,6,8,640]{3,2,1,0:T(8,128)S(1)} %get-tuple-element.32), channel_id=1, source_target_pairs={{4,8},{8,4},{5,9},{9,5},{6,10},{10,6},{7,11},{11,7},{20,24},{24,20... | collective-permute-start | bytes 737288 | tf_op jit(solution)/shard_map/ppermute | solution.py:445

commit v3 on v2

--- a/solution.py
+++ b/solution.py
@@ -14,7 +14,7 @@
 LANES = 128
 RATES = 4
 CHUNKS = (3, 2)
-ROWS_AT_ONCE = 2
+ROWS_AT_ONCE = 9
 PARAMS = pltpu.CompilerParams(vmem_limit_bytes=12 * 2**20)
 VMEM = pl.BlockSpec(memory_space=pltpu.VMEM)
 HBM = pl.BlockSpec(memory_space=pltpu.HBM)
@@ -279,7 +279,7 @@
     return power
 
 
-def face_kernel(sector, coupling, rate_own, rate_first, rate_second, own, first, second, level, moved, power_out):
+def face_kernel(sector, coupling, rate_own, rate_first, rate_second, own, first, second, level, power_out):
     power = coupling_power(coupling)
     for g, entries in enumerate(power):
         for f, value in enumerate(entries):
@@ -320,28 +320,14 @@
     def _():
         halos(rate_first, rate_second, first, second)
 
-    def combine(step, carry):
-        r = extent - 2 - step
-
-        def tiles_of(index, q):
-            return [level[index, q, :, t * LANES:(t + 1) * LANES] for t in range(tiles)]
-
-        north, south, east, behind = tiles_of(r, 0), tiles_of(r - 1, 1), tiles_of(r, 2), tiles_of(r, 3)
-        west = shifted(behind, 1)
-        north_moved, south_moved, east_moved = shifted(north, -1), shifted(south, -1), shifted(east, -1)
+    for r in range(extent - 2, 0, -1):
+        west = shifted([level[r, 3, :, t * LANES:(t + 1) * LANES] for t in range(tiles)], 1)
         for t in range(tiles):
             span = slice(t * LANES, (t + 1) * LANES)
-            level[r, 1, :, span] = south[t]
+            north, south, east = level[r, 0, :, span], level[r - 1, 1, :, span], level[r, 2, :, span]
+            level[r, 1, :, span] = south
             level[r, 3, :, span] = west[t]
-            level[r, 4, :, span] = 1.0 - east[t] - west[t] - north[t] - south[t]
-            moved[r, 0, :, span] = north_moved[t]
-            moved[r, 1, :, span] = south_moved[t]
-            moved[r, 2, :, span] = east_moved[t]
-            moved[r, 3, :, span] = behind[t]
-            moved[r, 4, :, span] = 1.0 - east_moved[t] - behind[t] - north_moved[t] - south_moved[t]
-        return carry
-
-    lax.fori_loop(0, extent - 2, combine, 0)
+            level[r, 4, :, span] = 1.0 - east - west[t] - north - south
 
 
 def shifted(tiles, step):
@@ -352,7 +338,7 @@
     return [jnp.where(border, rolled[(t - step) % count], rolled[t]) for t in range(count)]
 
 
-def transport_kernel(chunk, finished, sector, power_ref, level, moved, own_ref, first_ref, second_ref, *refs):
+def transport_kernel(chunk, finished, sector, power_ref, rates, own_ref, first_ref, second_ref, *refs):
     earlier = refs[:finished]
     out_ref, even, odd = refs[finished:]
     rows, levels, width = own_ref.shape[1:]
@@ -375,36 +361,34 @@
         return [source[field, r, :, t * LANES:(t + 1) * LANES] for t in range(tiles)]
 
     for step in range(SUBSTEPS):
-        forward = step % 2 == 0
-        source, target, rates, way = (even, odd, moved, -1) if forward else (odd, even, level, 1)
-
-        def move(r, field, below, here, above, twice):
+        source, target = (even, odd) if step % 2 == 0 else (odd, even)
+        count = extent - 2 - 2 * step
+
+        def finish(field, r, here, ahead, behind):
             for t in range(tiles):
                 span = slice(t * LANES, (t + 1) * LANES)
                 north, south, east, west, stay = (rates[r, q, :, span] for q in range(5))
-                plain = source[field, r, :, span]
-                ahead, behind = (twice[t], plain) if forward else (plain, twice[t])
                 target[field, r, :, span] = (
-                    (stay * here[t] + (north * above[t] + south * below[t]))
-                    + (east * ahead + west * behind)
+                    (stay * here[t] + (north * source[field, r + 1, :, span] + south * source[field, r - 1, :, span]))
+                    + (east * ahead[t] + west * behind[t])
                 )
 
+        def work(first, number, field):
+            for r in [first + j for j in range(number)]:
+                here = line(source, r, field)
+                finish(field, r, here, shifted(here, -1), shifted(here, 1))
+
         for field in range(chunk):
-            def turn(r):
-                return shifted(line(source, r, field), way)
-
-            def some_rows(index, carry):
-                r = step + 1 + ROWS_AT_ONCE * index
-                below, here = carry[:tiles], carry[tiles:]
-                for j in range(ROWS_AT_ONCE):
-                    above = turn(r + j + 1)
-                    move(r + j, field, below, here, above, shifted(here, way))
-                    below, here = here, above
-                return tuple(below) + tuple(here)
-
-            count = extent - 2 - 2 * step
-            start = tuple(turn(step)) + tuple(turn(step + 1))
-            lax.fori_loop(0, count // ROWS_AT_ONCE, some_rows, start, unroll=2)
+            def group(index, carry):
+                work(step + 1 + ROWS_AT_ONCE * index, ROWS_AT_ONCE, field)
+                return carry
+
+            groups, rest = count // ROWS_AT_ONCE, count % ROWS_AT_ONCE
+            if groups > 1:
+                lax.fori_loop(0, groups, group, 0)
+            else:
+                work(step + 1, groups * ROWS_AT_ONCE, field)
+            work(step + 1 + groups * ROWS_AT_ONCE, rest, field)
     result = even if SUBSTEPS % 2 == 0 else odd
 
     if not last:
@@ -463,7 +447,10 @@
         ],
         compiler_params=PARAMS,
         name="pack",
-    )(adjoint_in, lat_ahead, lat_behind, lon_ahead, lon_behind)
+    )(*(
+        pltpu.with_memory_space_constraint(array, pltpu.HBM)
+        for array in (adjoint_in, lat_ahead, lat_behind, lon_ahead, lon_behind)
+    ))
     circles = [[part] + [sector_ahead(part, k) for k in range(1, sectors)] for part in payloads]
     rate_first, rate_second = to_bands(rate_first, rate_second)
 
@@ -491,15 +478,14 @@
         )(limits, table, *circle)
         first, second = to_bands(first, second)
         if c == 0:
-            level, moved, power = pl.pallas_call(
+            level, power = pl.pallas_call(
                 functools.partial(face_kernel, sector),
                 out_shape=(
-                    jax.ShapeDtypeStruct((extent, 5, levels, width), f32),
                     jax.ShapeDtypeStruct((extent, 5, levels, width), f32),
                     jax.ShapeDtypeStruct((fields, fields, levels, LANES), f32),
                 ),
                 in_specs=[VMEM] * 7,
-                out_specs=(VMEM,) * 3,
+                out_specs=(VMEM,) * 2,
                 compiler_params=PARAMS,
                 name="faces",
             )(jnp.transpose(coupling, (1, 0, 2)), rate_own, rate_first, rate_second, own, first, second)
@@ -509,7 +495,7 @@
         results.append(pl.pallas_call(
             functools.partial(transport_kernel, n, len(earlier), sector),
             out_shape=jax.ShapeDtypeStruct(shape, f32),
-            in_specs=[VMEM] * (6 + len(earlier)),
+            in_specs=[VMEM] * (5 + len(earlier)),
             out_specs=VMEM,
             scratch_shapes=[
                 pltpu.VMEM((n, extent, levels, width), f32),
@@ -517,7 +503,7 @@
             ],
             compiler_params=PARAMS,
             name="transport",
-        )(power, level, moved, own, first, second, *earlier))
+        )(power, level, own, first, second, *earlier))
     return results[-1]
 
 

time: 59.2 us -> 41.1 us (0.69)
  Pallas kernels: 26.2 us -> 13.1 us
  local copies, waits for them, and re-layouts: 4.98 us -> 0.08 us
    pallas_call x2, Pallas kernels: 19.1 us -> 7.02 us  [shards(): pl.pallas_call(functools.partial(transport_kernel, n, len(earlier), secto...]
    unnamed x14 -> x4, local copies, waits for them, and re-layouts: 4.91 us -> 0.01 us
    pallas_call x1, Pallas kernels: 2.02 us -> 0.53 us  [shards(): pl.pallas_call(functools.partial(face_kernel, sector), out_shape=(jax.Sha...]
  transfers between devices with their start and end apart: 8 -> 8, of which waited for: 3 -> 3; matrix products, arithmetic and copies ran while one was open for 1% -> 2% of each run, Pallas kernels for 26% -> 17%
where the time goes in v3:
time: 41.1 us; the launch traced here: 40.9 us
  starting transfers between devices  15 us (36%)
  Pallas kernels  13.1 us (32%)
  waiting for transfers between devices  11.8 us (29%)
  other arithmetic  0.73 us (2%)
    ppermute x2, waiting for transfers between devices, sector_ahead(): lax.ppermute(values, 'lon', [(s, (s - offset) % sectors) for s in range(s...  7.94 us
    ppermute x3, starting transfers between devices, to_bands(): lax.ppermute(first, 'lat', even_pairs)  7.16 us
    pallas_call x2, Pallas kernels, shards(): pl.pallas_call(functools.partial(transport_kernel, n, len(earlier), secto...  7.02 us
    ppermute x3, starting transfers between devices, to_bands(): lax.ppermute(second, 'lat', odd_pairs)  5.73 us
    ppermute x3, waiting for transfers between devices, to_bands(): lax.ppermute(second, 'lat', odd_pairs)  3.34 us
    pallas_call x2, Pallas kernels, shards(): pl.pallas_call(functools.partial(filter_kernel, sectors, c == 0), out_sha...  2.79 us
    pallas_call x1, Pallas kernels, shards(): pl.pallas_call(functools.partial(pack_kernel, chunks), out_shape=(*(jax.S...  2.76 us
    ppermute x2, starting transfers between devices, sector_ahead(): lax.ppermute(values, 'lon', [(s, (s - offset) % sectors) for s in range(s...  2.09 us
  transfers between devices with their start and end apart: 8, of which 3 were waited for; matrix products, arithmetic and copies ran while one was open for 2% of the time, Pallas kernels for 17%

profile of v3, /device:TPU:16, one launch (start us, length us, event | category | flops | bytes accessed | tf_op | source)
XLA Modules:
  0.0 40.9 jit_solution(8295816739925182065)
XLA Ops:
  0.0 0.0 copy-start
  0.0 2.8 %pack.1 = (f32[3,8,8,640]{3,2,1,0:T(8,128)S(1)}, f32[2,8,8,640]{3,2,1,0:T(8,128)}, f32[8,4,8,640]{3,2,1,0:T(8,128)S(1)}, f32[6,4,8,640]{3,2,1,0:T(8,128)}, f32[6,4,8,640]{3,2,1,0:T(8,128)}) custom-call(f32[5,8,8,576]{3,2,1,0:T(8,128)} %adjoint.1, f32[8,8,576]{2,1,0:T(8,128)} %refs_0_.1, f32[8,8,576]{2,1,0:T(8,128)} %refs_1_.1, f32[8,8,576]{2,1,0:T(8,128)} %refs_2_.1, ...), custom_call_target="tpu_custom_call" | custom-call | tf_op jit(solution)/shard_map/pack/pallas_call | solution.py:433
  2.8 0.0 copy-start.1
  2.8 1.6 %collective-permute-start.2 = (f32[3,8,8,640]{3,2,1,0:T(8,128)S(1)}, f32[3,8,8,640]{3,2,1,0:T(8,128)}, u32[]{:S(2)}, u32[]{:S(2)}) collective-permute-start(f32[3,8,8,640]{3,2,1,0:T(8,128)S(1)} %get-tuple-element.21.refs_0_), channel_id=1, source_target_pairs={{0,2},{2,0},{1,3},{3,1},{4,6},{6,4},{5,7},{7,5},{8,10},{10,8},{9,1... | collective-permute-start | bytes 1474568 | tf_op jit(solution)/shard_map/ppermute | solution.py:426
  4.3 1.6 %collective-permute-start = (f32[6,4,8,640]{3,2,1,0:T(8,128)}, f32[6,4,8,640]{3,2,1,0:T(8,128)S(1)}, u32[]{:S(2)}, u32[]{:S(2)}) collective-permute-start(f32[6,4,8,640]{3,2,1,0:T(8,128)} %get-tuple-element.19), channel_id=1, source_target_pairs={{0,4},{8,12},{4,0},{12,8},{1,5},{9,13},{5,1},{13,9},{2,6},{10,14},... | collective-permute-start | bytes 1474568 | tf_op jit(solution)/shard_map/ppermute | solution.py:429
  5.9 0.5 %collective-permute-start.5 = (f32[2,8,8,640]{3,2,1,0:T(8,128)}, f32[2,8,8,640]{3,2,1,0:T(8,128)}, u32[]{:S(2)}, u32[]{:S(2)}) collective-permute-start(f32[2,8,8,640]{3,2,1,0:T(8,128)} %get-tuple-element.27.refs_0_), channel_id=1, source_target_pairs={{0,2},{2,0},{1,3},{3,1},{4,6},{6,4},{5,7},{7,5},{8,10},{10,8},{9,1... | collective-permute-start | bytes 983048 | tf_op jit(solution)/shard_map/ppermute | solution.py:426
  6.5 1.9 %collective-permute-start.1 = (f32[6,4,8,640]{3,2,1,0:T(8,128)}, f32[6,4,8,640]{3,2,1,0:T(8,128)S(1)}, u32[]{:S(2)}, u32[]{:S(2)}) collective-permute-start(f32[6,4,8,640]{3,2,1,0:T(8,128)} %get-tuple-element.20), channel_id=1, source_target_pairs={{4,8},{8,4},{5,9},{9,5},{6,10},{10,6},{7,11},{11,7},{20,24},{24,20... | collective-permute-start | bytes 1474568 | tf_op jit(solution)/shard_map/ppermute | solution.py:429
  8.4 0.7 %dynamic-slice_convert_fusion = f32[8]{0:T(128)S(1)} fusion(s32[32]{0:T(128)} %param.14, s32[]{:T(128)S(6)} %select_n.3), kind=kLoop, calls=%fused_computation | loop fusion | flops 8 | bytes 68 | tf_op jit(solution)/shard_map/convert_element_type | solution.py:182
  9.1 7.9 %collective-permute-done.2.refs_1_ = f32[3,8,8,640]{3,2,1,0:T(8,128)} collective-permute-done((f32[3,8,8,640]{3,2,1,0:T(8,128)S(1)}, f32[3,8,8,640]{3,2,1,0:T(8,128)}, u32[]{:S(2)}, u32[]{:S(2)}) %collective-permute-start.2) | collective-permute-done | bytes 491552 | tf_op jit(solution)/shard_map/ppermute | solution.py:426
  17.0 0.1 broadcast_in_dim.2.limit_ref
  17.1 0.0 copy-done
  17.1 1.4 %polar_filter.2 = (f32[3,8,8,640]{3,2,1,0:T(8,128)S(1)}, f32[3,6,8,640]{3,2,1,0:T(8,128)S(1)}, f32[3,6,8,640]{3,2,1,0:T(8,128)S(1)}) custom-call(f32[8,128]{1,0:T(8,128)S(1)} %broadcast_in_dim.2.limit_ref, bf16[9,256,256]{2,1,0:T(8,128)(2,1)S(1)} %copy-done, f32[3,8,8,640]{3,2,1,0:T(8,128)S(1)} %get-tuple-element.21.refs_0_, ...), custom_call_target="tpu_custom_call" | custom-call | tf_op jit(solution)/shard_map/polar_filter/pallas_call | solution.py:462
  18.5 3.4 %collective-permute-start.3 = (f32[3,6,8,640]{3,2,1,0:T(8,128)S(1)}, f32[3,6,8,640]{3,2,1,0:T(8,128)S(1)}, u32[]{:S(2)}, u32[]{:S(2)}) collective-permute-start(f32[3,6,8,640]{3,2,1,0:T(8,128)S(1)} %get-tuple-element.23), channel_id=1, source_target_pairs={{0,4},{8,12},{4,0},{12,8},{1,5},{9,13},{5,1},{13,9},{2,6},{10,14},... | collective-permute-start | bytes 1105928 | tf_op jit(solution)/shard_map/ppermute | solution.py:429
  22.0 1.9 %collective-permute-start.4 = (f32[3,6,8,640]{3,2,1,0:T(8,128)S(1)}, f32[3,6,8,640]{3,2,1,0:T(8,128)S(1)}, u32[]{:S(2)}, u32[]{:S(2)}) collective-permute-start(f32[3,6,8,640]{3,2,1,0:T(8,128)S(1)} %get-tuple-element.24), channel_id=1, source_target_pairs={{4,8},{8,4},{5,9},{9,5},{6,10},{10,6},{7,11},{11,7},{20,24},{24,20... | collective-permute-start | bytes 1105928 | tf_op jit(solution)/shard_map/ppermute | solution.py:429
  23.9 0.0 collective-permute-done.5.refs_1_
  23.9 1.4 %polar_filter.3 = (f32[2,8,8,640]{3,2,1,0:T(8,128)S(1)}, f32[2,6,8,640]{3,2,1,0:T(8,128)S(1)}, f32[2,6,8,640]{3,2,1,0:T(8,128)S(1)}) custom-call(f32[8,128]{1,0:T(8,128)S(1)} %broadcast_in_dim.2.limit_ref, bf16[9,256,256]{2,1,0:T(8,128)(2,1)S(1)} %copy-done, f32[2,8,8,640]{3,2,1,0:T(8,128)} %get-tuple-element.27.refs_0_, ...), custom_call_target="tpu_custom_call" | custom-call | tf_op jit(solution)/shard_map/polar_filter/pallas_call | solution.py:462
  25.3 2.1 %collective-permute-start.6 = (f32[2,6,8,640]{3,2,1,0:T(8,128)S(1)}, f32[2,6,8,640]{3,2,1,0:T(8,128)S(1)}, u32[]{:S(2)}, u32[]{:S(2)}) collective-permute-start(f32[2,6,8,640]{3,2,1,0:T(8,128)S(1)} %get-tuple-element.29), channel_id=1, source_target_pairs={{0,4},{8,12},{4,0},{12,8},{1,5},{9,13},{5,1},{13,9},{2,6},{10,14},... | collective-permute-start | bytes 737288 | tf_op jit(solution)/shard_map/ppermute | solution.py:429
  27.4 0.0 collective-permute-done.rate_first
  27.4 1.9 %collective-permute-start.7 = (f32[2,6,8,640]{3,2,1,0:T(8,128)S(1)}, f32[2,6,8,640]{3,2,1,0:T(8,128)S(1)}, u32[]{:S(2)}, u32[]{:S(2)}) collective-permute-start(f32[2,6,8,640]{3,2,1,0:T(8,128)S(1)} %get-tuple-element.30), channel_id=1, source_target_pairs={{4,8},{8,4},{5,9},{9,5},{6,10},{10,6},{7,11},{11,7},{20,24},{24,20... | collective-permute-start | bytes 737288 | tf_op jit(solution)/shard_map/ppermute | solution.py:429
  29.4 0.0 collective-permute-done.1.rate_second
  29.4 0.6 %collective-permute-done.3.first.first_ref = f32[3,6,8,640]{3,2,1,0:T(8,128)S(1)} collective-permute-done((f32[3,6,8,640]{3,2,1,0:T(8,128)S(1)}, f32[3,6,8,640]{3,2,1,0:T(8,128)S(1)}, u32[]{:S(2)}, u32[]{:S(2)}) %collective-permute-start.3) | collective-permute-done | bytes 368672 | tf_op jit(solution)/shard_map/ppermute | solution.py:429
  29.9 3.3 %collective-permute-done.4.second.second_ref = f32[3,6,8,640]{3,2,1,0:T(8,128)S(1)} collective-permute-done((f32[3,6,8,640]{3,2,1,0:T(8,128)S(1)}, f32[3,6,8,640]{3,2,1,0:T(8,128)S(1)}, u32[]{:S(2)}, u32[]{:S(2)}) %collective-permute-start.4) | collective-permute-done | bytes 368672 | tf_op jit(solution)/shard_map/ppermute | solution.py:429
  33.3 0.0 copy-done.1
  33.3 0.5 %faces.1 = (f32[20,5,8,640]{3,2,1,0:T(8,128)S(1)}, f32[5,5,8,128]{3,2,1,0:T(8,128)S(1)}) custom-call(f32[5,8,5]{2,1,0:T(8,128)S(1)} %bitcast.1, f32[8,4,8,640]{3,2,1,0:T(8,128)S(1)} %get-tuple-element.18.rate_own, f32[6,4,8,640]{3,2,1,0:T(8,128)S(1)} %collective-permute-done.rate_first, f32[6,4,8,640]{3,2,1,0:T(8,128)S(1)} %collective-permute-done.1.rate_second, ...), custom_call_target="tpu_custom_call" | custom-call | tf_op jit(solution)/shard_map/faces/pallas_call | solution.py:481
  33.8 3.4 %transport.2.refs_0_ = f32[3,8,8,640]{3,2,1,0:T(8,128)S(1)} custom-call(f32[5,5,8,128]{3,2,1,0:T(8,128)S(1)} %get-tuple-element.25.power_ref, f32[20,5,8,640]{3,2,1,0:T(8,128)S(1)} %get-tuple-element.26.rates, f32[3,8,8,640]{3,2,1,0:T(8,128)S(1)} %get-tuple-element.22.own.own_ref, f32[3,6,8,640]{3,2,1,0:T(8,128)S(1)} %collective-permute-done.3.first.first_ref, ...), custom_call_target="tpu_custom_call" | custom-call | tf_op jit(solution)/shard_map/transport/pallas_call | solution.py:495
  37.2 0.0 collective-permute-done.6.first_ref
  37.3 0.0 collective-permute-done.7.second_ref
  37.3 3.6 %transport.3 = f32[5,8,8,576]{3,2,1,0:T(8,128)} custom-call(f32[5,5,8,128]{3,2,1,0:T(8,128)S(1)} %get-tuple-element.25.power_ref, f32[20,5,8,640]{3,2,1,0:T(8,128)S(1)} %get-tuple-element.26.rates, f32[2,8,8,640]{3,2,1,0:T(8,128)S(1)} %get-tuple-element.28.own_ref, f32[2,6,8,640]{3,2,1,0:T(8,128)S(1)} %collective-permute-done.6.first_ref, ...), custom_call_target="tpu_custom_call" | custom-call | tf_op jit(solution)/shard_map/transport/pallas_call | solution.py:495
Async XLA Ops:
  0.0 17.1 %copy-start = (bf16[9,256,256]{2,1,0:T(8,128)(2,1)S(1)}, bf16[9,256,256]{2,1,0:T(8,128)(2,1)}, u32[]{:S(2)}) copy-start(bf16[9,256,256]{2,1,0:T(8,128)(2,1)} %constant.13.clone.table) | copy-start | bytes 3538948
  2.8 30.5 %copy-start.1 = (f32[8,5,5]{2,0,1:T(8,128)S(1)}, f32[8,5,5]{2,0,1:T(8,128)}, u32[]{:S(2)}) copy-start(f32[8,5,5]{2,0,1:T(8,128)} %param.13) | copy-start | bytes 2404
  2.8 14.3 %collective-permute-start.2 = (f32[3,8,8,640]{3,2,1,0:T(8,128)S(1)}, f32[3,8,8,640]{3,2,1,0:T(8,128)}, u32[]{:S(2)}, u32[]{:S(2)}) collective-permute-start(f32[3,8,8,640]{3,2,1,0:T(8,128)S(1)} %get-tuple-element.21.refs_0_), channel_id=1, source_target_pairs={{0,2},{2,0},{1,3},{3,1},{4,6},{6,4},{5,7},{7,5},{8,10},{10,8},{9,1... | collective-permute-start | bytes 1474568 | tf_op jit(solution)/shard_map/ppermute | solution.py:426
  4.3 23.1 %collective-permute-start = (f32[6,4,8,640]{3,2,1,0:T(8,128)}, f32[6,4,8,640]{3,2,1,0:T(8,128)S(1)}, u32[]{:S(2)}, u32[]{:S(2)}) collective-permute-start(f32[6,4,8,640]{3,2,1,0:T(8,128)} %get-tuple-element.19), channel_id=1, source_target_pairs={{0,4},{8,12},{4,0},{12,8},{1,5},{9,13},{5,1},{13,9},{2,6},{10,14},... | collective-permute-start | bytes 1474568 | tf_op jit(solution)/shard_map/ppermute | solution.py:429
  5.9 18.0 %collective-permute-start.5 = (f32[2,8,8,640]{3,2,1,0:T(8,128)}, f32[2,8,8,640]{3,2,1,0:T(8,128)}, u32[]{:S(2)}, u32[]{:S(2)}) collective-permute-start(f32[2,8,8,640]{3,2,1,0:T(8,128)} %get-tuple-element.27.refs_0_), channel_id=1, source_target_pairs={{0,2},{2,0},{1,3},{3,1},{4,6},{6,4},{5,7},{7,5},{8,10},{10,8},{9,1... | collective-permute-start | bytes 983048 | tf_op jit(solution)/shard_map/ppermute | solution.py:426
  6.5 22.9 %collective-permute-start.1 = (f32[6,4,8,640]{3,2,1,0:T(8,128)}, f32[6,4,8,640]{3,2,1,0:T(8,128)S(1)}, u32[]{:S(2)}, u32[]{:S(2)}) collective-permute-start(f32[6,4,8,640]{3,2,1,0:T(8,128)} %get-tuple-element.20), channel_id=1, source_target_pairs={{4,8},{8,4},{5,9},{9,5},{6,10},{10,6},{7,11},{11,7},{20,24},{24,20... | collective-permute-start | bytes 1474568 | tf_op jit(solution)/shard_map/ppermute | solution.py:429
  18.5 11.4 %collective-permute-start.3 = (f32[3,6,8,640]{3,2,1,0:T(8,128)S(1)}, f32[3,6,8,640]{3,2,1,0:T(8,128)S(1)}, u32[]{:S(2)}, u32[]{:S(2)}) collective-permute-start(f32[3,6,8,640]{3,2,1,0:T(8,128)S(1)} %get-tuple-element.23), channel_id=1, source_target_pairs={{0,4},{8,12},{4,0},{12,8},{1,5},{9,13},{5,1},{13,9},{2,6},{10,14},... | collective-permute-start | bytes 1105928 | tf_op jit(solution)/shard_map/ppermute | solution.py:429
  22.0 11.3 %collective-permute-start.4 = (f32[3,6,8,640]{3,2,1,0:T(8,128)S(1)}, f32[3,6,8,640]{3,2,1,0:T(8,128)S(1)}, u32[]{:S(2)}, u32[]{:S(2)}) collective-permute-start(f32[3,6,8,640]{3,2,1,0:T(8,128)S(1)} %get-tuple-element.24), channel_id=1, source_target_pairs={{4,8},{8,4},{5,9},{9,5},{6,10},{10,6},{7,11},{11,7},{20,24},{24,20... | collective-permute-start | bytes 1105928 | tf_op jit(solution)/shard_map/ppermute | solution.py:429
  25.3 12.0 %collective-permute-start.6 = (f32[2,6,8,640]{3,2,1,0:T(8,128)S(1)}, f32[2,6,8,640]{3,2,1,0:T(8,128)S(1)}, u32[]{:S(2)}, u32[]{:S(2)}) collective-permute-start(f32[2,6,8,640]{3,2,1,0:T(8,128)S(1)} %get-tuple-element.29), channel_id=1, source_target_pairs={{0,4},{8,12},{4,0},{12,8},{1,5},{9,13},{5,1},{13,9},{2,6},{10,14},... | collective-permute-start | bytes 737288 | tf_op jit(solution)/shard_map/ppermute | solution.py:429
  27.4 9.8 %collective-permute-start.7 = (f32[2,6,8,640]{3,2,1,0:T(8,128)S(1)}, f32[2,6,8,640]{3,2,1,0:T(8,128)S(1)}, u32[]{:S(2)}, u32[]{:S(2)}) collective-permute-start(f32[2,6,8,640]{3,2,1,0:T(8,128)S(1)} %get-tuple-element.30), channel_id=1, source_target_pairs={{4,8},{8,4},{5,9},{9,5},{6,10},{10,6},{7,11},{11,7},{20,24},{24,20... | collective-permute-start | bytes 737288 | tf_op jit(solution)/shard_map/ppermute | solution.py:429

commit v4 on v3

--- a/solution.py
+++ b/solution.py
@@ -72,25 +72,53 @@
     own_out, first_out, second_out = refs[sectors:sectors + 3]
     wide, real_wave, block_wave = refs[sectors + 3:]
     fields, levels, rows, width = circle_refs[0].shape
-    sector = wide.shape[1] // sectors
-    length = sector * sectors
-    ways = length // LANES
+    ways = wide.shape[0]
+    length = ways * LANES
+    sector = length // sectors
     pairs = (ways - 1) // 2
     tiles = width // LANES
     per_field = levels * rows
     lat = lax.axis_index("lat")
     limit = limit_ref[...]
 
-    for k in range(sectors):
-        wide[:, k * sector:(k + 1) * sector] = circle_refs[k][:, :, :, :sector].reshape(fields * per_field, sector)
+    lines = fields * per_field
+    line_lane = lax.broadcasted_iota(jnp.int32, (lines, LANES), 1)
+    rolled = {}
+
+    def part(k, t):
+        if (k, t) not in rolled:
+            tile = circle_refs[k][:, :, :, t * LANES:(t + 1) * LANES].reshape(lines, LANES)
+            offset = k * sector % LANES
+            rolled[k, t] = pltpu.roll(tile, offset, 1) if offset else tile
+        return rolled[k, t]
+
+    def assemble(a):
+        tile = None
+        for k in range(sectors):
+            low, high = k * sector, (k + 1) * sector
+            if high <= a * LANES or low >= (a + 1) * LANES:
+                continue
+            t, offset = a - low // LANES, low % LANES
+            here = part(k, t) if t * LANES < sector else part(k, t - 1)
+            if offset and t > 0 and t * LANES < sector:
+                here = jnp.where(line_lane < offset, part(k, t - 1), here)
+            tile = here if tile is None else jnp.where(line_lane < low - a * LANES, tile, here)
+        wide[a] = tile
+
+    for a in range(ways):
+        if a < tiles or a == ways - 1:
+            assemble(a)
 
     @pl.when(jnp.min(limit) < length // 2)
     def _():
+        rolled.clear()
+        for a in range(tiles, ways - 1):
+            assemble(a)
         lane = lax.broadcasted_iota(jnp.int32, (rows, LANES), 1)
 
         def forward(field, carry):
             span = pl.ds(pl.multiple_of(field * per_field, per_field), per_field)
-            tile = [wide[span, a * LANES:(a + 1) * LANES] for a in range(ways)]
+            tile = [wide[a, span, :] for a in range(ways)]
             even = [tile[a] + tile[ways - a] for a in range(1, pairs + 1)]
             odd = [tile[a] - tile[ways - a] for a in range(1, pairs + 1)]
             real_wave[span, :] = tile[0] + sum(even)
@@ -125,27 +153,28 @@
             base = real_wave[span, :] * (1.0 / ways)
             cosines = [block_wave[k, span, :LANES] for k in range(pairs)]
             sines = [block_wave[k, span, LANES:] for k in range(pairs)]
-            wide[span, :LANES] = base + (2.0 / ways) * sum(cosines)
+            wide[0, span, :] = base + (2.0 / ways) * sum(cosines)
             for a in range(1, pairs + 1):
                 turn = [2.0 * math.pi * (a * k % ways) / ways for k in range(1, pairs + 1)]
                 even = base + sum((2.0 / ways * math.cos(t)) * c for t, c in zip(turn, cosines))
                 odd = sum((2.0 / ways * math.sin(t)) * s for t, s in zip(turn, sines))
-                wide[span, a * LANES:(a + 1) * LANES] = even - odd
-                wide[span, (ways - a) * LANES:(ways - a + 1) * LANES] = even + odd
+                wide[a, span, :] = even - odd
+                if a == 1 or ways - a < tiles:
+                    wide[ways - a, span, :] = even + odd
             return carry
 
         lax.fori_loop(0, fields, backward, 0)
 
     def emit(field, carry):
-        span = pl.ds(pl.multiple_of(field * per_field, per_field), per_field)
-        lane = lax.broadcasted_iota(jnp.int32, (per_field, LANES), 1)
-        for a in range(tiles):
-            tile = wide[span, a * LANES:(a + 1) * LANES]
-            if a == tiles - 1:
-                behind = wide[span, (ways - 1) * LANES:]
-                tile = jnp.where(lane >= LANES - HALO, behind, tile)
-            turned = jnp.swapaxes(tile.reshape(levels, rows, LANES), 0, 1)
-            own_out[pl.ds(field, 1), :, :, a * LANES:(a + 1) * LANES] = turned[None]
+        lane = lax.broadcasted_iota(jnp.int32, (levels, LANES), 1)
+        for r in range(rows):
+            span = pl.ds(field * per_field + r, levels, stride=rows)
+            for a in range(tiles):
+                tile = wide[a, span, :]
+                if a == tiles - 1:
+                    behind = wide[ways - 1, span, :]
+                    tile = jnp.where(lane >= LANES - HALO, behind, tile)
+                own_out[field, r, :, a * LANES:(a + 1) * LANES] = tile
         return carry
 
     lax.fori_loop(0, fields, emit, 0)
@@ -183,29 +212,66 @@
     return jnp.broadcast_to(own[:, None], (rows, LANES))
 
 
-def pack_kernel(chunks, adjoint, *refs):
-    sources = (adjoint,) + refs[:RATES]
-    count = len(chunks)
+def write_state(state, payload, field, extra):
+    levels, rows, sector = state.shape[1:]
+    width = payload.shape[-1]
+    tail = sector - (width - LANES)
+    payload[field, :, :, :width - LANES] = state[field, :, :, :width - LANES]
+    end = jnp.concatenate([state[field, :, :, width - LANES:], extra[:, :, tail:]], axis=2)
+    payload[field, :, :, width - LANES:] = end
+
+
+def first_pack_kernel(adjoint, *refs):
+    sources, (payload, state, rates, sems) = refs[:RATES], refs[RATES:]
+    count, levels, rows, width = payload.shape
+    sector = state.shape[-1]
+    tail = sector - (width - LANES)
+    copies = [pltpu.make_async_copy(adjoint.at[:count], state, sems.at[RATES])]
+    for q, source in enumerate(sources):
+        copies.append(pltpu.make_async_copy(source, rates.at[q], sems.at[q]))
+    for copy in copies:
+        copy.start()
+    for copy in copies[1:]:
+        copy.wait()
+    lat = lax.axis_index("lat")
+    top = jnp.where(lat == lax.axis_size("lat") - 1, rows - 1, rows)
+    lane = lax.broadcasted_iota(jnp.int32, (levels, rows, LANES), 2)
+    row = lax.broadcasted_iota(jnp.int32, (levels, rows, LANES), 1)
+    edges = jnp.zeros((levels, rows, LANES), jnp.float32)
+    for q in range(RATES):
+        at = edge_lane(sector) + 2 * HALO * q
+        head = pltpu.roll(rates[q, :, :, :LANES], at, 2)
+        end = jnp.concatenate([rates[q, :, :, width - LANES:], jnp.zeros((levels, rows, LANES - tail), jnp.float32)], axis=2)
+        end = pltpu.roll(end, (at + HALO - (tail - HALO)) % LANES, 2)
+        if q == 0:
+            head, end = jnp.where(row < top, head, 0.0), jnp.where(row < top, end, 0.0)
+        edges = jnp.where((lane >= at) & (lane < at + HALO), head, edges)
+        edges = jnp.where((lane >= at + HALO) & (lane < at + 2 * HALO), end, edges)
+    copies[0].wait()
+    zero = jnp.zeros((levels, rows, LANES), jnp.float32)
+    for field in range(count):
+        write_state(state, payload, field, edges if field == 0 else zero)
+
+
+def rest_pack_kernel(chunks, adjoint, *refs):
+    sources = refs[:RATES]
+    count = len(chunks) - 1
     payloads = refs[RATES:RATES + count]
     own_out, first_out, second_out = refs[RATES + count:RATES + count + 3]
     state, rates, sems = refs[RATES + count + 3:]
-    levels, rows, sector = sources[1].shape
+    levels, rows, sector = sources[0].shape
     width = own_out.shape[-1]
-    final = slice(width - LANES, width)
-    tail = sector - (width - LANES)
-    copies = [pltpu.make_async_copy(src, rates.at[q], sems.at[q]) for q, src in enumerate(sources[1:])]
-    copies.append(pltpu.make_async_copy(adjoint, state, sems.at[RATES]))
+    copies = [pltpu.make_async_copy(src, rates.at[q], sems.at[q]) for q, src in enumerate(sources)]
+    if count:
+        copies.append(pltpu.make_async_copy(adjoint.at[chunks[0]:], state, sems.at[RATES]))
     for copy in copies:
         copy.start()
     for copy in copies[:RATES]:
         copy.wait()
     lat = lax.axis_index("lat")
     is_last = lat == lax.axis_size("lat") - 1
-    lane = lax.broadcasted_iota(jnp.int32, (levels, rows, LANES), 2)
     row = lax.broadcasted_iota(jnp.int32, (levels, rows, LANES), 1)
-    edges = jnp.zeros((levels, rows, LANES), jnp.float32)
     for q in range(RATES):
-        at = edge_lane(sector) + 2 * HALO * q
         for start in range(0, width, LANES):
             size = min(LANES, sector - start)
             tile = rates[q, :, :, start:start + size]
@@ -214,23 +280,14 @@
             if q == 0:
                 tile = jnp.where(jnp.logical_and(is_last, row == rows - 1), 0.0, tile)
             own_out[:, q, :, start:start + LANES] = jnp.swapaxes(tile, 0, 1)
-            if start == 0:
-                initial = pltpu.roll(tile, at, 2)
-                edges = jnp.where((lane >= at) & (lane < at + HALO), initial, edges)
-            if start == width - LANES:
-                last = pltpu.roll(tile, (at + HALO - (tail - HALO)) % LANES, 2)
-                edges = jnp.where((lane >= at + HALO) & (lane < at + 2 * HALO), last, edges)
-    copies[RATES].wait()
-    field = 0
+    if count:
+        copies[RATES].wait()
+    zero = jnp.zeros((levels, rows, LANES), jnp.float32)
+    at = 0
     for c in range(count):
-        for j in range(chunks[c]):
-            payloads[c][j, :, :, :width - LANES] = state[field, :, :, :width - LANES]
-            end = state[field, :, :, width - LANES:]
-            end = jnp.concatenate([end, jnp.zeros((levels, rows, LANES - tail), jnp.float32)], axis=2)
-            if field == 0:
-                end = jnp.where(lane < tail, end, edges)
-            payloads[c][j, :, :, final] = end
-            field += 1
+        for j in range(chunks[c + 1]):
+            write_state(state.at[at:at + 1], payloads[c].at[j:j + 1], 0, zero)
+            at += 1
     top = rows - HALO
     to_next = lax.rem(lat, 2) == 0
 
@@ -340,7 +397,7 @@
 
 def transport_kernel(chunk, finished, sector, power_ref, rates, own_ref, first_ref, second_ref, *refs):
     earlier = refs[:finished]
-    out_ref, even, odd = refs[finished:]
+    out_ref, even, odd, stage = refs[finished:]
     rows, levels, width = own_ref.shape[1:]
     extent = rows + 2 * HALO
     tiles = width // LANES
@@ -397,12 +454,19 @@
     sources = [(ref, j, 0) for ref in earlier for j in range(ref.shape[0])]
     sources += [(result, j, HALO) for j in range(chunk)]
     fields = len(sources)
-    for start in range(0, sector, LANES):
-        stop = min(start + LANES, sector)
-        values = [ref[j, base:base + rows, :, start:start + LANES] for ref, j, base in sources]
-        for f in range(fields):
-            total = functools.reduce(jnp.add, [power_ref[g, f][None] * values[g] for g in range(fields)])
-            out_ref[f, :, :, start:stop] = jnp.swapaxes(total, 0, 1)[:, :, :stop - start]
+    def mix(f, carry):
+        for start in range(0, sector, LANES):
+            stop = min(start + LANES, sector)
+            for r in range(rows):
+                terms = [power_ref[g, f] * ref[j, base + r, :, start:start + LANES]
+                         for g, (ref, j, base) in enumerate(sources)]
+                stage[start // LANES, r * levels:(r + 1) * levels] = functools.reduce(jnp.add, terms)
+            for level in range(levels):
+                value = stage[start // LANES, pl.ds(level, rows, stride=levels), :]
+                out_ref[f, level, :, start:stop] = value[:, :stop - start]
+        return carry
+
+    lax.fori_loop(0, fields, mix, 0)
 
 
 def lat_pairs(count):
@@ -430,28 +494,46 @@
 
     extent = rows + 2 * HALO
     rate_shape = (RATES, levels, width)
+    inputs = [
+        pltpu.with_memory_space_constraint(array, pltpu.HBM)
+        for array in (adjoint_in, lat_ahead, lat_behind, lon_ahead, lon_behind)
+    ]
+    payload_shapes = [jax.ShapeDtypeStruct((n, levels, rows, width), f32) for n in chunks]
+    later = max(fields - chunks[0], 1)
+    first_payload = pl.pallas_call(
+        first_pack_kernel,
+        out_shape=payload_shapes[0],
+        in_specs=[HBM] * (1 + RATES),
+        out_specs=VMEM,
+        scratch_shapes=[
+            pltpu.VMEM((chunks[0],) + adjoint_in.shape[1:], f32),
+            pltpu.VMEM((RATES,) + lat_ahead.shape, f32),
+            pltpu.SemaphoreType.DMA((1 + RATES,)),
+        ],
+        compiler_params=PARAMS,
+        name="first_pack",
+    )(*inputs)
+    first_circle = [first_payload] + [sector_ahead(first_payload, k) for k in range(1, sectors)]
     *payloads, rate_own, rate_first, rate_second = pl.pallas_call(
-        functools.partial(pack_kernel, chunks),
+        functools.partial(rest_pack_kernel, chunks),
         out_shape=(
-            *(jax.ShapeDtypeStruct((n, levels, rows, width), f32) for n in chunks),
+            *payload_shapes[1:],
             jax.ShapeDtypeStruct((rows,) + rate_shape, f32),
             jax.ShapeDtypeStruct((HALO,) + rate_shape, f32),
             jax.ShapeDtypeStruct((HALO,) + rate_shape, f32),
         ),
         in_specs=[HBM] * (1 + RATES),
-        out_specs=(VMEM,) * (len(chunks) + 3),
+        out_specs=(VMEM,) * (len(chunks) + 2),
         scratch_shapes=[
-            pltpu.VMEM(adjoint_in.shape, f32),
+            pltpu.VMEM((later,) + adjoint_in.shape[1:], f32),
             pltpu.VMEM((RATES,) + lat_ahead.shape, f32),
             pltpu.SemaphoreType.DMA((1 + RATES,)),
         ],
         compiler_params=PARAMS,
-        name="pack",
-    )(*(
-        pltpu.with_memory_space_constraint(array, pltpu.HBM)
-        for array in (adjoint_in, lat_ahead, lat_behind, lon_ahead, lon_behind)
-    ))
+        name="rest_pack",
+    )(*inputs)
     circles = [[part] + [sector_ahead(part, k) for k in range(1, sectors)] for part in payloads]
+    circles.insert(0, first_circle)
     rate_first, rate_second = to_bands(rate_first, rate_second)
 
     limits = limits_of(cutoff, rows)
@@ -469,7 +551,7 @@
             in_specs=[VMEM] * (sectors + 2),
             out_specs=(VMEM,) * 3,
             scratch_shapes=[
-                pltpu.VMEM((lines, length), f32),
+                pltpu.VMEM((length // LANES, lines, LANES), f32),
                 pltpu.VMEM((lines, LANES), f32),
                 pltpu.VMEM((table.shape[0] // 2, lines, 2 * LANES), f32),
             ],
@@ -500,6 +582,7 @@
             scratch_shapes=[
                 pltpu.VMEM((n, extent, levels, width), f32),
                 pltpu.VMEM((n, extent, levels, width), f32),
+                pltpu.VMEM((width // LANES, rows * levels, LANES), f32),
             ],
             compiler_params=PARAMS,
             name="transport",

time: 41.1 us -> 40.1 us (0.976)
  waiting for transfers between devices: 11.8 us -> 9.98 us
  Pallas kernels: 13.1 us -> 14.3 us
  other arithmetic: 0.73 us -> 0.08 us
    ppermute x2, waiting for transfers between devices: 7.94 us -> 6.02 us  [sector_ahead(): lax.ppermute(values, 'lon', [(s, (s - offset) % sectors) for s in range(s...]
    pallas_call x1 -> x2, Pallas kernels: 2.76 us -> 4.04 us  [the longest x1 2.48 us: shards(): pl.pallas_call(functools.partial(rest_pack_kernel, chunks), out_shape=(*p...]
    convert_element_type x1, other arithmetic: 0.73 us -> 0.08 us  [limits_of(): lax.dynamic_slice_in_dim(cutoff, lat * rows, rows, 0).astype(jnp.float32)]
  transfers between devices with their start and end apart: 8 -> 8, of which waited for: 3 -> 3; matrix products, arithmetic and copies ran while one was open for 2% -> 0% of each run, Pallas kernels for 17% -> 23%
where the time goes in v4:
time: 40.1 us; the launch traced here: 39.8 us
  starting transfers between devices  15.2 us (38%)
  Pallas kernels  14.3 us (36%)
  waiting for transfers between devices  9.98 us (25%)
    ppermute x3, starting transfers between devices, to_bands(): lax.ppermute(first, 'lat', even_pairs)  7.38 us
    pallas_call x2, Pallas kernels, shards(): pl.pallas_call(functools.partial(transport_kernel, n, len(earlier), secto...  7.03 us
    ppermute x2, waiting for transfers between devices, sector_ahead(): lax.ppermute(values, 'lon', [(s, (s - offset) % sectors) for s in range(s...  6.02 us
    ppermute x3, starting transfers between devices, to_bands(): lax.ppermute(second, 'lat', odd_pairs)  5.73 us
    ppermute x3, waiting for transfers between devices, to_bands(): lax.ppermute(second, 'lat', odd_pairs)  3.34 us
    pallas_call x2, Pallas kernels, shards(): pl.pallas_call(functools.partial(filter_kernel, sectors, c == 0), out_sha...  2.74 us
    pallas_call x1, Pallas kernels, shards(): pl.pallas_call(functools.partial(rest_pack_kernel, chunks), out_shape=(*p...  2.48 us
    ppermute x2, starting transfers between devices, sector_ahead(): lax.ppermute(values, 'lon', [(s, (s - offset) % sectors) for s in range(s...  2.09 us
  transfers between devices with their start and end apart: 8, of which 3 were waited for; matrix products, arithmetic and copies ran while one was open for 0% of the time, Pallas kernels for 23%

profile of v4, /device:TPU:16, one launch (start us, length us, event | category | flops | bytes accessed | tf_op | source)
XLA Modules:
  0.0 39.8 jit_solution(3754668925881097896)
XLA Ops:
  0.0 0.0 copy-start
  0.0 0.0 copy-start.2
  0.0 1.6 %first_pack.1.refs_0_ = f32[3,8,8,640]{3,2,1,0:T(8,128)S(1)} custom-call(f32[5,8,8,576]{3,2,1,0:T(8,128)} %adjoint.3, f32[8,8,576]{2,1,0:T(8,128)} %refs_0_.3, f32[8,8,576]{2,1,0:T(8,128)} %refs_1_.3, f32[8,8,576]{2,1,0:T(8,128)} %refs_2_.3, f32[8,8,576]{2,1,0:T(8,128)} %refs_3_.3), custom_call_target="tpu_custom_call" | custom-call | tf_op jit(solution)/shard_map/first_pack/pallas_call | solution.py:503
  1.6 1.6 %collective-permute-start.2 = (f32[3,8,8,640]{3,2,1,0:T(8,128)S(1)}, f32[3,8,8,640]{3,2,1,0:T(8,128)}, u32[]{:S(2)}, u32[]{:S(2)}) collective-permute-start(f32[3,8,8,640]{3,2,1,0:T(8,128)S(1)} %first_pack.1.refs_0_), channel_id=1, source_target_pairs={{0,2},{2,0},{1,3},{3,1},{4,6},{6,4},{5,7},{7,5},{8,10},{10,8},{9,1... | collective-permute-start | bytes 1474568 | tf_op jit(solution)/shard_map/ppermute | solution.py:490
  3.1 2.5 %rest_pack.1 = (f32[2,8,8,640]{3,2,1,0:T(8,128)}, f32[8,4,8,640]{3,2,1,0:T(8,128)S(1)}, f32[6,4,8,640]{3,2,1,0:T(8,128)}, f32[6,4,8,640]{3,2,1,0:T(8,128)}) custom-call(f32[5,8,8,576]{3,2,1,0:T(8,128)} %adjoint.3, f32[8,8,576]{2,1,0:T(8,128)} %refs_0_.3, f32[8,8,576]{2,1,0:T(8,128)} %refs_1_.3, f32[8,8,576]{2,1,0:T(8,128)} %refs_2_.3, f32[8,8,576]{2,1,0:T(8,128)} %refs_3_.3), custom_call_target="tpu_custom_call" | custom-call | tf_op jit(solution)/shard_map/rest_pack/pallas_call | solution.py:517
  5.6 0.0 copy-start.1
  5.6 1.6 %collective-permute-start = (f32[6,4,8,640]{3,2,1,0:T(8,128)}, f32[6,4,8,640]{3,2,1,0:T(8,128)S(1)}, u32[]{:S(2)}, u32[]{:S(2)}) collective-permute-start(f32[6,4,8,640]{3,2,1,0:T(8,128)} %get-tuple-element.18), channel_id=1, source_target_pairs={{0,4},{8,12},{4,0},{12,8},{1,5},{9,13},{5,1},{13,9},{2,6},{10,14},... | collective-permute-start | bytes 1474568 | tf_op jit(solution)/shard_map/ppermute | solution.py:493
  7.3 0.5 %collective-permute-start.5 = (f32[2,8,8,640]{3,2,1,0:T(8,128)}, f32[2,8,8,640]{3,2,1,0:T(8,128)}, u32[]{:S(2)}, u32[]{:S(2)}) collective-permute-start(f32[2,8,8,640]{3,2,1,0:T(8,128)} %get-tuple-element.25.refs_0_), channel_id=1, source_target_pairs={{0,2},{2,0},{1,3},{3,1},{4,6},{6,4},{5,7},{7,5},{8,10},{10,8},{9,1... | collective-permute-start | bytes 983048 | tf_op jit(solution)/shard_map/ppermute | solution.py:490
  7.8 1.9 %collective-permute-start.1 = (f32[6,4,8,640]{3,2,1,0:T(8,128)}, f32[6,4,8,640]{3,2,1,0:T(8,128)S(1)}, u32[]{:S(2)}, u32[]{:S(2)}) collective-permute-start(f32[6,4,8,640]{3,2,1,0:T(8,128)} %get-tuple-element.19), channel_id=1, source_target_pairs={{4,8},{8,4},{5,9},{9,5},{6,10},{10,6},{7,11},{11,7},{20,24},{24,20... | collective-permute-start | bytes 1474568 | tf_op jit(solution)/shard_map/ppermute | solution.py:493
  9.7 0.0 copy-done.2
  9.7 0.1 dynamic-slice_convert_fusion
  9.8 6.0 %collective-permute-done.2.refs_1_ = f32[3,8,8,640]{3,2,1,0:T(8,128)} collective-permute-done((f32[3,8,8,640]{3,2,1,0:T(8,128)S(1)}, f32[3,8,8,640]{3,2,1,0:T(8,128)}, u32[]{:S(2)}, u32[]{:S(2)}) %collective-permute-start.2) | collective-permute-done | bytes 491552 | tf_op jit(solution)/shard_map/ppermute | solution.py:490
  15.8 0.1 broadcast_in_dim.2.limit_ref
  15.9 0.0 copy-done
  15.9 1.4 %polar_filter.2 = (f32[3,8,8,640]{3,2,1,0:T(8,128)S(1)}, f32[3,6,8,640]{3,2,1,0:T(8,128)S(1)}, f32[3,6,8,640]{3,2,1,0:T(8,128)S(1)}) custom-call(f32[8,128]{1,0:T(8,128)S(1)} %broadcast_in_dim.2.limit_ref, bf16[9,256,256]{2,1,0:T(8,128)(2,1)S(1)} %copy-done, f32[3,8,8,640]{3,2,1,0:T(8,128)S(1)} %first_pack.1.refs_0_, ...), custom_call_target="tpu_custom_call" | custom-call | tf_op jit(solution)/shard_map/polar_filter/pallas_call | solution.py:544
  17.3 3.6 %collective-permute-start.3 = (f32[3,6,8,640]{3,2,1,0:T(8,128)S(1)}, f32[3,6,8,640]{3,2,1,0:T(8,128)S(1)}, u32[]{:S(2)}, u32[]{:S(2)}) collective-permute-start(f32[3,6,8,640]{3,2,1,0:T(8,128)S(1)} %get-tuple-element.21), channel_id=1, source_target_pairs={{0,4},{8,12},{4,0},{12,8},{1,5},{9,13},{5,1},{13,9},{2,6},{10,14},... | collective-permute-start | bytes 1105928 | tf_op jit(solution)/shard_map/ppermute | solution.py:493
  20.9 1.9 %collective-permute-start.4 = (f32[3,6,8,640]{3,2,1,0:T(8,128)S(1)}, f32[3,6,8,640]{3,2,1,0:T(8,128)S(1)}, u32[]{:S(2)}, u32[]{:S(2)}) collective-permute-start(f32[3,6,8,640]{3,2,1,0:T(8,128)S(1)} %get-tuple-element.22), channel_id=1, source_target_pairs={{4,8},{8,4},{5,9},{9,5},{6,10},{10,6},{7,11},{11,7},{20,24},{24,20... | collective-permute-start | bytes 1105928 | tf_op jit(solution)/shard_map/ppermute | solution.py:493
  22.8 0.0 collective-permute-done.5.refs_1_
  22.8 1.3 %polar_filter.3 = (f32[2,8,8,640]{3,2,1,0:T(8,128)S(1)}, f32[2,6,8,640]{3,2,1,0:T(8,128)S(1)}, f32[2,6,8,640]{3,2,1,0:T(8,128)S(1)}) custom-call(f32[8,128]{1,0:T(8,128)S(1)} %broadcast_in_dim.2.limit_ref, bf16[9,256,256]{2,1,0:T(8,128)(2,1)S(1)} %copy-done, f32[2,8,8,640]{3,2,1,0:T(8,128)} %get-tuple-element.25.refs_0_, ...), custom_call_target="tpu_custom_call" | custom-call | tf_op jit(solution)/shard_map/polar_filter/pallas_call | solution.py:544
  24.2 2.1 %collective-permute-start.6 = (f32[2,6,8,640]{3,2,1,0:T(8,128)S(1)}, f32[2,6,8,640]{3,2,1,0:T(8,128)S(1)}, u32[]{:S(2)}, u32[]{:S(2)}) collective-permute-start(f32[2,6,8,640]{3,2,1,0:T(8,128)S(1)} %get-tuple-element.27), channel_id=1, source_target_pairs={{0,4},{8,12},{4,0},{12,8},{1,5},{9,13},{5,1},{13,9},{2,6},{10,14},... | collective-permute-start | bytes 737288 | tf_op jit(solution)/shard_map/ppermute | solution.py:493
  26.3 0.0 collective-permute-done.rate_first
  26.3 1.9 %collective-permute-start.7 = (f32[2,6,8,640]{3,2,1,0:T(8,128)S(1)}, f32[2,6,8,640]{3,2,1,0:T(8,128)S(1)}, u32[]{:S(2)}, u32[]{:S(2)}) collective-permute-start(f32[2,6,8,640]{3,2,1,0:T(8,128)S(1)} %get-tuple-element.28), channel_id=1, source_target_pairs={{4,8},{8,4},{5,9},{9,5},{6,10},{10,6},{7,11},{11,7},{20,24},{24,20... | collective-permute-start | bytes 737288 | tf_op jit(solution)/shard_map/ppermute | solution.py:493
  28.2 0.0 collective-permute-done.1.rate_second
  28.3 0.6 %collective-permute-done.3.first.first_ref = f32[3,6,8,640]{3,2,1,0:T(8,128)S(1)} collective-permute-done((f32[3,6,8,640]{3,2,1,0:T(8,128)S(1)}, f32[3,6,8,640]{3,2,1,0:T(8,128)S(1)}, u32[]{:S(2)}, u32[]{:S(2)}) %collective-permute-start.3) | collective-permute-done | bytes 368672 | tf_op jit(solution)/shard_map/ppermute | solution.py:493
  28.9 3.3 %collective-permute-done.4.second.second_ref = f32[3,6,8,640]{3,2,1,0:T(8,128)S(1)} collective-permute-done((f32[3,6,8,640]{3,2,1,0:T(8,128)S(1)}, f32[3,6,8,640]{3,2,1,0:T(8,128)S(1)}, u32[]{:S(2)}, u32[]{:S(2)}) %collective-permute-start.4) | collective-permute-done | bytes 368672 | tf_op jit(solution)/shard_map/ppermute | solution.py:493
  32.2 0.0 copy-done.1
  32.2 0.5 %faces.1 = (f32[20,5,8,640]{3,2,1,0:T(8,128)S(1)}, f32[5,5,8,128]{3,2,1,0:T(8,128)S(1)}) custom-call(f32[5,8,5]{2,1,0:T(8,128)S(1)} %bitcast.1, f32[8,4,8,640]{3,2,1,0:T(8,128)S(1)} %get-tuple-element.17.rate_own, f32[6,4,8,640]{3,2,1,0:T(8,128)S(1)} %collective-permute-done.rate_first, f32[6,4,8,640]{3,2,1,0:T(8,128)S(1)} %collective-permute-done.1.rate_second, ...), custom_call_target="tpu_custom_call" | custom-call | tf_op jit(solution)/shard_map/faces/pallas_call | solution.py:563
  32.7 3.4 %transport.2.refs_0_ = f32[3,8,8,640]{3,2,1,0:T(8,128)S(1)} custom-call(f32[5,5,8,128]{3,2,1,0:T(8,128)S(1)} %get-tuple-element.23.power_ref, f32[20,5,8,640]{3,2,1,0:T(8,128)S(1)} %get-tuple-element.24.rates, f32[3,8,8,640]{3,2,1,0:T(8,128)S(1)} %get-tuple-element.20.own.own_ref, f32[3,6,8,640]{3,2,1,0:T(8,128)S(1)} %collective-permute-done.3.first.first_ref, ...), custom_call_target="tpu_custom_call" | custom-call | tf_op jit(solution)/shard_map/transport/pallas_call | solution.py:577
  36.2 0.0 collective-permute-done.6.first_ref
  36.2 0.0 collective-permute-done.7.second_ref
  36.2 3.6 %transport.3 = f32[5,8,8,576]{3,2,1,0:T(8,128)} custom-call(f32[5,5,8,128]{3,2,1,0:T(8,128)S(1)} %get-tuple-element.23.power_ref, f32[20,5,8,640]{3,2,1,0:T(8,128)S(1)} %get-tuple-element.24.rates, f32[2,8,8,640]{3,2,1,0:T(8,128)S(1)} %get-tuple-element.26.own_ref, f32[2,6,8,640]{3,2,1,0:T(8,128)S(1)} %collective-permute-done.6.first_ref, ...), custom_call_target="tpu_custom_call" | custom-call | tf_op jit(solution)/shard_map/transport/pallas_call | solution.py:577
Async XLA Ops:
  0.0 15.9 %copy-start = (bf16[9,256,256]{2,1,0:T(8,128)(2,1)S(1)}, bf16[9,256,256]{2,1,0:T(8,128)(2,1)}, u32[]{:S(2)}) copy-start(bf16[9,256,256]{2,1,0:T(8,128)(2,1)} %constant.13.clone.table) | copy-start | bytes 3538948
  0.0 9.7 %copy-start.2 = (s32[32]{0:T(128)S(1)}, s32[32]{0:T(128)}, u32[]{:S(2)}) copy-start(s32[32]{0:T(128)} %param.14) | copy-start | bytes 388
  1.6 14.3 %collective-permute-start.2 = (f32[3,8,8,640]{3,2,1,0:T(8,128)S(1)}, f32[3,8,8,640]{3,2,1,0:T(8,128)}, u32[]{:S(2)}, u32[]{:S(2)}) collective-permute-start(f32[3,8,8,640]{3,2,1,0:T(8,128)S(1)} %first_pack.1.refs_0_), channel_id=1, source_target_pairs={{0,2},{2,0},{1,3},{3,1},{4,6},{6,4},{5,7},{7,5},{8,10},{10,8},{9,1... | collective-permute-start | bytes 1474568 | tf_op jit(solution)/shard_map/ppermute | solution.py:490
  5.6 26.6 %copy-start.1 = (f32[8,5,5]{2,0,1:T(8,128)S(1)}, f32[8,5,5]{2,0,1:T(8,128)}, u32[]{:S(2)}) copy-start(f32[8,5,5]{2,0,1:T(8,128)} %param.13) | copy-start | bytes 2404
  5.6 20.7 %collective-permute-start = (f32[6,4,8,640]{3,2,1,0:T(8,128)}, f32[6,4,8,640]{3,2,1,0:T(8,128)S(1)}, u32[]{:S(2)}, u32[]{:S(2)}) collective-permute-start(f32[6,4,8,640]{3,2,1,0:T(8,128)} %get-tuple-element.18), channel_id=1, source_target_pairs={{0,4},{8,12},{4,0},{12,8},{1,5},{9,13},{5,1},{13,9},{2,6},{10,14},... | collective-permute-start | bytes 1474568 | tf_op jit(solution)/shard_map/ppermute | solution.py:493
  7.3 15.6 %collective-permute-start.5 = (f32[2,8,8,640]{3,2,1,0:T(8,128)}, f32[2,8,8,640]{3,2,1,0:T(8,128)}, u32[]{:S(2)}, u32[]{:S(2)}) collective-permute-start(f32[2,8,8,640]{3,2,1,0:T(8,128)} %get-tuple-element.25.refs_0_), channel_id=1, source_target_pairs={{0,2},{2,0},{1,3},{3,1},{4,6},{6,4},{5,7},{7,5},{8,10},{10,8},{9,1... | collective-permute-start | bytes 983048 | tf_op jit(solution)/shard_map/ppermute | solution.py:490
  7.8 20.4 %collective-permute-start.1 = (f32[6,4,8,640]{3,2,1,0:T(8,128)}, f32[6,4,8,640]{3,2,1,0:T(8,128)S(1)}, u32[]{:S(2)}, u32[]{:S(2)}) collective-permute-start(f32[6,4,8,640]{3,2,1,0:T(8,128)} %get-tuple-element.19), channel_id=1, source_target_pairs={{4,8},{8,4},{5,9},{9,5},{6,10},{10,6},{7,11},{11,7},{20,24},{24,20... | collective-permute-start | bytes 1474568 | tf_op jit(solution)/shard_map/ppermute | solution.py:493
  17.3 11.6 %collective-permute-start.3 = (f32[3,6,8,640]{3,2,1,0:T(8,128)S(1)}, f32[3,6,8,640]{3,2,1,0:T(8,128)S(1)}, u32[]{:S(2)}, u32[]{:S(2)}) collective-permute-start(f32[3,6,8,640]{3,2,1,0:T(8,128)S(1)} %get-tuple-element.21), channel_id=1, source_target_pairs={{0,4},{8,12},{4,0},{12,8},{1,5},{9,13},{5,1},{13,9},{2,6},{10,14},... | collective-permute-start | bytes 1105928 | tf_op jit(solution)/shard_map/ppermute | solution.py:493
  20.9 11.3 %collective-permute-start.4 = (f32[3,6,8,640]{3,2,1,0:T(8,128)S(1)}, f32[3,6,8,640]{3,2,1,0:T(8,128)S(1)}, u32[]{:S(2)}, u32[]{:S(2)}) collective-permute-start(f32[3,6,8,640]{3,2,1,0:T(8,128)S(1)} %get-tuple-element.22), channel_id=1, source_target_pairs={{4,8},{8,4},{5,9},{9,5},{6,10},{10,6},{7,11},{11,7},{20,24},{24,20... | collective-permute-start | bytes 1105928 | tf_op jit(solution)/shard_map/ppermute | solution.py:493
  24.2 12.0 %collective-permute-start.6 = (f32[2,6,8,640]{3,2,1,0:T(8,128)S(1)}, f32[2,6,8,640]{3,2,1,0:T(8,128)S(1)}, u32[]{:S(2)}, u32[]{:S(2)}) collective-permute-start(f32[2,6,8,640]{3,2,1,0:T(8,128)S(1)} %get-tuple-element.27), channel_id=1, source_target_pairs={{0,4},{8,12},{4,0},{12,8},{1,5},{9,13},{5,1},{13,9},{2,6},{10,14},... | collective-permute-start | bytes 737288 | tf_op jit(solution)/shard_map/ppermute | solution.py:493
  26.3 9.9 %collective-permute-start.7 = (f32[2,6,8,640]{3,2,1,0:T(8,128)S(1)}, f32[2,6,8,640]{3,2,1,0:T(8,128)S(1)}, u32[]{:S(2)}, u32[]{:S(2)}) collective-permute-start(f32[2,6,8,640]{3,2,1,0:T(8,128)S(1)} %get-tuple-element.28), channel_id=1, source_target_pairs={{4,8},{8,4},{5,9},{9,5},{6,10},{10,6},{7,11},{11,7},{20,24},{24,20... | collective-permute-start | bytes 737288 | tf_op jit(solution)/shard_map/ppermute | solution.py:493

commit v5 on v4

--- a/solution.py
+++ b/solution.py
@@ -70,7 +70,7 @@
 def filter_kernel(sectors, edges, limit_ref, table, *refs):
     circle_refs = refs[:sectors]
     own_out, first_out, second_out = refs[sectors:sectors + 3]
-    wide, real_wave, block_wave = refs[sectors + 3:]
+    wide, sums = refs[sectors + 3:]
     fields, levels, rows, width = circle_refs[0].shape
     ways = wide.shape[0]
     length = ways * LANES
@@ -116,54 +116,46 @@
             assemble(a)
         lane = lax.broadcasted_iota(jnp.int32, (rows, LANES), 1)
 
-        def forward(field, carry):
-            span = pl.ds(pl.multiple_of(field * per_field, per_field), per_field)
-            tile = [wide[a, span, :] for a in range(ways)]
-            even = [tile[a] + tile[ways - a] for a in range(1, pairs + 1)]
-            odd = [tile[a] - tile[ways - a] for a in range(1, pairs + 1)]
-            real_wave[span, :] = tile[0] + sum(even)
-            for k in range(1, pairs + 1):
-                turn = [2.0 * math.pi * (a * k % ways) / ways for a in range(1, pairs + 1)]
-                block_wave[k - 1, span, :LANES] = tile[0] + sum(math.cos(t) * e for t, e in zip(turn, even))
-                block_wave[k - 1, span, LANES:] = -sum(math.sin(t) * o for t, o in zip(turn, odd))
-            return carry
-
-        lax.fori_loop(0, fields, forward, 0)
-
         def damp(spectrum, damping):
             shaped = spectrum.reshape(fields * levels, rows, damping.shape[-1])
             return (shaped * damping[None]).reshape(spectrum.shape)
 
+        folds = range(1, pairs + 1)
+        wanted = [a for a in folds if a == 1 or a < tiles or ways - a < tiles]
+        origin = wide[0]
+        total = origin
+        for a in folds:
+            low, high = wide[a], wide[ways - a]
+            wide[a], wide[ways - a] = low + high, low - high
+            total = total + wide[a]
         half = LANES // 2
         wave = (jnp.where(lane <= half, lane, lane - half) * ways).astype(jnp.float32)
         real_high, real_low = table[2 * pairs, :LANES, :LANES], table[2 * pairs, :LANES, LANES:]
-        spectrum = dot_split(real_wave[...], real_high, real_low, False)
-        spectrum = damp(spectrum, damping_of(limit, wave))
-        real_wave[...] = dot_split(spectrum, real_high, real_low, True)
-        for k in range(1, pairs + 1):
+        spectrum = damp(dot_split(total, real_high, real_low, False), damping_of(limit, wave))
+        base = dot_split(spectrum, real_high, real_low, True) * (1.0 / ways)
+        for k in folds:
+            turn = [2.0 * math.pi * (a * k % ways) / ways for a in folds]
+            cosines = wide[0] + sum(math.cos(t) * wide[a] for t, a in zip(turn, folds))
+            sines = -sum(math.sin(t) * wide[ways - a] for t, a in zip(turn, folds))
             mode = k + ways * lane
             one = damping_of(limit, jnp.minimum(mode, length - mode).astype(jnp.float32))
-            damping = jnp.concatenate([one, one], axis=1)
+            damping = jnp.concatenate([one, one], axis=1) * (2.0 / ways)
             high, low = table[k - 1], table[pairs + k - 1]
-            spectrum = dot_split(block_wave[k - 1], high, low, False)
-            block_wave[k - 1] = dot_split(damp(spectrum, damping), high, low, True)
-
-        def backward(field, carry):
-            span = pl.ds(pl.multiple_of(field * per_field, per_field), per_field)
-            base = real_wave[span, :] * (1.0 / ways)
-            cosines = [block_wave[k, span, :LANES] for k in range(pairs)]
-            sines = [block_wave[k, span, LANES:] for k in range(pairs)]
-            wide[0, span, :] = base + (2.0 / ways) * sum(cosines)
-            for a in range(1, pairs + 1):
-                turn = [2.0 * math.pi * (a * k % ways) / ways for k in range(1, pairs + 1)]
-                even = base + sum((2.0 / ways * math.cos(t)) * c for t, c in zip(turn, cosines))
-                odd = sum((2.0 / ways * math.sin(t)) * s for t, s in zip(turn, sines))
-                wide[a, span, :] = even - odd
-                if a == 1 or ways - a < tiles:
-                    wide[ways - a, span, :] = even + odd
-            return carry
-
-        lax.fori_loop(0, fields, backward, 0)
+            spectrum = dot_split(jnp.concatenate([cosines, sines], axis=1), high, low, False)
+            wave_back = dot_split(damp(spectrum, damping), high, low, True)
+            cosines, sines = wave_back[:, :LANES], wave_back[:, LANES:]
+            sums[0] = (base if k == 1 else sums[0]) + cosines
+            for a in wanted:
+                t = 2.0 * math.pi * (a * k % ways) / ways
+                sums[a] = (base if k == 1 else sums[a]) + math.cos(t) * cosines
+                part_sines = math.sin(t) * sines
+                sums[pairs + a] = part_sines if k == 1 else sums[pairs + a] + part_sines
+        wide[0] = sums[0]
+        for a in wanted:
+            if a < tiles:
+                wide[a] = sums[a] - sums[pairs + a]
+            if a == 1 or ways - a < tiles:
+                wide[ways - a] = sums[a] + sums[pairs + a]
 
     def emit(field, carry):
         lane = lax.broadcasted_iota(jnp.int32, (levels, LANES), 1)
@@ -552,8 +544,7 @@
             out_specs=(VMEM,) * 3,
             scratch_shapes=[
                 pltpu.VMEM((length // LANES, lines, LANES), f32),
-                pltpu.VMEM((lines, LANES), f32),
-                pltpu.VMEM((table.shape[0] // 2, lines, 2 * LANES), f32),
+                pltpu.VMEM((length // LANES, lines, LANES), f32),
             ],
             compiler_params=PARAMS,
             name="polar_filter",

time: 40.1 us -> 39.6 us (0.988)
  no operation moved by 1% of the time
where the time goes in v5:
time: 39.6 us; the launch traced here: 39.3 us
  starting transfers between devices  14.8 us (37%)
  Pallas kernels  14.3 us (36%)
  waiting for transfers between devices  9.9 us (25%)
    pallas_call x2, Pallas kernels, shards(): pl.pallas_call(functools.partial(transport_kernel, n, len(earlier), secto...  7.03 us
    ppermute x3, starting transfers between devices, to_bands(): lax.ppermute(first, 'lat', even_pairs)  6.99 us
    ppermute x2, waiting for transfers between devices, sector_ahead(): lax.ppermute(values, 'lon', [(s, (s - offset) % sectors) for s in range(s...  6.02 us
    ppermute x3, starting transfers between devices, to_bands(): lax.ppermute(second, 'lat', odd_pairs)  5.73 us
    ppermute x3, waiting for transfers between devices, to_bands(): lax.ppermute(second, 'lat', odd_pairs)  3.35 us
    pallas_call x2, Pallas kernels, shards(): pl.pallas_call(functools.partial(filter_kernel, sectors, c == 0), out_sha...  2.74 us
    pallas_call x1, Pallas kernels, shards(): pl.pallas_call(functools.partial(rest_pack_kernel, chunks), out_shape=(*p...  2.48 us
    ppermute x2, starting transfers between devices, sector_ahead(): lax.ppermute(values, 'lon', [(s, (s - offset) % sectors) for s in range(s...  2.09 us
  transfers between devices with their start and end apart: 8, of which 3 were waited for; matrix products, arithmetic and copies ran while one was open for 0% of the time, Pallas kernels for 23%

profile of v5, /device:TPU:16, one launch (start us, length us, event | category | flops | bytes accessed | tf_op | source)
XLA Modules:
  0.0 39.3 jit_solution(17801073485859904670)
XLA Ops:
  0.0 0.0 copy-start
  0.0 0.0 copy-start.2
  0.0 1.6 %first_pack.1.refs_0_ = f32[3,8,8,640]{3,2,1,0:T(8,128)S(1)} custom-call(f32[5,8,8,576]{3,2,1,0:T(8,128)} %adjoint.3, f32[8,8,576]{2,1,0:T(8,128)} %refs_0_.3, f32[8,8,576]{2,1,0:T(8,128)} %refs_1_.3, f32[8,8,576]{2,1,0:T(8,128)} %refs_2_.3, f32[8,8,576]{2,1,0:T(8,128)} %refs_3_.3), custom_call_target="tpu_custom_call" | custom-call | tf_op jit(solution)/shard_map/first_pack/pallas_call | solution.py:495
  1.6 1.6 %collective-permute-start.2 = (f32[3,8,8,640]{3,2,1,0:T(8,128)S(1)}, f32[3,8,8,640]{3,2,1,0:T(8,128)}, u32[]{:S(2)}, u32[]{:S(2)}) collective-permute-start(f32[3,8,8,640]{3,2,1,0:T(8,128)S(1)} %first_pack.1.refs_0_), channel_id=1, source_target_pairs={{0,2},{2,0},{1,3},{3,1},{4,6},{6,4},{5,7},{7,5},{8,10},{10,8},{9,1... | collective-permute-start | bytes 1474568 | tf_op jit(solution)/shard_map/ppermute | solution.py:482
  3.1 2.5 %rest_pack.1 = (f32[2,8,8,640]{3,2,1,0:T(8,128)}, f32[8,4,8,640]{3,2,1,0:T(8,128)S(1)}, f32[6,4,8,640]{3,2,1,0:T(8,128)}, f32[6,4,8,640]{3,2,1,0:T(8,128)}) custom-call(f32[5,8,8,576]{3,2,1,0:T(8,128)} %adjoint.3, f32[8,8,576]{2,1,0:T(8,128)} %refs_0_.3, f32[8,8,576]{2,1,0:T(8,128)} %refs_1_.3, f32[8,8,576]{2,1,0:T(8,128)} %refs_2_.3, f32[8,8,576]{2,1,0:T(8,128)} %refs_3_.3), custom_call_target="tpu_custom_call" | custom-call | tf_op jit(solution)/shard_map/rest_pack/pallas_call | solution.py:509
  5.6 0.0 copy-start.1
  5.6 1.6 %collective-permute-start = (f32[6,4,8,640]{3,2,1,0:T(8,128)}, f32[6,4,8,640]{3,2,1,0:T(8,128)S(1)}, u32[]{:S(2)}, u32[]{:S(2)}) collective-permute-start(f32[6,4,8,640]{3,2,1,0:T(8,128)} %get-tuple-element.18), channel_id=1, source_target_pairs={{0,4},{8,12},{4,0},{12,8},{1,5},{9,13},{5,1},{13,9},{2,6},{10,14},... | collective-permute-start | bytes 1474568 | tf_op jit(solution)/shard_map/ppermute | solution.py:485
  7.3 0.5 %collective-permute-start.5 = (f32[2,8,8,640]{3,2,1,0:T(8,128)}, f32[2,8,8,640]{3,2,1,0:T(8,128)}, u32[]{:S(2)}, u32[]{:S(2)}) collective-permute-start(f32[2,8,8,640]{3,2,1,0:T(8,128)} %get-tuple-element.25.refs_0_), channel_id=1, source_target_pairs={{0,2},{2,0},{1,3},{3,1},{4,6},{6,4},{5,7},{7,5},{8,10},{10,8},{9,1... | collective-permute-start | bytes 983048 | tf_op jit(solution)/shard_map/ppermute | solution.py:482
  7.8 1.9 %collective-permute-start.1 = (f32[6,4,8,640]{3,2,1,0:T(8,128)}, f32[6,4,8,640]{3,2,1,0:T(8,128)S(1)}, u32[]{:S(2)}, u32[]{:S(2)}) collective-permute-start(f32[6,4,8,640]{3,2,1,0:T(8,128)} %get-tuple-element.19), channel_id=1, source_target_pairs={{4,8},{8,4},{5,9},{9,5},{6,10},{10,6},{7,11},{11,7},{20,24},{24,20... | collective-permute-start | bytes 1474568 | tf_op jit(solution)/shard_map/ppermute | solution.py:485
  9.7 0.0 copy-done.2
  9.7 0.1 dynamic-slice_convert_fusion
  9.8 6.0 %collective-permute-done.2.refs_1_ = f32[3,8,8,640]{3,2,1,0:T(8,128)} collective-permute-done((f32[3,8,8,640]{3,2,1,0:T(8,128)S(1)}, f32[3,8,8,640]{3,2,1,0:T(8,128)}, u32[]{:S(2)}, u32[]{:S(2)}) %collective-permute-start.2) | collective-permute-done | bytes 491552 | tf_op jit(solution)/shard_map/ppermute | solution.py:482
  15.8 0.1 broadcast_in_dim.2.limit_ref
  15.9 0.0 copy-done
  15.9 1.4 %polar_filter.2 = (f32[3,8,8,640]{3,2,1,0:T(8,128)S(1)}, f32[3,6,8,640]{3,2,1,0:T(8,128)S(1)}, f32[3,6,8,640]{3,2,1,0:T(8,128)S(1)}) custom-call(f32[8,128]{1,0:T(8,128)S(1)} %broadcast_in_dim.2.limit_ref, bf16[9,256,256]{2,1,0:T(8,128)(2,1)S(1)} %copy-done, f32[3,8,8,640]{3,2,1,0:T(8,128)S(1)} %first_pack.1.refs_0_, ...), custom_call_target="tpu_custom_call" | custom-call | tf_op jit(solution)/shard_map/polar_filter/pallas_call | solution.py:536
  17.3 3.2 %collective-permute-start.3 = (f32[3,6,8,640]{3,2,1,0:T(8,128)S(1)}, f32[3,6,8,640]{3,2,1,0:T(8,128)S(1)}, u32[]{:S(2)}, u32[]{:S(2)}) collective-permute-start(f32[3,6,8,640]{3,2,1,0:T(8,128)S(1)} %get-tuple-element.21), channel_id=1, source_target_pairs={{0,4},{8,12},{4,0},{12,8},{1,5},{9,13},{5,1},{13,9},{2,6},{10,14},... | collective-permute-start | bytes 1105928 | tf_op jit(solution)/shard_map/ppermute | solution.py:485
  20.5 1.9 %collective-permute-start.4 = (f32[3,6,8,640]{3,2,1,0:T(8,128)S(1)}, f32[3,6,8,640]{3,2,1,0:T(8,128)S(1)}, u32[]{:S(2)}, u32[]{:S(2)}) collective-permute-start(f32[3,6,8,640]{3,2,1,0:T(8,128)S(1)} %get-tuple-element.22), channel_id=1, source_target_pairs={{4,8},{8,4},{5,9},{9,5},{6,10},{10,6},{7,11},{11,7},{20,24},{24,20... | collective-permute-start | bytes 1105928 | tf_op jit(solution)/shard_map/ppermute | solution.py:485
  22.4 0.0 collective-permute-done.5.refs_1_
  22.4 1.3 %polar_filter.3 = (f32[2,8,8,640]{3,2,1,0:T(8,128)S(1)}, f32[2,6,8,640]{3,2,1,0:T(8,128)S(1)}, f32[2,6,8,640]{3,2,1,0:T(8,128)S(1)}) custom-call(f32[8,128]{1,0:T(8,128)S(1)} %broadcast_in_dim.2.limit_ref, bf16[9,256,256]{2,1,0:T(8,128)(2,1)S(1)} %copy-done, f32[2,8,8,640]{3,2,1,0:T(8,128)} %get-tuple-element.25.refs_0_, ...), custom_call_target="tpu_custom_call" | custom-call | tf_op jit(solution)/shard_map/polar_filter/pallas_call | solution.py:536
  23.8 2.2 %collective-permute-start.6 = (f32[2,6,8,640]{3,2,1,0:T(8,128)S(1)}, f32[2,6,8,640]{3,2,1,0:T(8,128)S(1)}, u32[]{:S(2)}, u32[]{:S(2)}) collective-permute-start(f32[2,6,8,640]{3,2,1,0:T(8,128)S(1)} %get-tuple-element.27), channel_id=1, source_target_pairs={{0,4},{8,12},{4,0},{12,8},{1,5},{9,13},{5,1},{13,9},{2,6},{10,14},... | collective-permute-start | bytes 737288 | tf_op jit(solution)/shard_map/ppermute | solution.py:485
  25.9 0.0 collective-permute-done.rate_first
  25.9 1.9 %collective-permute-start.7 = (f32[2,6,8,640]{3,2,1,0:T(8,128)S(1)}, f32[2,6,8,640]{3,2,1,0:T(8,128)S(1)}, u32[]{:S(2)}, u32[]{:S(2)}) collective-permute-start(f32[2,6,8,640]{3,2,1,0:T(8,128)S(1)} %get-tuple-element.28), channel_id=1, source_target_pairs={{4,8},{8,4},{5,9},{9,5},{6,10},{10,6},{7,11},{11,7},{20,24},{24,20... | collective-permute-start | bytes 737288 | tf_op jit(solution)/shard_map/ppermute | solution.py:485
  27.9 0.0 collective-permute-done.1.rate_second
  27.9 0.5 %collective-permute-done.3.first.first_ref = f32[3,6,8,640]{3,2,1,0:T(8,128)S(1)} collective-permute-done((f32[3,6,8,640]{3,2,1,0:T(8,128)S(1)}, f32[3,6,8,640]{3,2,1,0:T(8,128)S(1)}, u32[]{:S(2)}, u32[]{:S(2)}) %collective-permute-start.3) | collective-permute-done | bytes 368672 | tf_op jit(solution)/shard_map/ppermute | solution.py:485
  28.4 3.3 %collective-permute-done.4.second.second_ref = f32[3,6,8,640]{3,2,1,0:T(8,128)S(1)} collective-permute-done((f32[3,6,8,640]{3,2,1,0:T(8,128)S(1)}, f32[3,6,8,640]{3,2,1,0:T(8,128)S(1)}, u32[]{:S(2)}, u32[]{:S(2)}) %collective-permute-start.4) | collective-permute-done | bytes 368672 | tf_op jit(solution)/shard_map/ppermute | solution.py:485
  31.7 0.0 copy-done.1
  31.7 0.5 %faces.1 = (f32[20,5,8,640]{3,2,1,0:T(8,128)S(1)}, f32[5,5,8,128]{3,2,1,0:T(8,128)S(1)}) custom-call(f32[5,8,5]{2,1,0:T(8,128)S(1)} %bitcast.1, f32[8,4,8,640]{3,2,1,0:T(8,128)S(1)} %get-tuple-element.17.rate_own, f32[6,4,8,640]{3,2,1,0:T(8,128)S(1)} %collective-permute-done.rate_first, f32[6,4,8,640]{3,2,1,0:T(8,128)S(1)} %collective-permute-done.1.rate_second, ...), custom_call_target="tpu_custom_call" | custom-call | tf_op jit(solution)/shard_map/faces/pallas_call | solution.py:554
  32.3 3.4 %transport.2.refs_0_ = f32[3,8,8,640]{3,2,1,0:T(8,128)S(1)} custom-call(f32[5,5,8,128]{3,2,1,0:T(8,128)S(1)} %get-tuple-element.23.power_ref, f32[20,5,8,640]{3,2,1,0:T(8,128)S(1)} %get-tuple-element.24.rates, f32[3,8,8,640]{3,2,1,0:T(8,128)S(1)} %get-tuple-element.20.own.own_ref, f32[3,6,8,640]{3,2,1,0:T(8,128)S(1)} %collective-permute-done.3.first.first_ref, ...), custom_call_target="tpu_custom_call" | custom-call | tf_op jit(solution)/shard_map/transport/pallas_call | solution.py:568
  35.7 0.0 collective-permute-done.6.first_ref
  35.7 0.0 collective-permute-done.7.second_ref
  35.7 3.6 %transport.3 = f32[5,8,8,576]{3,2,1,0:T(8,128)} custom-call(f32[5,5,8,128]{3,2,1,0:T(8,128)S(1)} %get-tuple-element.23.power_ref, f32[20,5,8,640]{3,2,1,0:T(8,128)S(1)} %get-tuple-element.24.rates, f32[2,8,8,640]{3,2,1,0:T(8,128)S(1)} %get-tuple-element.26.own_ref, f32[2,6,8,640]{3,2,1,0:T(8,128)S(1)} %collective-permute-done.6.first_ref, ...), custom_call_target="tpu_custom_call" | custom-call | tf_op jit(solution)/shard_map/transport/pallas_call | solution.py:568
Async XLA Ops:
  0.0 15.9 %copy-start = (bf16[9,256,256]{2,1,0:T(8,128)(2,1)S(1)}, bf16[9,256,256]{2,1,0:T(8,128)(2,1)}, u32[]{:S(2)}) copy-start(bf16[9,256,256]{2,1,0:T(8,128)(2,1)} %constant.13.clone.table) | copy-start | bytes 3538948
  0.0 9.7 %copy-start.2 = (s32[32]{0:T(128)S(1)}, s32[32]{0:T(128)}, u32[]{:S(2)}) copy-start(s32[32]{0:T(128)} %param.14) | copy-start | bytes 388
  1.6 14.3 %collective-permute-start.2 = (f32[3,8,8,640]{3,2,1,0:T(8,128)S(1)}, f32[3,8,8,640]{3,2,1,0:T(8,128)}, u32[]{:S(2)}, u32[]{:S(2)}) collective-permute-start(f32[3,8,8,640]{3,2,1,0:T(8,128)S(1)} %first_pack.1.refs_0_), channel_id=1, source_target_pairs={{0,2},{2,0},{1,3},{3,1},{4,6},{6,4},{5,7},{7,5},{8,10},{10,8},{9,1... | collective-permute-start | bytes 1474568 | tf_op jit(solution)/shard_map/ppermute | solution.py:482
  5.6 26.1 %copy-start.1 = (f32[8,5,5]{2,0,1:T(8,128)S(1)}, f32[8,5,5]{2,0,1:T(8,128)}, u32[]{:S(2)}) copy-start(f32[8,5,5]{2,0,1:T(8,128)} %param.13) | copy-start | bytes 2404
  5.6 20.3 %collective-permute-start = (f32[6,4,8,640]{3,2,1,0:T(8,128)}, f32[6,4,8,640]{3,2,1,0:T(8,128)S(1)}, u32[]{:S(2)}, u32[]{:S(2)}) collective-permute-start(f32[6,4,8,640]{3,2,1,0:T(8,128)} %get-tuple-element.18), channel_id=1, source_target_pairs={{0,4},{8,12},{4,0},{12,8},{1,5},{9,13},{5,1},{13,9},{2,6},{10,14},... | collective-permute-start | bytes 1474568 | tf_op jit(solution)/shard_map/ppermute | solution.py:485
  7.3 15.1 %collective-permute-start.5 = (f32[2,8,8,640]{3,2,1,0:T(8,128)}, f32[2,8,8,640]{3,2,1,0:T(8,128)}, u32[]{:S(2)}, u32[]{:S(2)}) collective-permute-start(f32[2,8,8,640]{3,2,1,0:T(8,128)} %get-tuple-element.25.refs_0_), channel_id=1, source_target_pairs={{0,2},{2,0},{1,3},{3,1},{4,6},{6,4},{5,7},{7,5},{8,10},{10,8},{9,1... | collective-permute-start | bytes 983048 | tf_op jit(solution)/shard_map/ppermute | solution.py:482
  7.8 20.1 %collective-permute-start.1 = (f32[6,4,8,640]{3,2,1,0:T(8,128)}, f32[6,4,8,640]{3,2,1,0:T(8,128)S(1)}, u32[]{:S(2)}, u32[]{:S(2)}) collective-permute-start(f32[6,4,8,640]{3,2,1,0:T(8,128)} %get-tuple-element.19), channel_id=1, source_target_pairs={{4,8},{8,4},{5,9},{9,5},{6,10},{10,6},{7,11},{11,7},{20,24},{24,20... | collective-permute-start | bytes 1474568 | tf_op jit(solution)/shard_map/ppermute | solution.py:485
  17.3 11.1 %collective-permute-start.3 = (f32[3,6,8,640]{3,2,1,0:T(8,128)S(1)}, f32[3,6,8,640]{3,2,1,0:T(8,128)S(1)}, u32[]{:S(2)}, u32[]{:S(2)}) collective-permute-start(f32[3,6,8,640]{3,2,1,0:T(8,128)S(1)} %get-tuple-element.21), channel_id=1, source_target_pairs={{0,4},{8,12},{4,0},{12,8},{1,5},{9,13},{5,1},{13,9},{2,6},{10,14},... | collective-permute-start | bytes 1105928 | tf_op jit(solution)/shard_map/ppermute | solution.py:485
  20.5 11.3 %collective-permute-start.4 = (f32[3,6,8,640]{3,2,1,0:T(8,128)S(1)}, f32[3,6,8,640]{3,2,1,0:T(8,128)S(1)}, u32[]{:S(2)}, u32[]{:S(2)}) collective-permute-start(f32[3,6,8,640]{3,2,1,0:T(8,128)S(1)} %get-tuple-element.22), channel_id=1, source_target_pairs={{4,8},{8,4},{5,9},{9,5},{6,10},{10,6},{7,11},{11,7},{20,24},{24,20... | collective-permute-start | bytes 1105928 | tf_op jit(solution)/shard_map/ppermute | solution.py:485
  23.8 12.0 %collective-permute-start.6 = (f32[2,6,8,640]{3,2,1,0:T(8,128)S(1)}, f32[2,6,8,640]{3,2,1,0:T(8,128)S(1)}, u32[]{:S(2)}, u32[]{:S(2)}) collective-permute-start(f32[2,6,8,640]{3,2,1,0:T(8,128)S(1)} %get-tuple-element.27), channel_id=1, source_target_pairs={{0,4},{8,12},{4,0},{12,8},{1,5},{9,13},{5,1},{13,9},{2,6},{10,14},... | collective-permute-start | bytes 737288 | tf_op jit(solution)/shard_map/ppermute | solution.py:485
  25.9 9.8 %collective-permute-start.7 = (f32[2,6,8,640]{3,2,1,0:T(8,128)S(1)}, f32[2,6,8,640]{3,2,1,0:T(8,128)S(1)}, u32[]{:S(2)}, u32[]{:S(2)}) collective-permute-start(f32[2,6,8,640]{3,2,1,0:T(8,128)S(1)} %get-tuple-element.28), channel_id=1, source_target_pairs={{4,8},{8,4},{5,9},{9,5},{6,10},{10,6},{7,11},{11,7},{20,24},{24,20... | collective-permute-start | bytes 737288 | tf_op jit(solution)/shard_map/ppermute | solution.py:485

commit v6 on v5

--- a/solution.py
+++ b/solution.py
@@ -198,12 +198,6 @@
     return sector % LANES + HALO
 
 
-def limits_of(cutoff, rows):
-    lat = lax.axis_index("lat")
-    own = lax.dynamic_slice_in_dim(cutoff, lat * rows, rows, 0).astype(jnp.float32)
-    return jnp.broadcast_to(own[:, None], (rows, LANES))
-
-
 def write_state(state, payload, field, extra):
     levels, rows, sector = state.shape[1:]
     width = payload.shape[-1]
@@ -245,14 +239,16 @@
         write_state(state, payload, field, edges if field == 0 else zero)
 
 
-def rest_pack_kernel(chunks, adjoint, *refs):
+def rest_pack_kernel(chunks, cutoff, adjoint, *refs):
     sources = refs[:RATES]
     count = len(chunks) - 1
     payloads = refs[RATES:RATES + count]
-    own_out, first_out, second_out = refs[RATES + count:RATES + count + 3]
-    state, rates, sems = refs[RATES + count + 3:]
+    own_out, first_out, second_out, limit_out = refs[RATES + count:RATES + count + 4]
+    state, rates, cutoffs, sems = refs[RATES + count + 4:]
     levels, rows, sector = sources[0].shape
     width = own_out.shape[-1]
+    cutoff_copy = pltpu.make_async_copy(cutoff, cutoffs, sems.at[RATES + 1])
+    cutoff_copy.start()
     copies = [pltpu.make_async_copy(src, rates.at[q], sems.at[q]) for q, src in enumerate(sources)]
     if count:
         copies.append(pltpu.make_async_copy(adjoint.at[chunks[0]:], state, sems.at[RATES]))
@@ -272,6 +268,12 @@
             if q == 0:
                 tile = jnp.where(jnp.logical_and(is_last, row == rows - 1), 0.0, tile)
             own_out[:, q, :, start:start + LANES] = jnp.swapaxes(tile, 0, 1)
+    cutoff_copy.wait()
+    sublane = lax.broadcasted_iota(jnp.int32, (rows, LANES), 0)
+    limit = jnp.zeros((rows, LANES), jnp.float32)
+    for j in range(rows):
+        limit = jnp.where(sublane == j, cutoffs[lat * rows + j].astype(jnp.float32), limit)
+    limit_out[...] = limit
     if count:
         copies[RATES].wait()
     zero = jnp.zeros((levels, rows, LANES), jnp.float32)
@@ -506,29 +508,30 @@
         name="first_pack",
     )(*inputs)
     first_circle = [first_payload] + [sector_ahead(first_payload, k) for k in range(1, sectors)]
-    *payloads, rate_own, rate_first, rate_second = pl.pallas_call(
+    *payloads, rate_own, rate_first, rate_second, limits = pl.pallas_call(
         functools.partial(rest_pack_kernel, chunks),
         out_shape=(
             *payload_shapes[1:],
             jax.ShapeDtypeStruct((rows,) + rate_shape, f32),
             jax.ShapeDtypeStruct((HALO,) + rate_shape, f32),
             jax.ShapeDtypeStruct((HALO,) + rate_shape, f32),
+            jax.ShapeDtypeStruct((rows, LANES), f32),
         ),
-        in_specs=[HBM] * (1 + RATES),
-        out_specs=(VMEM,) * (len(chunks) + 2),
+        in_specs=[HBM] * (2 + RATES),
+        out_specs=(VMEM,) * (len(chunks) + 3),
         scratch_shapes=[
             pltpu.VMEM((later,) + adjoint_in.shape[1:], f32),
             pltpu.VMEM((RATES,) + lat_ahead.shape, f32),
-            pltpu.SemaphoreType.DMA((1 + RATES,)),
+            pltpu.SMEM(cutoff.shape, cutoff.dtype),
+            pltpu.SemaphoreType.DMA((2 + RATES,)),
         ],
         compiler_params=PARAMS,
         name="rest_pack",
-    )(*inputs)
+    )(pltpu.with_memory_space_constraint(cutoff, pltpu.HBM), *inputs)
     circles = [[part] + [sector_ahead(part, k) for k in range(1, sectors)] for part in payloads]
     circles.insert(0, first_circle)
     rate_first, rate_second = to_bands(rate_first, rate_second)
 
-    limits = limits_of(cutoff, rows)
     table = jnp.asarray(mode_tables(length))
     results = []
     for c, (n, circle) in enumerate(zip(chunks, circles)):

time: 39.6 us -> 38.3 us (0.967)
  Pallas kernels: 14.3 us -> 11.1 us
  waiting for transfers between devices: 9.9 us -> 11.3 us
  starting transfers between devices: 14.8 us -> 15.6 us
    pallas_call x2, Pallas kernels: 2.74 us -> 0.59 us  [shards(): pl.pallas_call(functools.partial(filter_kernel, sectors, c == 0), out_sha...]
    ppermute x2, waiting for transfers between devices: 6.02 us -> 7.47 us  [sector_ahead(): lax.ppermute(values, 'lon', [(s, (s - offset) % sectors) for s in range(s...]
    pallas_call x1, Pallas kernels: 2.48 us -> 1.43 us  [shards(): pl.pallas_call(functools.partial(rest_pack_kernel, chunks), out_shape=(*p...]
    ppermute x3, starting transfers between devices: 6.99 us -> 7.76 us  [to_bands(): lax.ppermute(first, 'lat', even_pairs)]
  transfers between devices with their start and end apart: 8 -> 8, of which waited for: 3 -> 4; matrix products, arithmetic and copies ran while one was open for 0% -> 0% of each run, Pallas kernels for 23% -> 16%
where the time goes in v6:
time: 38.3 us; the launch traced here: 38.1 us
  starting transfers between devices  15.6 us (41%)
  waiting for transfers between devices  11.3 us (30%)
  Pallas kernels  11.1 us (29%)
    ppermute x3, starting transfers between devices, to_bands(): lax.ppermute(first, 'lat', even_pairs)  7.76 us
    ppermute x2, waiting for transfers between devices, sector_ahead(): lax.ppermute(values, 'lon', [(s, (s - offset) % sectors) for s in range(s...  7.47 us
    pallas_call x2, Pallas kernels, shards(): pl.pallas_call(functools.partial(transport_kernel, n, len(earlier), secto...  7.03 us
    ppermute x3, starting transfers between devices, to_bands(): lax.ppermute(second, 'lat', odd_pairs)  5.73 us
    ppermute x3, waiting for transfers between devices, to_bands(): lax.ppermute(second, 'lat', odd_pairs)  3.35 us
    ppermute x2, starting transfers between devices, sector_ahead(): lax.ppermute(values, 'lon', [(s, (s - offset) % sectors) for s in range(s...  2.09 us
    pallas_call x1, Pallas kernels, shards(): pl.pallas_call(first_pack_kernel, out_shape=payload_shapes[0], in_specs=[...  1.55 us
    pallas_call x1, Pallas kernels, shards(): pl.pallas_call(functools.partial(rest_pack_kernel, chunks), out_shape=(*p...  1.43 us
  transfers between devices with their start and end apart: 8, of which 4 were waited for; matrix products, arithmetic and copies ran while one was open for 0% of the time, Pallas kernels for 16%

profile of v6, /device:TPU:16, one launch (start us, length us, event | category | flops | bytes accessed | tf_op | source)
XLA Modules:
  0.0 38.1 jit_solution(12413616349350830914)
XLA Ops:
  0.0 0.0 copy-start
  0.0 1.5 %first_pack.1.refs_0_ = f32[3,8,8,640]{3,2,1,0:T(8,128)S(1)} custom-call(f32[5,8,8,576]{3,2,1,0:T(8,128)} %adjoint.3, f32[8,8,576]{2,1,0:T(8,128)} %refs_0_.3, f32[8,8,576]{2,1,0:T(8,128)} %refs_1_.3, f32[8,8,576]{2,1,0:T(8,128)} %refs_2_.3, f32[8,8,576]{2,1,0:T(8,128)} %refs_3_.3), custom_call_target="tpu_custom_call" | custom-call | tf_op jit(solution)/shard_map/first_pack/pallas_call | solution.py:497
  1.6 1.6 %collective-permute-start.2 = (f32[3,8,8,640]{3,2,1,0:T(8,128)S(1)}, f32[3,8,8,640]{3,2,1,0:T(8,128)S(1)}, u32[]{:S(2)}, u32[]{:S(2)}) collective-permute-start(f32[3,8,8,640]{3,2,1,0:T(8,128)S(1)} %first_pack.1.refs_0_), channel_id=1, source_target_pairs={{0,2},{2,0},{1,3},{3,1},{4,6},{6,4},{5,7},{7,5},{8,10},{10,8},{9,1... | collective-permute-start | bytes 1474568 | tf_op jit(solution)/shard_map/ppermute | solution.py:484
  3.1 1.4 %rest_pack.1 = (f32[2,8,8,640]{3,2,1,0:T(8,128)S(1)}, f32[8,4,8,640]{3,2,1,0:T(8,128)S(1)}, f32[6,4,8,640]{3,2,1,0:T(8,128)S(1)}, f32[6,4,8,640]{3,2,1,0:T(8,128)S(1)}, f32[8,128]{1,0:T(8,128)S(1)}) custom-call(s32[32]{0:T(128)} %cutoff.1, f32[5,8,8,576]{3,2,1,0:T(8,128)} %adjoint.3, f32[8,8,576]{2,1,0:T(8,128)} %refs_0_.3, f32[8,8,576]{2,1,0:T(8,128)} %refs_1_.3, ...), custom_call_target="tpu_custom_call" | custom-call | tf_op jit(solution)/shard_map/rest_pack/pallas_call | solution.py:511
  4.6 0.0 copy-start.1
  4.6 1.6 %collective-permute-start = (f32[6,4,8,640]{3,2,1,0:T(8,128)S(1)}, f32[6,4,8,640]{3,2,1,0:T(8,128)S(1)}, u32[]{:S(2)}, u32[]{:S(2)}) collective-permute-start(f32[6,4,8,640]{3,2,1,0:T(8,128)S(1)} %get-tuple-element.19), channel_id=1, source_target_pairs={{0,4},{8,12},{4,0},{12,8},{1,5},{9,13},{5,1},{13,9},{2,6},{10,14},... | collective-permute-start | bytes 1474568 | tf_op jit(solution)/shard_map/ppermute | solution.py:487
  6.2 0.5 %collective-permute-start.5 = (f32[2,8,8,640]{3,2,1,0:T(8,128)S(1)}, f32[2,8,8,640]{3,2,1,0:T(8,128)S(1)}, u32[]{:S(2)}, u32[]{:S(2)}) collective-permute-start(f32[2,8,8,640]{3,2,1,0:T(8,128)S(1)} %get-tuple-element.27.refs_0_), channel_id=1, source_target_pairs={{0,2},{2,0},{1,3},{3,1},{4,6},{6,4},{5,7},{7,5},{8,10},{10,8},{9,1... | collective-permute-start | bytes 983048 | tf_op jit(solution)/shard_map/ppermute | solution.py:484
  6.7 1.9 %collective-permute-start.1 = (f32[6,4,8,640]{3,2,1,0:T(8,128)S(1)}, f32[6,4,8,640]{3,2,1,0:T(8,128)S(1)}, u32[]{:S(2)}, u32[]{:S(2)}) collective-permute-start(f32[6,4,8,640]{3,2,1,0:T(8,128)S(1)} %get-tuple-element.20), channel_id=1, source_target_pairs={{4,8},{8,4},{5,9},{9,5},{6,10},{10,6},{7,11},{11,7},{20,24},{24,20... | collective-permute-start | bytes 1474568 | tf_op jit(solution)/shard_map/ppermute | solution.py:487
  8.7 7.1 %collective-permute-done.2.refs_1_ = f32[3,8,8,640]{3,2,1,0:T(8,128)S(1)} collective-permute-done((f32[3,8,8,640]{3,2,1,0:T(8,128)S(1)}, f32[3,8,8,640]{3,2,1,0:T(8,128)S(1)}, u32[]{:S(2)}, u32[]{:S(2)}) %collective-permute-start.2) | collective-permute-done | bytes 491552 | tf_op jit(solution)/shard_map/ppermute | solution.py:484
  15.7 0.0 copy-done
  15.7 0.3 polar_filter.2
  16.1 3.2 %collective-permute-start.3 = (f32[3,6,8,640]{3,2,1,0:T(8,128)S(1)}, f32[3,6,8,640]{3,2,1,0:T(8,128)S(1)}, u32[]{:S(2)}, u32[]{:S(2)}) collective-permute-start(f32[3,6,8,640]{3,2,1,0:T(8,128)S(1)} %get-tuple-element.23), channel_id=1, source_target_pairs={{0,4},{8,12},{4,0},{12,8},{1,5},{9,13},{5,1},{13,9},{2,6},{10,14},... | collective-permute-start | bytes 1105928 | tf_op jit(solution)/shard_map/ppermute | solution.py:487
  19.3 1.9 %collective-permute-start.4 = (f32[3,6,8,640]{3,2,1,0:T(8,128)S(1)}, f32[3,6,8,640]{3,2,1,0:T(8,128)S(1)}, u32[]{:S(2)}, u32[]{:S(2)}) collective-permute-start(f32[3,6,8,640]{3,2,1,0:T(8,128)S(1)} %get-tuple-element.24), channel_id=1, source_target_pairs={{4,8},{8,4},{5,9},{9,5},{6,10},{10,6},{7,11},{11,7},{20,24},{24,20... | collective-permute-start | bytes 1105928 | tf_op jit(solution)/shard_map/ppermute | solution.py:487
  21.2 0.4 %collective-permute-done.5.refs_1_ = f32[2,8,8,640]{3,2,1,0:T(8,128)S(1)} collective-permute-done((f32[2,8,8,640]{3,2,1,0:T(8,128)S(1)}, f32[2,8,8,640]{3,2,1,0:T(8,128)S(1)}, u32[]{:S(2)}, u32[]{:S(2)}) %collective-permute-start.5) | collective-permute-done | bytes 327712 | tf_op jit(solution)/shard_map/ppermute | solution.py:484
  21.6 0.3 polar_filter.3
  21.9 2.9 %collective-permute-start.6 = (f32[2,6,8,640]{3,2,1,0:T(8,128)S(1)}, f32[2,6,8,640]{3,2,1,0:T(8,128)S(1)}, u32[]{:S(2)}, u32[]{:S(2)}) collective-permute-start(f32[2,6,8,640]{3,2,1,0:T(8,128)S(1)} %get-tuple-element.29), channel_id=1, source_target_pairs={{0,4},{8,12},{4,0},{12,8},{1,5},{9,13},{5,1},{13,9},{2,6},{10,14},... | collective-permute-start | bytes 737288 | tf_op jit(solution)/shard_map/ppermute | solution.py:487
  24.8 0.0 collective-permute-done.rate_first
  24.8 1.9 %collective-permute-start.7 = (f32[2,6,8,640]{3,2,1,0:T(8,128)S(1)}, f32[2,6,8,640]{3,2,1,0:T(8,128)S(1)}, u32[]{:S(2)}, u32[]{:S(2)}) collective-permute-start(f32[2,6,8,640]{3,2,1,0:T(8,128)S(1)} %get-tuple-element.30), channel_id=1, source_target_pairs={{4,8},{8,4},{5,9},{9,5},{6,10},{10,6},{7,11},{11,7},{20,24},{24,20... | collective-permute-start | bytes 737288 | tf_op jit(solution)/shard_map/ppermute | solution.py:487
  26.7 0.0 collective-permute-done.1.rate_second
  26.7 0.5 %collective-permute-done.3.first.first_ref = f32[3,6,8,640]{3,2,1,0:T(8,128)S(1)} collective-permute-done((f32[3,6,8,640]{3,2,1,0:T(8,128)S(1)}, f32[3,6,8,640]{3,2,1,0:T(8,128)S(1)}, u32[]{:S(2)}, u32[]{:S(2)}) %collective-permute-start.3) | collective-permute-done | bytes 368672 | tf_op jit(solution)/shard_map/ppermute | solution.py:487
  27.2 3.3 %collective-permute-done.4.second.second_ref = f32[3,6,8,640]{3,2,1,0:T(8,128)S(1)} collective-permute-done((f32[3,6,8,640]{3,2,1,0:T(8,128)S(1)}, f32[3,6,8,640]{3,2,1,0:T(8,128)S(1)}, u32[]{:S(2)}, u32[]{:S(2)}) %collective-permute-start.4) | collective-permute-done | bytes 368672 | tf_op jit(solution)/shard_map/ppermute | solution.py:487
  30.5 0.0 copy-done.1
  30.5 0.5 %faces.1 = (f32[20,5,8,640]{3,2,1,0:T(8,128)S(1)}, f32[5,5,8,128]{3,2,1,0:T(8,128)S(1)}) custom-call(f32[5,8,5]{2,1,0:T(8,128)S(1)} %bitcast.1, f32[8,4,8,640]{3,2,1,0:T(8,128)S(1)} %get-tuple-element.18.rate_own, f32[6,4,8,640]{3,2,1,0:T(8,128)S(1)} %collective-permute-done.rate_first, f32[6,4,8,640]{3,2,1,0:T(8,128)S(1)} %collective-permute-done.1.rate_second, ...), custom_call_target="tpu_custom_call" | custom-call | tf_op jit(solution)/shard_map/faces/pallas_call | solution.py:557
  31.0 3.4 %transport.2.refs_0_ = f32[3,8,8,640]{3,2,1,0:T(8,128)S(1)} custom-call(f32[5,5,8,128]{3,2,1,0:T(8,128)S(1)} %get-tuple-element.25.power_ref, f32[20,5,8,640]{3,2,1,0:T(8,128)S(1)} %get-tuple-element.26.rates, f32[3,8,8,640]{3,2,1,0:T(8,128)S(1)} %get-tuple-element.22.own.own_ref, f32[3,6,8,640]{3,2,1,0:T(8,128)S(1)} %collective-permute-done.3.first.first_ref, ...), custom_call_target="tpu_custom_call" | custom-call | tf_op jit(solution)/shard_map/transport/pallas_call | solution.py:571
  34.5 0.0 collective-permute-done.6.first_ref
  34.5 0.0 collective-permute-done.7.second_ref
  34.5 3.6 %transport.3 = f32[5,8,8,576]{3,2,1,0:T(8,128)} custom-call(f32[5,5,8,128]{3,2,1,0:T(8,128)S(1)} %get-tuple-element.25.power_ref, f32[20,5,8,640]{3,2,1,0:T(8,128)S(1)} %get-tuple-element.26.rates, f32[2,8,8,640]{3,2,1,0:T(8,128)S(1)} %get-tuple-element.28.own_ref, f32[2,6,8,640]{3,2,1,0:T(8,128)S(1)} %collective-permute-done.6.first_ref, ...), custom_call_target="tpu_custom_call" | custom-call | tf_op jit(solution)/shard_map/transport/pallas_call | solution.py:571
Async XLA Ops:
  0.0 15.7 %copy-start = (bf16[9,256,256]{2,1,0:T(8,128)(2,1)S(1)}, bf16[9,256,256]{2,1,0:T(8,128)(2,1)}, u32[]{:S(2)}) copy-start(bf16[9,256,256]{2,1,0:T(8,128)(2,1)} %constant.2.clone.table) | copy-start | bytes 3538948
  1.6 14.2 %collective-permute-start.2 = (f32[3,8,8,640]{3,2,1,0:T(8,128)S(1)}, f32[3,8,8,640]{3,2,1,0:T(8,128)S(1)}, u32[]{:S(2)}, u32[]{:S(2)}) collective-permute-start(f32[3,8,8,640]{3,2,1,0:T(8,128)S(1)} %first_pack.1.refs_0_), channel_id=1, source_target_pairs={{0,2},{2,0},{1,3},{3,1},{4,6},{6,4},{5,7},{7,5},{8,10},{10,8},{9,1... | collective-permute-start | bytes 1474568 | tf_op jit(solution)/shard_map/ppermute | solution.py:484
  4.6 25.9 %copy-start.1 = (f32[8,5,5]{2,0,1:T(8,128)S(1)}, f32[8,5,5]{2,0,1:T(8,128)}, u32[]{:S(2)}) copy-start(f32[8,5,5]{2,0,1:T(8,128)} %param.13) | copy-start | bytes 2404
  4.6 20.2 %collective-permute-start = (f32[6,4,8,640]{3,2,1,0:T(8,128)S(1)}, f32[6,4,8,640]{3,2,1,0:T(8,128)S(1)}, u32[]{:S(2)}, u32[]{:S(2)}) collective-permute-start(f32[6,4,8,640]{3,2,1,0:T(8,128)S(1)} %get-tuple-element.19), channel_id=1, source_target_pairs={{0,4},{8,12},{4,0},{12,8},{1,5},{9,13},{5,1},{13,9},{2,6},{10,14},... | collective-permute-start | bytes 1474568 | tf_op jit(solution)/shard_map/ppermute | solution.py:487
  6.2 15.4 %collective-permute-start.5 = (f32[2,8,8,640]{3,2,1,0:T(8,128)S(1)}, f32[2,8,8,640]{3,2,1,0:T(8,128)S(1)}, u32[]{:S(2)}, u32[]{:S(2)}) collective-permute-start(f32[2,8,8,640]{3,2,1,0:T(8,128)S(1)} %get-tuple-element.27.refs_0_), channel_id=1, source_target_pairs={{0,2},{2,0},{1,3},{3,1},{4,6},{6,4},{5,7},{7,5},{8,10},{10,8},{9,1... | collective-permute-start | bytes 983048 | tf_op jit(solution)/shard_map/ppermute | solution.py:484
  6.7 20.0 %collective-permute-start.1 = (f32[6,4,8,640]{3,2,1,0:T(8,128)S(1)}, f32[6,4,8,640]{3,2,1,0:T(8,128)S(1)}, u32[]{:S(2)}, u32[]{:S(2)}) collective-permute-start(f32[6,4,8,640]{3,2,1,0:T(8,128)S(1)} %get-tuple-element.20), channel_id=1, source_target_pairs={{4,8},{8,4},{5,9},{9,5},{6,10},{10,6},{7,11},{11,7},{20,24},{24,20... | collective-permute-start | bytes 1474568 | tf_op jit(solution)/shard_map/ppermute | solution.py:487
  16.1 11.1 %collective-permute-start.3 = (f32[3,6,8,640]{3,2,1,0:T(8,128)S(1)}, f32[3,6,8,640]{3,2,1,0:T(8,128)S(1)}, u32[]{:S(2)}, u32[]{:S(2)}) collective-permute-start(f32[3,6,8,640]{3,2,1,0:T(8,128)S(1)} %get-tuple-element.23), channel_id=1, source_target_pairs={{0,4},{8,12},{4,0},{12,8},{1,5},{9,13},{5,1},{13,9},{2,6},{10,14},... | collective-permute-start | bytes 1105928 | tf_op jit(solution)/shard_map/ppermute | solution.py:487
  19.3 11.2 %collective-permute-start.4 = (f32[3,6,8,640]{3,2,1,0:T(8,128)S(1)}, f32[3,6,8,640]{3,2,1,0:T(8,128)S(1)}, u32[]{:S(2)}, u32[]{:S(2)}) collective-permute-start(f32[3,6,8,640]{3,2,1,0:T(8,128)S(1)} %get-tuple-element.24), channel_id=1, source_target_pairs={{4,8},{8,4},{5,9},{9,5},{6,10},{10,6},{7,11},{11,7},{20,24},{24,20... | collective-permute-start | bytes 1105928 | tf_op jit(solution)/shard_map/ppermute | solution.py:487
  21.9 12.6 %collective-permute-start.6 = (f32[2,6,8,640]{3,2,1,0:T(8,128)S(1)}, f32[2,6,8,640]{3,2,1,0:T(8,128)S(1)}, u32[]{:S(2)}, u32[]{:S(2)}) collective-permute-start(f32[2,6,8,640]{3,2,1,0:T(8,128)S(1)} %get-tuple-element.29), channel_id=1, source_target_pairs={{0,4},{8,12},{4,0},{12,8},{1,5},{9,13},{5,1},{13,9},{2,6},{10,14},... | collective-permute-start | bytes 737288 | tf_op jit(solution)/shard_map/ppermute | solution.py:487
  24.8 9.7 %collective-permute-start.7 = (f32[2,6,8,640]{3,2,1,0:T(8,128)S(1)}, f32[2,6,8,640]{3,2,1,0:T(8,128)S(1)}, u32[]{:S(2)}, u32[]{:S(2)}) collective-permute-start(f32[2,6,8,640]{3,2,1,0:T(8,128)S(1)} %get-tuple-element.30), channel_id=1, source_target_pairs={{4,8},{8,4},{5,9},{9,5},{6,10},{10,6},{7,11},{11,7},{20,24},{24,20... | collective-permute-start | bytes 737288 | tf_op jit(solution)/shard_map/ppermute | solution.py:487

commit v7 on v6

--- a/solution.py
+++ b/solution.py
@@ -67,7 +67,13 @@
     return jnp.where(wavenumber > limit, ratio * ratio, 1.0)
 
 
-def filter_kernel(sectors, edges, limit_ref, table, *refs):
+def filter_kernel(sectors, edges, powered, limit_ref, table, *refs):
+    if powered:
+        coupling, *refs = refs
+        power_out = refs.pop(sectors + 3)
+        for g, entries in enumerate(coupling_power(coupling)):
+            for f, value in enumerate(entries):
+                power_out[g, f] = value
     circle_refs = refs[:sectors]
     own_out, first_out, second_out = refs[sectors:sectors + 3]
     wide, sums = refs[sectors + 3:]
@@ -330,11 +336,7 @@
     return power
 
 
-def face_kernel(sector, coupling, rate_own, rate_first, rate_second, own, first, second, level, power_out):
-    power = coupling_power(coupling)
-    for g, entries in enumerate(power):
-        for f, value in enumerate(entries):
-            power_out[g, f] = value
+def face_kernel(sector, rate_own, rate_first, rate_second, own, first, second, level):
     rows, kinds, levels, width = rate_own.shape
     extent = rows + 2 * HALO
     tiles = width // LANES
@@ -536,36 +538,34 @@
     results = []
     for c, (n, circle) in enumerate(zip(chunks, circles)):
         lines = n * levels * rows
-        own, first, second = pl.pallas_call(
-            functools.partial(filter_kernel, sectors, c == 0),
+        is_last = c == len(chunks) - 1
+        own, first, second, *power = pl.pallas_call(
+            functools.partial(filter_kernel, sectors, c == 0, is_last),
             out_shape=(
                 jax.ShapeDtypeStruct((n, rows, levels, width), f32),
                 jax.ShapeDtypeStruct((n, HALO, levels, width), f32),
                 jax.ShapeDtypeStruct((n, HALO, levels, width), f32),
+                *([jax.ShapeDtypeStruct((fields, fields, levels, LANES), f32)] if is_last else []),
             ),
-            in_specs=[VMEM] * (sectors + 2),
-            out_specs=(VMEM,) * 3,
+            in_specs=[VMEM] * (sectors + 2 + is_last),
+            out_specs=(VMEM,) * (3 + is_last),
             scratch_shapes=[
                 pltpu.VMEM((length // LANES, lines, LANES), f32),
                 pltpu.VMEM((length // LANES, lines, LANES), f32),
             ],
             compiler_params=PARAMS,
             name="polar_filter",
-        )(limits, table, *circle)
+        )(limits, table, *([jnp.transpose(coupling, (1, 0, 2))] if is_last else []), *circle)
         first, second = to_bands(first, second)
         if c == 0:
-            level, power = pl.pallas_call(
+            level = pl.pallas_call(
                 functools.partial(face_kernel, sector),
-                out_shape=(
-                    jax.ShapeDtypeStruct((extent, 5, levels, width), f32),
-                    jax.ShapeDtypeStruct((fields, fields, levels, LANES), f32),
-                ),
-                in_specs=[VMEM] * 7,
-                out_specs=(VMEM,) * 2,
+                out_shape=jax.ShapeDtypeStruct((extent, 5, levels, width), f32),
+                in_specs=[VMEM] * 6,
+                out_specs=VMEM,
                 compiler_params=PARAMS,
                 name="faces",
-            )(jnp.transpose(coupling, (1, 0, 2)), rate_own, rate_first, rate_second, own, first, second)
-        is_last = c == len(chunks) - 1
+            )(rate_own, rate_first, rate_second, own, first, second)
         earlier = results if is_last else []
         shape = adjoint_in.shape if is_last else (n, rows, levels, width)
         results.append(pl.pallas_call(
@@ -580,7 +580,7 @@
             ],
             compiler_params=PARAMS,
             name="transport",
-        )(power, level, own, first, second, *earlier))
+        )(power[0] if is_last else level, level, own, first, second, *earlier))
     return results[-1]
 
 

time: 38.3 us -> 38 us (level)
  Pallas kernels: 11.1 us -> 10.5 us
  waiting for transfers between devices: 11.3 us -> 11.7 us
    pallas_call x2, Pallas kernels: 7.03 us -> 6.38 us  [shards(): pl.pallas_call(functools.partial(transport_kernel, n, len(earlier), secto...]
    ppermute x3, waiting for transfers between devices: 3.35 us -> 3.91 us  [to_bands(): lax.ppermute(second, 'lat', odd_pairs)]
  transfers between devices with their start and end apart: 8 -> 8, of which waited for: 4 -> 5; matrix products, arithmetic and copies ran while one was open for 0% -> 0% of each run, Pallas kernels for 16% -> 15%
where the time goes in v7:
time: 38 us; the launch traced here: 37.8 us
  starting transfers between devices  15.6 us (41%)
  waiting for transfers between devices  11.7 us (31%)
  Pallas kernels  10.5 us (28%)
    ppermute x3, starting transfers between devices, to_bands(): lax.ppermute(first, 'lat', even_pairs)  7.74 us
    ppermute x2, waiting for transfers between devices, sector_ahead(): lax.ppermute(values, 'lon', [(s, (s - offset) % sectors) for s in range(s...  7.48 us
    pallas_call x2, Pallas kernels, shards(): pl.pallas_call(functools.partial(transport_kernel, n, len(earlier), secto...  6.38 us
    ppermute x3, starting transfers between devices, to_bands(): lax.ppermute(second, 'lat', odd_pairs)  5.73 us
    ppermute x3, waiting for transfers between devices, to_bands(): lax.ppermute(second, 'lat', odd_pairs)  3.91 us
    ppermute x2, starting transfers between devices, sector_ahead(): lax.ppermute(values, 'lon', [(s, (s - offset) % sectors) for s in range(s...  2.09 us
    pallas_call x1, Pallas kernels, shards(): pl.pallas_call(first_pack_kernel, out_shape=payload_shapes[0], in_specs=[...  1.55 us
    pallas_call x1, Pallas kernels, shards(): pl.pallas_call(functools.partial(rest_pack_kernel, chunks), out_shape=(*p...  1.43 us
  transfers between devices with their start and end apart: 8, of which 5 were waited for; matrix products, arithmetic and copies ran while one was open for 0% of the time, Pallas kernels for 15%

profile of v7, /device:TPU:16, one launch (start us, length us, event | category | flops | bytes accessed | tf_op | source)
XLA Modules:
  0.0 37.8 jit_solution(9292434952101456900)
XLA Ops:
  0.0 0.0 copy-start
  0.0 1.5 %first_pack.1.refs_0_ = f32[3,8,8,640]{3,2,1,0:T(8,128)S(1)} custom-call(f32[5,8,8,576]{3,2,1,0:T(8,128)} %adjoint.3, f32[8,8,576]{2,1,0:T(8,128)} %refs_0_.3, f32[8,8,576]{2,1,0:T(8,128)} %refs_1_.3, f32[8,8,576]{2,1,0:T(8,128)} %refs_2_.3, f32[8,8,576]{2,1,0:T(8,128)} %refs_3_.3), custom_call_target="tpu_custom_call" | custom-call | tf_op jit(solution)/shard_map/first_pack/pallas_call | solution.py:499
  1.6 0.0 copy-start.1
  1.6 1.6 %collective-permute-start.3 = (f32[3,8,8,640]{3,2,1,0:T(8,128)S(1)}, f32[3,8,8,640]{3,2,1,0:T(8,128)S(1)}, u32[]{:S(2)}, u32[]{:S(2)}) collective-permute-start(f32[3,8,8,640]{3,2,1,0:T(8,128)S(1)} %first_pack.1.refs_0_), channel_id=1, source_target_pairs={{0,2},{2,0},{1,3},{3,1},{4,6},{6,4},{5,7},{7,5},{8,10},{10,8},{9,1... | collective-permute-start | bytes 1474568 | tf_op jit(solution)/shard_map/ppermute | solution.py:486
  3.1 1.4 %rest_pack.1 = (f32[2,8,8,640]{3,2,1,0:T(8,128)S(1)}, f32[8,4,8,640]{3,2,1,0:T(8,128)S(1)}, f32[6,4,8,640]{3,2,1,0:T(8,128)S(1)}, f32[6,4,8,640]{3,2,1,0:T(8,128)S(1)}, f32[8,128]{1,0:T(8,128)S(1)}) custom-call(s32[32]{0:T(128)} %cutoff.1, f32[5,8,8,576]{3,2,1,0:T(8,128)} %adjoint.3, f32[8,8,576]{2,1,0:T(8,128)} %refs_0_.3, f32[8,8,576]{2,1,0:T(8,128)} %refs_1_.3, ...), custom_call_target="tpu_custom_call" | custom-call | tf_op jit(solution)/shard_map/rest_pack/pallas_call | solution.py:513
  4.6 1.6 %collective-permute-start.1 = (f32[6,4,8,640]{3,2,1,0:T(8,128)S(1)}, f32[6,4,8,640]{3,2,1,0:T(8,128)S(1)}, u32[]{:S(2)}, u32[]{:S(2)}) collective-permute-start(f32[6,4,8,640]{3,2,1,0:T(8,128)S(1)} %get-tuple-element.21), channel_id=1, source_target_pairs={{0,4},{8,12},{4,0},{12,8},{1,5},{9,13},{5,1},{13,9},{2,6},{10,14},... | collective-permute-start | bytes 1474568 | tf_op jit(solution)/shard_map/ppermute | solution.py:489
  6.2 0.5 %collective-permute-start = (f32[2,8,8,640]{3,2,1,0:T(8,128)S(1)}, f32[2,8,8,640]{3,2,1,0:T(8,128)S(1)}, u32[]{:S(2)}, u32[]{:S(2)}) collective-permute-start(f32[2,8,8,640]{3,2,1,0:T(8,128)S(1)} %get-tuple-element.18.refs_1_), channel_id=1, source_target_pairs={{0,2},{2,0},{1,3},{3,1},{4,6},{6,4},{5,7},{7,5},{8,10},{10,8},{9,1... | collective-permute-start | bytes 983048 | tf_op jit(solution)/shard_map/ppermute | solution.py:486
  6.7 1.9 %collective-permute-start.2 = (f32[6,4,8,640]{3,2,1,0:T(8,128)S(1)}, f32[6,4,8,640]{3,2,1,0:T(8,128)S(1)}, u32[]{:S(2)}, u32[]{:S(2)}) collective-permute-start(f32[6,4,8,640]{3,2,1,0:T(8,128)S(1)} %get-tuple-element.22), channel_id=1, source_target_pairs={{4,8},{8,4},{5,9},{9,5},{6,10},{10,6},{7,11},{11,7},{20,24},{24,20... | collective-permute-start | bytes 1474568 | tf_op jit(solution)/shard_map/ppermute | solution.py:489
  8.7 7.1 %collective-permute-done.3.refs_1_ = f32[3,8,8,640]{3,2,1,0:T(8,128)S(1)} collective-permute-done((f32[3,8,8,640]{3,2,1,0:T(8,128)S(1)}, f32[3,8,8,640]{3,2,1,0:T(8,128)S(1)}, u32[]{:S(2)}, u32[]{:S(2)}) %collective-permute-start.3) | collective-permute-done | bytes 491552 | tf_op jit(solution)/shard_map/ppermute | solution.py:486
  15.7 0.0 copy-done
  15.7 0.3 polar_filter.3
  16.1 3.2 %collective-permute-start.4 = (f32[3,6,8,640]{3,2,1,0:T(8,128)S(1)}, f32[3,6,8,640]{3,2,1,0:T(8,128)S(1)}, u32[]{:S(2)}, u32[]{:S(2)}) collective-permute-start(f32[3,6,8,640]{3,2,1,0:T(8,128)S(1)} %get-tuple-element.24), channel_id=1, source_target_pairs={{0,4},{8,12},{4,0},{12,8},{1,5},{9,13},{5,1},{13,9},{2,6},{10,14},... | collective-permute-start | bytes 1105928 | tf_op jit(solution)/shard_map/ppermute | solution.py:489
  19.3 1.9 %collective-permute-start.5 = (f32[3,6,8,640]{3,2,1,0:T(8,128)S(1)}, f32[3,6,8,640]{3,2,1,0:T(8,128)S(1)}, u32[]{:S(2)}, u32[]{:S(2)}) collective-permute-start(f32[3,6,8,640]{3,2,1,0:T(8,128)S(1)} %get-tuple-element.25), channel_id=1, source_target_pairs={{4,8},{8,4},{5,9},{9,5},{6,10},{10,6},{7,11},{11,7},{20,24},{24,20... | collective-permute-start | bytes 1105928 | tf_op jit(solution)/shard_map/ppermute | solution.py:489
  21.2 0.4 %collective-permute-done.refs_2_ = f32[2,8,8,640]{3,2,1,0:T(8,128)S(1)} collective-permute-done((f32[2,8,8,640]{3,2,1,0:T(8,128)S(1)}, f32[2,8,8,640]{3,2,1,0:T(8,128)S(1)}, u32[]{:S(2)}, u32[]{:S(2)}) %collective-permute-start) | collective-permute-done | bytes 327712 | tf_op jit(solution)/shard_map/ppermute | solution.py:486
  21.6 0.0 copy-done.1
  21.6 0.3 polar_filter.2
  22.0 2.9 %collective-permute-start.6 = (f32[2,6,8,640]{3,2,1,0:T(8,128)S(1)}, f32[2,6,8,640]{3,2,1,0:T(8,128)S(1)}, u32[]{:S(2)}, u32[]{:S(2)}) collective-permute-start(f32[2,6,8,640]{3,2,1,0:T(8,128)S(1)} %get-tuple-element.27), channel_id=1, source_target_pairs={{0,4},{8,12},{4,0},{12,8},{1,5},{9,13},{5,1},{13,9},{2,6},{10,14},... | collective-permute-start | bytes 737288 | tf_op jit(solution)/shard_map/ppermute | solution.py:489
  24.9 0.0 collective-permute-done.1.rate_first
  24.9 1.9 %collective-permute-start.7 = (f32[2,6,8,640]{3,2,1,0:T(8,128)S(1)}, f32[2,6,8,640]{3,2,1,0:T(8,128)S(1)}, u32[]{:S(2)}, u32[]{:S(2)}) collective-permute-start(f32[2,6,8,640]{3,2,1,0:T(8,128)S(1)} %get-tuple-element.28), channel_id=1, source_target_pairs={{4,8},{8,4},{5,9},{9,5},{6,10},{10,6},{7,11},{11,7},{20,24},{24,20... | collective-permute-start | bytes 737288 | tf_op jit(solution)/shard_map/ppermute | solution.py:489
  26.8 0.0 collective-permute-done.2.rate_second
  26.8 0.3 collective-permute-done.4.first.first_ref
  27.1 3.3 %collective-permute-done.5.second.second_ref = f32[3,6,8,640]{3,2,1,0:T(8,128)S(1)} collective-permute-done((f32[3,6,8,640]{3,2,1,0:T(8,128)S(1)}, f32[3,6,8,640]{3,2,1,0:T(8,128)S(1)}, u32[]{:S(2)}, u32[]{:S(2)}) %collective-permute-start.5) | collective-permute-done | bytes 368672 | tf_op jit(solution)/shard_map/ppermute | solution.py:489
  30.4 0.4 %faces.1.power_ref.rates = f32[20,5,8,640]{3,2,1,0:T(8,128)S(1)} custom-call(f32[8,4,8,640]{3,2,1,0:T(8,128)S(1)} %get-tuple-element.20.rate_own, f32[6,4,8,640]{3,2,1,0:T(8,128)S(1)} %collective-permute-done.1.rate_first, f32[6,4,8,640]{3,2,1,0:T(8,128)S(1)} %collective-permute-done.2.rate_second, f32[3,8,8,640]{3,2,1,0:T(8,128)S(1)} %get-tuple-element.23.own.own_ref, ...), custom_call_target="tpu_custom_call" | custom-call | tf_op jit(solution)/shard_map/faces/pallas_call | solution.py:561
  30.9 3.1 %transport.2.refs_0_ = f32[3,8,8,640]{3,2,1,0:T(8,128)S(1)} custom-call(f32[20,5,8,640]{3,2,1,0:T(8,128)S(1)} %faces.1.power_ref.rates, f32[20,5,8,640]{3,2,1,0:T(8,128)S(1)} %faces.1.power_ref.rates, f32[3,8,8,640]{3,2,1,0:T(8,128)S(1)} %get-tuple-element.23.own.own_ref, f32[3,6,8,640]{3,2,1,0:T(8,128)S(1)} %collective-permute-done.4.first.first_ref, ...), custom_call_target="tpu_custom_call" | custom-call | tf_op jit(solution)/shard_map/transport/pallas_call | solution.py:571
  33.9 0.0 collective-permute-done.6.first_ref
  33.9 0.6 %collective-permute-done.7.second_ref = f32[2,6,8,640]{3,2,1,0:T(8,128)S(1)} collective-permute-done((f32[2,6,8,640]{3,2,1,0:T(8,128)S(1)}, f32[2,6,8,640]{3,2,1,0:T(8,128)S(1)}, u32[]{:S(2)}, u32[]{:S(2)}) %collective-permute-start.7) | collective-permute-done | bytes 245792 | tf_op jit(solution)/shard_map/ppermute | solution.py:489
  34.5 3.3 %transport.3 = f32[5,8,8,576]{3,2,1,0:T(8,128)} custom-call(f32[5,5,8,128]{3,2,1,0:T(8,128)S(1)} %get-tuple-element.19.power_ref, f32[20,5,8,640]{3,2,1,0:T(8,128)S(1)} %faces.1.power_ref.rates, f32[2,8,8,640]{3,2,1,0:T(8,128)S(1)} %get-tuple-element.26.own_ref, f32[2,6,8,640]{3,2,1,0:T(8,128)S(1)} %collective-permute-done.6.first_ref, ...), custom_call_target="tpu_custom_call" | custom-call | tf_op jit(solution)/shard_map/transport/pallas_call | solution.py:571
Async XLA Ops:
  0.0 15.7 %copy-start = (bf16[9,256,256]{2,1,0:T(8,128)(2,1)S(1)}, bf16[9,256,256]{2,1,0:T(8,128)(2,1)}, u32[]{:S(2)}) copy-start(bf16[9,256,256]{2,1,0:T(8,128)(2,1)} %constant.2.clone.table) | copy-start | bytes 3538948
  1.6 20.1 %copy-start.1 = (f32[8,5,5]{2,0,1:T(8,128)S(1)}, f32[8,5,5]{2,0,1:T(8,128)}, u32[]{:S(2)}) copy-start(f32[8,5,5]{2,0,1:T(8,128)} %param.13) | copy-start | bytes 2404
  1.6 14.2 %collective-permute-start.3 = (f32[3,8,8,640]{3,2,1,0:T(8,128)S(1)}, f32[3,8,8,640]{3,2,1,0:T(8,128)S(1)}, u32[]{:S(2)}, u32[]{:S(2)}) collective-permute-start(f32[3,8,8,640]{3,2,1,0:T(8,128)S(1)} %first_pack.1.refs_0_), channel_id=1, source_target_pairs={{0,2},{2,0},{1,3},{3,1},{4,6},{6,4},{5,7},{7,5},{8,10},{10,8},{9,1... | collective-permute-start | bytes 1474568 | tf_op jit(solution)/shard_map/ppermute | solution.py:486
  4.6 20.3 %collective-permute-start.1 = (f32[6,4,8,640]{3,2,1,0:T(8,128)S(1)}, f32[6,4,8,640]{3,2,1,0:T(8,128)S(1)}, u32[]{:S(2)}, u32[]{:S(2)}) collective-permute-start(f32[6,4,8,640]{3,2,1,0:T(8,128)S(1)} %get-tuple-element.21), channel_id=1, source_target_pairs={{0,4},{8,12},{4,0},{12,8},{1,5},{9,13},{5,1},{13,9},{2,6},{10,14},... | collective-permute-start | bytes 1474568 | tf_op jit(solution)/shard_map/ppermute | solution.py:489
  6.2 15.4 %collective-permute-start = (f32[2,8,8,640]{3,2,1,0:T(8,128)S(1)}, f32[2,8,8,640]{3,2,1,0:T(8,128)S(1)}, u32[]{:S(2)}, u32[]{:S(2)}) collective-permute-start(f32[2,8,8,640]{3,2,1,0:T(8,128)S(1)} %get-tuple-element.18.refs_1_), channel_id=1, source_target_pairs={{0,2},{2,0},{1,3},{3,1},{4,6},{6,4},{5,7},{7,5},{8,10},{10,8},{9,1... | collective-permute-start | bytes 983048 | tf_op jit(solution)/shard_map/ppermute | solution.py:486
  6.7 20.1 %collective-permute-start.2 = (f32[6,4,8,640]{3,2,1,0:T(8,128)S(1)}, f32[6,4,8,640]{3,2,1,0:T(8,128)S(1)}, u32[]{:S(2)}, u32[]{:S(2)}) collective-permute-start(f32[6,4,8,640]{3,2,1,0:T(8,128)S(1)} %get-tuple-element.22), channel_id=1, source_target_pairs={{4,8},{8,4},{5,9},{9,5},{6,10},{10,6},{7,11},{11,7},{20,24},{24,20... | collective-permute-start | bytes 1474568 | tf_op jit(solution)/shard_map/ppermute | solution.py:489
  16.1 11.0 %collective-permute-start.4 = (f32[3,6,8,640]{3,2,1,0:T(8,128)S(1)}, f32[3,6,8,640]{3,2,1,0:T(8,128)S(1)}, u32[]{:S(2)}, u32[]{:S(2)}) collective-permute-start(f32[3,6,8,640]{3,2,1,0:T(8,128)S(1)} %get-tuple-element.24), channel_id=1, source_target_pairs={{0,4},{8,12},{4,0},{12,8},{1,5},{9,13},{5,1},{13,9},{2,6},{10,14},... | collective-permute-start | bytes 1105928 | tf_op jit(solution)/shard_map/ppermute | solution.py:489
  19.3 11.1 %collective-permute-start.5 = (f32[3,6,8,640]{3,2,1,0:T(8,128)S(1)}, f32[3,6,8,640]{3,2,1,0:T(8,128)S(1)}, u32[]{:S(2)}, u32[]{:S(2)}) collective-permute-start(f32[3,6,8,640]{3,2,1,0:T(8,128)S(1)} %get-tuple-element.25), channel_id=1, source_target_pairs={{4,8},{8,4},{5,9},{9,5},{6,10},{10,6},{7,11},{11,7},{20,24},{24,20... | collective-permute-start | bytes 1105928 | tf_op jit(solution)/shard_map/ppermute | solution.py:489
  22.0 11.9 %collective-permute-start.6 = (f32[2,6,8,640]{3,2,1,0:T(8,128)S(1)}, f32[2,6,8,640]{3,2,1,0:T(8,128)S(1)}, u32[]{:S(2)}, u32[]{:S(2)}) collective-permute-start(f32[2,6,8,640]{3,2,1,0:T(8,128)S(1)} %get-tuple-element.27), channel_id=1, source_target_pairs={{0,4},{8,12},{4,0},{12,8},{1,5},{9,13},{5,1},{13,9},{2,6},{10,14},... | collective-permute-start | bytes 737288 | tf_op jit(solution)/shard_map/ppermute | solution.py:489
  24.9 9.6 %collective-permute-start.7 = (f32[2,6,8,640]{3,2,1,0:T(8,128)S(1)}, f32[2,6,8,640]{3,2,1,0:T(8,128)S(1)}, u32[]{:S(2)}, u32[]{:S(2)}) collective-permute-start(f32[2,6,8,640]{3,2,1,0:T(8,128)S(1)} %get-tuple-element.28), channel_id=1, source_target_pairs={{4,8},{8,4},{5,9},{9,5},{6,10},{10,6},{7,11},{11,7},{20,24},{24,20... | collective-permute-start | bytes 737288 | tf_op jit(solution)/shard_map/ppermute | solution.py:489
